TPU v7x, 256 devices: a whole 4x4x8 slice. The times are simulated.
256 devices in a mesh: row: 8 (over x, y_lo), col: 32 (over y_hi, z, core).
Axes of the slice: x: 4, y: 4 (y_hi: 2, y_lo: 2; y = y_hi * 2 + y_lo), z: 8, core: 2. Of those that a mesh axis runs over, the one named last changes fastest.
Arguments:
- features: bfloat16 [65536, 128], P(('row', 'col')), may hold values from -6 to 6
- degrees: int32 [65536], P(('row', 'col')), may hold values from 32 to 159
- adj_tiles: bfloat16 [8, 32, 256, 4096], P('row', 'col'), may hold values from 0 to 0.22472483, as said below
- tile_rows: int32 [8, 32, 256], P('row', 'col'), may hold values from 0 to 127
- tile_cols: int32 [8, 32, 256], P('row', 'col'), may hold values from 0 to 31
- tile_counts: int32 [8, 32], P('row', 'col'), may hold values from 64 to 256, as said below
Outputs:
- propagated: bfloat16 [65536, 128], P(('row', 'col'))
Inputs may be any that keep to these rules, and one draw needn't show every extreme that they name: Each block holds at most 256 live tiles, in its first tile_counts slots; some block holds exactly 256. `adj_tiles`: edge weights are zero or positive.
All inputs are finite; a program needn't handle non-finite values.
Results may differ from a plain program's by a relative error of at most 0.0054.
Values may be sent and summed in bfloat16 or wider, within the bound.
A program may use at most 128 MiB of HBM per device.

v0:
```python
import jax
import jax.numpy as jnp
from jax import lax
from jax.sharding import PartitionSpec as P

TILE = 64
KNN = 32
STEPS = 2


ALPHA = 0.1


def shards(features, degrees, adj_tiles, tile_rows, tile_cols, tile_counts):
    col_count = lax.axis_size("col")
    nodes_dev = features.shape[0]
    feat_width = features.shape[1]
    tile_slots = adj_tiles.shape[2]
    dev_tiles = adj_tiles.reshape(tile_slots, TILE, TILE)
    row_ids_all = tile_rows.reshape(tile_slots)
    col_ids_all = tile_cols.reshape(tile_slots)
    live_count = tile_counts.reshape(())
    block_len = min(256, tile_slots)
    num_turns = tile_slots // block_len
    row_tiles = nodes_dev * col_count // TILE
    norm_scale = jnp.sqrt(KNN / degrees.astype(jnp.float32))[:, None]
    teleport = ALPHA * features.astype(jnp.float32)
    current = features.astype(jnp.float32)
    for repeat in range(STEPS):
        source = (norm_scale * current).astype(jnp.bfloat16)
        col_panel = lax.all_gather(source, "row", axis=0, tiled=True).reshape(-1, TILE, feat_width)

        def add_block(turn_index, totals):
            first_tile = turn_index * block_len
            live_mask = first_tile + jnp.arange(block_len, dtype=jnp.int32) < live_count
            inputs = col_panel[col_ids_all]
            products = jnp.einsum(
                "tab,tbf->taf", dev_tiles, inputs, preferred_element_type=jnp.float32
            )
            products = jnp.where(live_mask[:, None, None], products, jnp.zeros_like(products))
            return totals.at[row_ids_all].add(products)

        start_tot = jnp.zeros((row_tiles, TILE, feat_width), jnp.float32)
        totals = lax.fori_loop(0, num_turns, add_block, start_tot)
        partial_rows = totals.reshape(row_tiles * TILE, feat_width)
        summed = lax.psum(partial_rows, "col")
        own_rows = lax.dynamic_slice_in_dim(summed, lax.axis_index("col") * nodes_dev, nodes_dev, 0)
        current = (1.0 - ALPHA) * norm_scale * own_rows + teleport
    return current.astype(jnp.bfloat16)


def solution(mesh):
    return jax.shard_map(
        shards,
        mesh=mesh,
        in_specs=(
            P(("row", "col"), None),
            P(("row", "col")),
            P("row", "col", None, None),
            P("row", "col", None),
            P("row", "col", None),
            P("row", "col"),
        ),
        out_specs=P(("row", "col"), None),
        check_vma=False,
    )
```

profile of v0, /device:TPU:8, one launch (start us, length us, event | category | flops | bytes accessed | tf_op | source)
XLA Modules:
  0.0 746.7 jit_solution(6147863713044268704)
XLA Ops:
  6.5 0.0 all-reduce.3.cloned.1.call-start
  7.2 0.7 compare_select_fusion.1
  7.9 0.7 compare_select_fusion
  8.6 0.7 broadcast_multiply_fusion
  9.3 0.9 fusion.5
  10.2 29.2 %all_gather.6 = bf16[2048,128]{1,0:T(8,128)(2,1)S(1)} all-gather(bf16[256,128]{1,0:T(8,128)(2,1)S(1)} %fusion.5), channel_id=1, replica_groups=mesh['row'=8,'col'=32] {'row'}, dimensions={0}, use_global_device_ids=true | all-gather | bytes 589824 | tf_op jit(solution)/shard_map/all_gather | solution.py:31
  39.4 3.3 copy.7
  42.7 6.6 copy.8
  49.3 3.0 gather_fusion
  52.4 7.9 %select_bitcast_fusion.1 = f32[256,64,128]{2,1,0:T(8,128)} fusion(pred[256]{0:T(512)(128)(4,1)S(1)} %iota_compare_fusion, bf16[256,64,64]{2,1,0:T(8,128)(2,1)} %copy.8, bf16[256,64,128]{2,1,0:T(8,128)(2,1)} %gather_fusion), kind=kOutput, calls=%fused_computation.5 | convolution fusion | flops 270532608 | bytes 14680320 | tf_op jit(solution)/shard_map/while/body/eval_jaxpr/tab,tbf->taf/dot_general | solution.py:37
  60.3 2.5 broadcast.71.clone
  62.8 39.4 %scatter_fusion = f32[128,64,128]{2,1,0:T(8,128)} fusion(f32[128,64,128]{2,1,0:T(8,128)} %broadcast.71.clone, s32[256]{0:T(256)S(1)} %bitcast.26, f32[256,64,128]{2,1,0:T(8,128)} %select_bitcast_fusion.1), kind=kCustom, calls=%fused_computation.2 | custom fusion | flops 2097152 | bytes 25166848 | tf_op jit(solution)/shard_map/while/body/eval_jaxpr/scatter-add | solution.py:41
  102.2 0.0 all-reduce.3.cloned.1.call-update
  102.2 0.0 all-reduce.5.cloned.1.call-start
  102.3 280.0 %all-reduce.3.cloned.1.call-done = f32[8192,128]{1,0:T(8,128)} async-done(((f32[8192,128]{1,0:T(8,128)}), f32[8192,128]{1,0:T(8,128)}) %all-reduce.3.cloned.1.call-update) | async-done | bytes 4194320 | tf_op jit(solution)/shard_map/psum | solution.py:46
  382.3 1.0 fusion.3
  383.3 29.2 %all_gather.7 = bf16[2048,128]{1,0:T(8,128)(2,1)S(1)} all-gather(bf16[256,128]{1,0:T(8,128)(2,1)S(1)} %fusion.3), channel_id=1, replica_groups=mesh['row'=8,'col'=32] {'row'}, dimensions={0}, use_global_device_ids=true | all-gather | bytes 589824 | tf_op jit(solution)/shard_map/all_gather | solution.py:31
  412.5 3.1 gather_fusion.1
  415.6 7.9 %select_bitcast_fusion = f32[256,64,128]{2,1,0:T(8,128)} fusion(pred[256]{0:T(512)(128)(4,1)S(1)} %iota_compare_fusion, bf16[256,64,64]{2,1,0:T(8,128)(2,1)} %copy.8, bf16[256,64,128]{2,1,0:T(8,128)(2,1)} %gather_fusion.1), kind=kOutput, calls=%fused_computation.4 | convolution fusion | flops 270532608 | bytes 14680320 | tf_op jit(solution)/shard_map/while/body/eval_jaxpr/tab,tbf->taf/dot_general | solution.py:37
  423.5 2.5 broadcast.71
  426.0 39.3 %scatter_fusion.1 = f32[128,64,128]{2,1,0:T(8,128)} fusion(f32[128,64,128]{2,1,0:T(8,128)} %broadcast.71, s32[256]{0:T(256)S(1)} %bitcast.27, f32[256,64,128]{2,1,0:T(8,128)} %select_bitcast_fusion), kind=kCustom, calls=%fused_computation.3 | custom fusion | flops 2097152 | bytes 25166848 | tf_op jit(solution)/shard_map/while/body/eval_jaxpr/scatter-add | solution.py:41
  465.3 0.0 all-reduce.5.cloned.1.call-update
  465.3 272.9 %all-reduce.5.cloned.1.call-done = f32[8192,128]{1,0:T(8,128)} async-done(((f32[8192,128]{1,0:T(8,128)}), f32[8192,128]{1,0:T(8,128)}) %all-reduce.5.cloned.1.call-update) | async-done | bytes 4194320 | tf_op jit(solution)/shard_map/psum | solution.py:46
  738.3 1.6 fusion.4
  (4 shorter events, 0.0 us)
Async XLA Ops:
  6.5 375.7 %all-reduce.3.cloned.1.call-start = ((), (), s32[]{:S(2)}) async-start(), calls=%async_computation | async-start | bytes 8388608 | tf_op jit(solution)/shard_map/psum | solution.py:46
  102.2 280.1 %copy-start = (bf16[256,128]{1,0:T(8,128)(2,1)S(1)}, bf16[256,128]{1,0:T(8,128)(2,1)}, u32[]{:S(2)}) copy-start(bf16[256,128]{1,0:T(8,128)(2,1)} %param.6) | copy-start | bytes 196612
  102.2 636.1 %all-reduce.5.cloned.1.call-start = ((), (), s32[]{:S(2)}) async-start(), calls=%async_computation.1 | async-start | bytes 8388608 | tf_op jit(solution)/shard_map/psum | solution.py:46
Sparse Core Ops, SparseCore 0:
  102.3 279.8 all-reduce.2
  465.5 272.7 all-reduce.4
where the time goes:
time: 750 us; the launch traced here: 747 us
  waiting for transfers between devices  553 us (74%)
  other arithmetic  84.4 us (11%)
  blocking collectives  58.4 us (8%)
  local copies, waits for them, and re-layouts  21 us (3%)
  matrix products  15.9 us (2%)
  between operations  14.1 us (2%)
    psum x2, waiting for transfers between devices, shards(): summed = lax.psum(partial_rows, 'col')  553 us
    scatter-add x2, other arithmetic, add_block(): return totals.at[row_ids_all].add(products)  78.7 us
    all_gather x2, blocking collectives, shards(): lax.all_gather(source, 'row', axis=0, tiled=True)  58.4 us
    dot_general x2, matrix products, add_block(): jnp.einsum('tab,tbf->taf', dev_tiles, inputs, preferred_element_type=jnp....  15.9 us
  transfers between devices with their start and end apart: 2, of which 2 were waited for; matrix products, arithmetic and copies ran while one was open for 0% of the time, Pallas kernels for 0%

commit v1 on v0

--- a/solution.py
+++ b/solution.py
@@ -43,8 +43,7 @@
         start_tot = jnp.zeros((row_tiles, TILE, feat_width), jnp.float32)
         totals = lax.fori_loop(0, num_turns, add_block, start_tot)
         partial_rows = totals.reshape(row_tiles * TILE, feat_width)
-        summed = lax.psum(partial_rows, "col")
-        own_rows = lax.dynamic_slice_in_dim(summed, lax.axis_index("col") * nodes_dev, nodes_dev, 0)
+        own_rows = lax.psum_scatter(partial_rows, "col", scatter_dimension=0, tiled=True)
         current = (1.0 - ALPHA) * norm_scale * own_rows + teleport
     return current.astype(jnp.bfloat16)
 

time: 750 us -> 451 us (0.60)
  waiting for transfers between devices: 553 us -> 255 us
    psum x2 -> x0, waiting for transfers between devices: 553 us -> none  [shards(): summed = lax.psum(partial_rows, 'col')]
    reduce_scatter x0 -> x2, waiting for transfers between devices: none -> 255 us  [shards(): lax.psum_scatter(partial_rows, 'col', scatter_dimension=0, tiled=True)]
where the time goes in v1:
time: 451 us; the launch traced here: 449 us
  waiting for transfers between devices  255 us (57%)
  other arithmetic  84.4 us (19%)
  blocking collectives  58.2 us (13%)
  local copies, waits for them, and re-layouts  21 us (5%)
  matrix products  15.9 us (4%)
  between operations  14.1 us (3%)
    reduce_scatter x2, waiting for transfers between devices, shards(): lax.psum_scatter(partial_rows, 'col', scatter_dimension=0, tiled=True)  255 us
    scatter-add x2, other arithmetic, add_block(): return totals.at[row_ids_all].add(products)  78.7 us
    all_gather x2, blocking collectives, shards(): lax.all_gather(source, 'row', axis=0, tiled=True)  58.2 us
    dot_general x2, matrix products, add_block(): jnp.einsum('tab,tbf->taf', dev_tiles, inputs, preferred_element_type=jnp....  15.9 us
  transfers between devices with their start and end apart: 2, of which 2 were waited for; matrix products, arithmetic and copies ran while one was open for 0% of the time, Pallas kernels for 0%

profile of v1, /device:TPU:8, one launch (start us, length us, event | category | flops | bytes accessed | tf_op | source)
XLA Modules:
  0.0 448.6 jit_solution(6399208129320878904)
XLA Ops:
  7.2 0.7 compare_select_fusion.1
  7.9 0.7 compare_select_fusion
  8.6 0.7 broadcast_multiply_fusion
  9.3 0.9 fusion.5
  10.2 29.2 %all_gather.6 = bf16[2048,128]{1,0:T(8,128)(2,1)S(1)} all-gather(bf16[256,128]{1,0:T(8,128)(2,1)S(1)} %fusion.5), channel_id=1, replica_groups=mesh['row'=8,'col'=32] {'row'}, dimensions={0}, use_global_device_ids=true | all-gather | bytes 589824 | tf_op jit(solution)/shard_map/all_gather | solution.py:31
  39.4 3.3 copy.7
  42.7 6.6 %copy.8 = bf16[256,64,64]{2,1,0:T(8,128)(2,1)} copy(bf16[256,64,64]{0,2,1:T(8,128)(2,1)S(1)} %bitcast.25) | data formatting | bytes 4194304 | tf_op jit(solution)/shard_map/reshape | solution.py:19
  49.3 3.0 gather_fusion
  52.4 7.9 %select_bitcast_fusion.1 = f32[256,64,128]{2,1,0:T(8,128)} fusion(pred[256]{0:T(512)(128)(4,1)S(1)} %iota_compare_fusion, bf16[256,64,64]{2,1,0:T(8,128)(2,1)} %copy.8, bf16[256,64,128]{2,1,0:T(8,128)(2,1)} %gather_fusion), kind=kOutput, calls=%fused_computation.5 | convolution fusion | flops 270532608 | bytes 14680320 | tf_op jit(solution)/shard_map/while/body/eval_jaxpr/tab,tbf->taf/dot_general | solution.py:37
  60.3 2.5 broadcast.71.clone
  62.8 39.4 %scatter_fusion = f32[128,64,128]{2,1,0:T(8,128)} fusion(f32[128,64,128]{2,1,0:T(8,128)} %broadcast.71.clone, s32[256]{0:T(256)S(1)} %bitcast.26, f32[256,64,128]{2,1,0:T(8,128)} %select_bitcast_fusion.1), kind=kCustom, calls=%fused_computation.2 | custom fusion | flops 2097152 | bytes 25166848 | tf_op jit(solution)/shard_map/while/body/eval_jaxpr/scatter-add | solution.py:41
  102.1 0.0 reduce-scatter.3.cloned.1.call-update
  102.2 0.0 reduce-scatter.5.cloned.1.call-start
  102.2 129.5 %reduce-scatter.3.cloned.1.call-done = f32[256,128]{1,0:T(8,128)} async-done(((f32[8192,128]{1,0:T(8,128)}), f32[256,128]{1,0:T(8,128)}) %reduce-scatter.3.cloned.1.call-update) | async-done | bytes 131088 | tf_op jit(solution)/shard_map/reduce_scatter | solution.py:46
  231.7 0.0 copy-done
  231.7 1.0 fusion.3
  232.8 29.0 %all_gather.7 = bf16[2048,128]{1,0:T(8,128)(2,1)S(1)} all-gather(bf16[256,128]{1,0:T(8,128)(2,1)S(1)} %fusion.3), channel_id=1, replica_groups=mesh['row'=8,'col'=32] {'row'}, dimensions={0}, use_global_device_ids=true | all-gather | bytes 589824 | tf_op jit(solution)/shard_map/all_gather | solution.py:31
  261.8 3.1 gather_fusion.1
  264.9 7.9 %select_bitcast_fusion = f32[256,64,128]{2,1,0:T(8,128)} fusion(pred[256]{0:T(512)(128)(4,1)S(1)} %iota_compare_fusion, bf16[256,64,64]{2,1,0:T(8,128)(2,1)} %copy.8, bf16[256,64,128]{2,1,0:T(8,128)(2,1)} %gather_fusion.1), kind=kOutput, calls=%fused_computation.4 | convolution fusion | flops 270532608 | bytes 14680320 | tf_op jit(solution)/shard_map/while/body/eval_jaxpr/tab,tbf->taf/dot_general | solution.py:37
  272.8 2.5 broadcast.71
  275.3 39.4 %scatter_fusion.1 = f32[128,64,128]{2,1,0:T(8,128)} fusion(f32[128,64,128]{2,1,0:T(8,128)} %broadcast.71, s32[256]{0:T(256)S(1)} %bitcast.27, f32[256,64,128]{2,1,0:T(8,128)} %select_bitcast_fusion), kind=kCustom, calls=%fused_computation.3 | custom fusion | flops 2097152 | bytes 25166848 | tf_op jit(solution)/shard_map/while/body/eval_jaxpr/scatter-add | solution.py:41
  314.7 0.0 reduce-scatter.5.cloned.1.call-update
  314.7 125.4 %reduce-scatter.5.cloned.1.call-done = f32[256,128]{1,0:T(8,128)} async-done(((f32[8192,128]{1,0:T(8,128)}), f32[256,128]{1,0:T(8,128)}) %reduce-scatter.5.cloned.1.call-update) | async-done | bytes 131088 | tf_op jit(solution)/shard_map/reduce_scatter | solution.py:46
  440.1 1.6 fusion.4
  (4 shorter events, 0.0 us)
Async XLA Ops:
  6.5 225.2 %reduce-scatter.3.cloned.1.call-start = ((), (), s32[]{:S(2)}) async-start(), calls=%async_computation.2 | async-start | bytes 4325376 | tf_op jit(solution)/shard_map/reduce_scatter | solution.py:46
  102.1 129.6 %copy-start = (bf16[256,128]{1,0:T(8,128)(2,1)S(1)}, bf16[256,128]{1,0:T(8,128)(2,1)}, u32[]{:S(2)}) copy-start(bf16[256,128]{1,0:T(8,128)(2,1)} %param.6) | copy-start | bytes 196612
  102.2 337.9 %reduce-scatter.5.cloned.1.call-start = ((), (), s32[]{:S(2)}) async-start(), calls=%async_computation.3 | async-start | bytes 4325376 | tf_op jit(solution)/shard_map/reduce_scatter | solution.py:46
Sparse Core Ops, SparseCore 0:
  102.3 129.4 reduce-scatter.2
  314.8 125.2 reduce-scatter.4

commit v2 on v1

--- a/solution.py
+++ b/solution.py
@@ -1,14 +1,96 @@
+import functools
+
 import jax
 import jax.numpy as jnp
 from jax import lax
+from jax.experimental import pallas as pl
+from jax.experimental.pallas import tpu as pltpu
 from jax.sharding import PartitionSpec as P
 
 TILE = 64
 KNN = 32
 STEPS = 2
 
+MESH = pl.DeviceIdType.MESH
 
 ALPHA = 0.1
+
+
+def reduce_scatter_kernel(n, part_ref, own_ref, out_ref, recv, send_sem, recv_sem):
+    me = lax.axis_index("col")
+    row = lax.axis_index("row")
+
+    barrier = pltpu.get_barrier_semaphore()
+
+    def greet(k, carry):
+        peer = lax.rem(me + k, n)
+        pl.semaphore_signal(barrier, inc=1, device_id=(row, peer), device_id_type=MESH)
+        return carry
+
+    lax.fori_loop(1, n, greet, 0)
+    pl.semaphore_wait(barrier, n - 1)
+
+    def send(peer):
+        return pltpu.make_async_remote_copy(
+            src_ref=part_ref.at[peer],
+            dst_ref=recv.at[me],
+            send_sem=send_sem.at[peer],
+            recv_sem=recv_sem.at[me],
+            device_id=(row, peer),
+            device_id_type=MESH,
+        )
+
+    def arrival(sender):
+        return pltpu.make_async_remote_copy(
+            src_ref=part_ref.at[sender],
+            dst_ref=recv.at[sender],
+            send_sem=send_sem.at[sender],
+            recv_sem=recv_sem.at[sender],
+            device_id=(row, sender),
+            device_id_type=MESH,
+        )
+
+    def start(k, carry):
+        send(lax.rem(me + k, n)).start()
+        return carry
+
+    lax.fori_loop(1, n, start, 0)
+
+    out_ref[...] = own_ref[...]
+
+    def finish(k, carry):
+        sender = lax.rem(me + n - k, n)
+        arrival(sender).wait_recv()
+        out_ref[...] += recv[sender].astype(jnp.float32)
+        return carry
+
+    lax.fori_loop(1, n, finish, 0)
+
+    def drain(k, carry):
+        send(lax.rem(me + k, n)).wait_send()
+        return carry
+
+    lax.fori_loop(1, n, drain, 0)
+
+
+def col_reduce_scatter(partial_rows, nodes_dev):
+    n = lax.axis_size("col")
+    feat_width = partial_rows.shape[1]
+    me = lax.axis_index("col")
+    own = lax.dynamic_slice_in_dim(partial_rows, me * nodes_dev, nodes_dev, 0)
+    pieces = partial_rows.reshape(n, nodes_dev, feat_width).astype(jnp.bfloat16)
+    return pl.pallas_call(
+        functools.partial(reduce_scatter_kernel, n),
+        out_shape=jax.ShapeDtypeStruct((nodes_dev, feat_width), jnp.float32),
+        in_specs=[pl.BlockSpec(memory_space=pltpu.VMEM)] * 2,
+        out_specs=pl.BlockSpec(memory_space=pltpu.VMEM),
+        scratch_shapes=[
+            pltpu.VMEM((n, nodes_dev, feat_width), jnp.bfloat16),
+            pltpu.SemaphoreType.DMA((n,)),
+            pltpu.SemaphoreType.DMA((n,)),
+        ],
+        compiler_params=pltpu.CompilerParams(collective_id=0, has_side_effects=True),
+    )(pieces, own)
 
 
 def shards(features, degrees, adj_tiles, tile_rows, tile_cols, tile_counts):
@@ -43,7 +125,7 @@
         start_tot = jnp.zeros((row_tiles, TILE, feat_width), jnp.float32)
         totals = lax.fori_loop(0, num_turns, add_block, start_tot)
         partial_rows = totals.reshape(row_tiles * TILE, feat_width)
-        own_rows = lax.psum_scatter(partial_rows, "col", scatter_dimension=0, tiled=True)
+        own_rows = col_reduce_scatter(partial_rows, nodes_dev)
         current = (1.0 - ALPHA) * norm_scale * own_rows + teleport
     return current.astype(jnp.bfloat16)
 

time: 451 us -> 314 us (0.70)
  waiting for transfers between devices: 255 us -> 0 us
  Pallas kernels: 0 us -> 119 us
  between operations: 14.1 us -> 0.72 us
  other arithmetic: 84.4 us -> 91.9 us
    reduce_scatter x2 -> x0, waiting for transfers between devices: 255 us -> none  [shards(): lax.psum_scatter(partial_rows, 'col', scatter_dimension=0, tiled=True)]
    pallas_call x0 -> x2, Pallas kernels: none -> 119 us  [col_reduce_scatter(): pl.pallas_call(functools.partial(reduce_scatter_kernel, n), out_shape=jax...]
    convert_element_type x0 -> x2, other arithmetic: none -> 8.12 us  [col_reduce_scatter(): pieces = partial_rows.reshape(n, nodes_dev, feat_width).astype(jnp.bfloat16)]
  transfers between devices with their start and end apart: 2 -> 0, of which waited for: 2 -> 0; matrix products, arithmetic and copies ran while one was open for 0% -> 0% of each run, Pallas kernels for 0% -> 0%
where the time goes in v2:
time: 314 us; the launch traced here: 310 us
  Pallas kernels  119 us (38%)
  other arithmetic  91.9 us (29%)
  blocking collectives  58.4 us (19%)
  local copies, waits for them, and re-layouts  24.1 us (8%)
  matrix products  15.9 us (5%)
    pallas_call x2, Pallas kernels, col_reduce_scatter(): pl.pallas_call(functools.partial(reduce_scatter_kernel, n), out_shape=jax...  119 us
    scatter-add x2, other arithmetic, add_block(): return totals.at[row_ids_all].add(products)  78.8 us
    all_gather x2, blocking collectives, shards(): lax.all_gather(source, 'row', axis=0, tiled=True)  58.4 us
    dot_general x2, matrix products, add_block(): jnp.einsum('tab,tbf->taf', dev_tiles, inputs, preferred_element_type=jnp....  15.9 us
    convert_element_type x2, other arithmetic, col_reduce_scatter(): pieces = partial_rows.reshape(n, nodes_dev, feat_width).astype(jnp.bfloat16)  8.12 us
    reshape x1, local copies, waits for them, and re-layouts, shards(): dev_tiles = adj_tiles.reshape(tile_slots, TILE, TILE)  6.64 us

profile of v2, /device:TPU:8, one launch (start us, length us, event | category | flops | bytes accessed | tf_op | source)
XLA Modules:
  0.0 310.0 jit_solution(337625941309179392)
XLA Ops:
  0.0 0.7 broadcast_multiply_fusion
  0.7 0.9 fusion.5
  1.6 29.2 %all_gather.6 = bf16[2048,128]{1,0:T(8,128)(2,1)S(1)} all-gather(bf16[256,128]{1,0:T(8,128)(2,1)S(1)} %fusion.5), channel_id=1, replica_groups=mesh['row'=8,'col'=32] {'row'}, dimensions={0}, use_global_device_ids=true | all-gather | bytes 589824 | tf_op jit(solution)/shard_map/all_gather | solution.py:113
  30.8 0.7 compare_select_fusion
  31.5 3.0 gather_fusion
  34.6 3.3 %copy.7 = bf16[1,1,256,4096]{2,3,1,0:T(8,128)(2,1)S(1)} copy(bf16[1,1,256,4096]{3,2,1,0:T(8,128)(2,1)} %param.8) | data formatting | bytes 4194304 | tf_op args[2]
  37.8 6.6 %copy.8 = bf16[256,64,64]{2,1,0:T(8,128)(2,1)} copy(bf16[256,64,64]{0,2,1:T(8,128)(2,1)S(1)} %bitcast.29) | data formatting | bytes 4194304 | tf_op jit(solution)/shard_map/reshape | solution.py:101
  45.2 0.0 copy-start.1
  45.2 7.9 %select_bitcast_fusion.1 = f32[256,64,128]{2,1,0:T(8,128)} fusion(pred[256]{0:T(512)(128)(4,1)S(1)} %iota_compare_fusion, bf16[256,64,64]{2,1,0:T(8,128)(2,1)} %copy.8, bf16[256,64,128]{2,1,0:T(8,128)(2,1)} %gather_fusion), kind=kOutput, calls=%fused_computation.5 | convolution fusion | flops 270532608 | bytes 14680320 | tf_op jit(solution)/shard_map/while/body/eval_jaxpr/tab,tbf->taf/dot_general | solution.py:119
  53.1 2.5 broadcast.71.clone
  55.6 39.4 %scatter_fusion = f32[128,64,128]{2,1,0:T(8,128)} fusion(f32[128,64,128]{2,1,0:T(8,128)} %broadcast.71.clone, s32[256]{0:T(256)S(1)} %bitcast.30, f32[256,64,128]{2,1,0:T(8,128)} %select_bitcast_fusion.1), kind=kCustom, calls=%fused_computation.2 | custom fusion | flops 2097152 | bytes 25166848 | tf_op jit(solution)/shard_map/while/body/eval_jaxpr/scatter-add | solution.py:123
  95.0 1.6 constant_dynamic-slice_fusion.1.own_ref
  96.6 4.1 %convert_element_type.29 = bf16[128,64,128]{2,1,0:T(8,128)(2,1)} convert(f32[128,64,128]{2,1,0:T(8,128)} %scatter_fusion) | non-fusion elementwise | flops 1048576 | bytes 6291456 | tf_op jit(solution)/shard_map/convert_element_type | solution.py:81
  100.7 59.2 %shard_map.64 = f32[256,128]{1,0:T(8,128)} custom-call(bf16[32,256,128]{2,1,0:T(8,128)(2,1)} %bitcast.27, f32[256,128]{1,0:T(8,128)} %constant_dynamic-slice_fusion.1.own_ref), custom_call_target="tpu_custom_call" | custom-call | tf_op jit(solution)/shard_map/pallas_call | solution.py:82
  159.9 1.0 fusion.3
  160.9 29.2 %all_gather.7 = bf16[2048,128]{1,0:T(8,128)(2,1)S(1)} all-gather(bf16[256,128]{1,0:T(8,128)(2,1)S(1)} %fusion.3), channel_id=1, replica_groups=mesh['row'=8,'col'=32] {'row'}, dimensions={0}, use_global_device_ids=true | all-gather | bytes 589824 | tf_op jit(solution)/shard_map/all_gather | solution.py:113
  190.1 3.1 gather_fusion.1
  193.2 7.9 %select_bitcast_fusion = f32[256,64,128]{2,1,0:T(8,128)} fusion(pred[256]{0:T(512)(128)(4,1)S(1)} %iota_compare_fusion, bf16[256,64,64]{2,1,0:T(8,128)(2,1)} %copy.8, bf16[256,64,128]{2,1,0:T(8,128)(2,1)} %gather_fusion.1), kind=kOutput, calls=%fused_computation.4 | convolution fusion | flops 270532608 | bytes 14680320 | tf_op jit(solution)/shard_map/while/body/eval_jaxpr/tab,tbf->taf/dot_general | solution.py:119
  201.1 2.5 broadcast.71
  203.6 39.4 %scatter_fusion.1 = f32[128,64,128]{2,1,0:T(8,128)} fusion(f32[128,64,128]{2,1,0:T(8,128)} %broadcast.71, s32[256]{0:T(256)S(1)} %bitcast.31, f32[256,64,128]{2,1,0:T(8,128)} %select_bitcast_fusion), kind=kCustom, calls=%fused_computation.3 | custom fusion | flops 2097152 | bytes 25166848 | tf_op jit(solution)/shard_map/while/body/eval_jaxpr/scatter-add | solution.py:123
  243.0 1.6 constant_dynamic-slice_fusion.own_ref
  244.6 4.0 %convert_element_type.32 = bf16[128,64,128]{2,1,0:T(8,128)(2,1)} convert(f32[128,64,128]{2,1,0:T(8,128)} %scatter_fusion.1) | non-fusion elementwise | flops 1048576 | bytes 6291456 | tf_op jit(solution)/shard_map/convert_element_type | solution.py:81
  248.6 59.7 %shard_map.65 = f32[256,128]{1,0:T(8,128)} custom-call(bf16[32,256,128]{2,1,0:T(8,128)(2,1)} %bitcast.28, f32[256,128]{1,0:T(8,128)} %constant_dynamic-slice_fusion.own_ref), custom_call_target="tpu_custom_call" | custom-call | tf_op jit(solution)/shard_map/pallas_call | solution.py:82
  308.3 1.6 fusion.4
  (6 shorter events, 0.0 us)
Async XLA Ops:
  45.2 8.0 %copy-start.1 = (s32[1,1,256]{2,1,0:T(1,128)S(1)}, s32[1,1,256]{2,1,0:T(1,128)}, u32[]{:S(2)}) copy-start(s32[1,1,256]{2,1,0:T(1,128)} %param.9) | copy-start | bytes 3076
  96.6 63.3 %copy-start = (bf16[256,128]{1,0:T(8,128)(2,1)S(1)}, bf16[256,128]{1,0:T(8,128)(2,1)}, u32[]{:S(2)}) copy-start(bf16[256,128]{1,0:T(8,128)(2,1)} %param.6) | copy-start | bytes 196612

commit v3 on v2

--- a/solution.py
+++ b/solution.py
@@ -73,12 +73,8 @@
     lax.fori_loop(1, n, drain, 0)
 
 
-def col_reduce_scatter(partial_rows, nodes_dev):
-    n = lax.axis_size("col")
-    feat_width = partial_rows.shape[1]
-    me = lax.axis_index("col")
-    own = lax.dynamic_slice_in_dim(partial_rows, me * nodes_dev, nodes_dev, 0)
-    pieces = partial_rows.reshape(n, nodes_dev, feat_width).astype(jnp.bfloat16)
+def col_reduce_scatter(pieces, own):
+    n, nodes_dev, feat_width = pieces.shape
     return pl.pallas_call(
         functools.partial(reduce_scatter_kernel, n),
         out_shape=jax.ShapeDtypeStruct((nodes_dev, feat_width), jnp.float32),
@@ -93,6 +89,55 @@
     )(pieces, own)
 
 
+def block_product_kernel(group, rows_ref, cols_ref, count_ref, adj_ref, panel_ref,
+                         pieces_ref, own_ref, acc_ref):
+    acc_ref[...] = jnp.zeros_like(acc_ref)
+    count = count_ref[0]
+    slots = adj_ref.shape[0]
+
+    def body(g, carry):
+        base = g * group
+        prods = []
+        for i in range(group):
+            t = base + i
+            p = jnp.dot(adj_ref[t], panel_ref[cols_ref[t]], preferred_element_type=jnp.float32)
+            prods.append(jnp.where(t < count, p, jnp.zeros_like(p)))
+        for i in range(group):
+            r = rows_ref[base + i]
+            acc_ref[r] += prods[i]
+        return carry
+
+    lax.fori_loop(0, slots // group, body, 0)
+    pieces_ref[...] = acc_ref[...].astype(pieces_ref.dtype)
+    per_piece = own_ref.shape[0]
+    me = lax.axis_index("col")
+    own_ref[...] = acc_ref[pl.ds(me * per_piece, per_piece)]
+
+
+def block_product(row_ids, col_ids, count, dev_tiles, col_panel, row_tiles, nodes_dev):
+    slots = dev_tiles.shape[0]
+    feat_width = col_panel.shape[2]
+    per_piece = nodes_dev // TILE
+    group = 4 if slots % 4 == 0 else 1
+    smem = pl.BlockSpec(memory_space=pltpu.SMEM)
+    vmem = pl.BlockSpec(memory_space=pltpu.VMEM)
+    return pl.pallas_call(
+        functools.partial(block_product_kernel, group),
+        out_shape=(
+            jax.ShapeDtypeStruct((row_tiles, TILE, feat_width), jnp.bfloat16),
+            jax.ShapeDtypeStruct((per_piece, TILE, feat_width), jnp.float32),
+        ),
+        in_specs=[smem, smem, smem, vmem, vmem],
+        out_specs=(vmem, vmem),
+        scratch_shapes=[pltpu.VMEM((row_tiles, TILE, feat_width), jnp.float32)],
+        cost_estimate=pl.CostEstimate(
+            flops=2 * slots * TILE * TILE * feat_width,
+            bytes_accessed=slots * TILE * TILE * 2 + row_tiles * TILE * feat_width * 2,
+            transcendentals=0,
+        ),
+    )(row_ids, col_ids, count, dev_tiles, col_panel)
+
+
 def shards(features, degrees, adj_tiles, tile_rows, tile_cols, tile_counts):
     col_count = lax.axis_size("col")
     nodes_dev = features.shape[0]
@@ -101,9 +146,7 @@
     dev_tiles = adj_tiles.reshape(tile_slots, TILE, TILE)
     row_ids_all = tile_rows.reshape(tile_slots)
     col_ids_all = tile_cols.reshape(tile_slots)
-    live_count = tile_counts.reshape(())
-    block_len = min(256, tile_slots)
-    num_turns = tile_slots // block_len
+    live_count = tile_counts.reshape(1)
     row_tiles = nodes_dev * col_count // TILE
     norm_scale = jnp.sqrt(KNN / degrees.astype(jnp.float32))[:, None]
     teleport = ALPHA * features.astype(jnp.float32)
@@ -111,21 +154,12 @@
     for repeat in range(STEPS):
         source = (norm_scale * current).astype(jnp.bfloat16)
         col_panel = lax.all_gather(source, "row", axis=0, tiled=True).reshape(-1, TILE, feat_width)
-
-        def add_block(turn_index, totals):
-            first_tile = turn_index * block_len
-            live_mask = first_tile + jnp.arange(block_len, dtype=jnp.int32) < live_count
-            inputs = col_panel[col_ids_all]
-            products = jnp.einsum(
-                "tab,tbf->taf", dev_tiles, inputs, preferred_element_type=jnp.float32
-            )
-            products = jnp.where(live_mask[:, None, None], products, jnp.zeros_like(products))
-            return totals.at[row_ids_all].add(products)
-
-        start_tot = jnp.zeros((row_tiles, TILE, feat_width), jnp.float32)
-        totals = lax.fori_loop(0, num_turns, add_block, start_tot)
-        partial_rows = totals.reshape(row_tiles * TILE, feat_width)
-        own_rows = col_reduce_scatter(partial_rows, nodes_dev)
+        pieces, own = block_product(
+            row_ids_all, col_ids_all, live_count, dev_tiles, col_panel, row_tiles, nodes_dev
+        )
+        own_rows = col_reduce_scatter(
+            pieces.reshape(col_count, nodes_dev, feat_width), own.reshape(nodes_dev, feat_width)
+        )
         current = (1.0 - ALPHA) * norm_scale * own_rows + teleport
     return current.astype(jnp.bfloat16)
 

time: 314 us -> 228 us (0.73)
  other arithmetic: 91.9 us -> 4.31 us
  Pallas kernels: 119 us -> 148 us
  matrix products: 15.9 us -> 0 us
  local copies, waits for them, and re-layouts: 24.1 us -> 9.97 us
  blocking collectives: 58.4 us -> 62.2 us
    scatter-add x2 -> x0, other arithmetic: 78.8 us -> none  [add_block(): return totals.at[row_ids_all].add(products)]
    pallas_call x0 -> x2, Pallas kernels: none -> 28.8 us  [block_product(): pl.pallas_call(functools.partial(block_product_kernel, group), out_shape=...]
    dot_general x2 -> x0, matrix products: 15.9 us -> none  [add_block(): jnp.einsum('tab,tbf->taf', dev_tiles, inputs, preferred_element_type=jnp....]
    convert_element_type x2 -> x0, other arithmetic: 8.12 us -> none  [col_reduce_scatter(): pieces = partial_rows.reshape(n, nodes_dev, feat_width).astype(jnp.bfloat16)]
    gather x2 -> x0, local copies, waits for them, and re-layouts: 6.1 us -> none  [add_block(): inputs = col_panel[col_ids_all]]
    another operation x2 -> x0, local copies, waits for them, and re-layouts: 4.99 us -> none
    all_gather x2, blocking collectives: 58.4 us -> 62.2 us  [shards(): lax.all_gather(source, 'row', axis=0, tiled=True)]
where the time goes in v3:
time: 228 us; the launch traced here: 225 us
  Pallas kernels  148 us (65%)
  blocking collectives  62.2 us (27%)
  local copies, waits for them, and re-layouts  9.97 us (4%)
  other arithmetic  4.31 us (2%)
    pallas_call x2, Pallas kernels, col_reduce_scatter(): pl.pallas_call(functools.partial(reduce_scatter_kernel, n), out_shape=jax...  119 us
    all_gather x2, blocking collectives, shards(): lax.all_gather(source, 'row', axis=0, tiled=True)  62.2 us
    pallas_call x2, Pallas kernels, block_product(): pl.pallas_call(functools.partial(block_product_kernel, group), out_shape=...  28.8 us
    reshape x1, local copies, waits for them, and re-layouts, shards(): dev_tiles = adj_tiles.reshape(tile_slots, TILE, TILE)  6.7 us

profile of v3, /device:TPU:8, one launch (start us, length us, event | category | flops | bytes accessed | tf_op | source)
XLA Modules:
  0.0 225.0 jit_solution(17104781000357126488)
XLA Ops:
  0.7 0.7 broadcast_multiply_fusion
  1.3 0.9 fusion.5
  2.3 31.1 %all_gather.6 = bf16[2048,128]{1,0:T(8,128)(2,1)} all-gather(bf16[256,128]{1,0:T(8,128)(2,1)S(1)} %fusion.5), channel_id=1, replica_groups=mesh['row'=8,'col'=32] {'row'}, dimensions={0}, use_global_device_ids=true | all-gather | bytes 589824 | tf_op jit(solution)/shard_map/all_gather | solution.py:156
  33.4 3.3 %copy.7 = bf16[1,1,256,4096]{2,3,1,0:T(8,128)(2,1)S(1)} copy(bf16[1,1,256,4096]{3,2,1,0:T(8,128)(2,1)} %param.8) | data formatting | bytes 4194304 | tf_op args[2]
  36.6 6.7 %copy.9.adj_ref = bf16[256,64,64]{2,1,0:T(8,128)(2,1)} copy(bf16[256,64,64]{0,2,1:T(8,128)(2,1)S(1)} %bitcast.12) | data formatting | bytes 4194304 | tf_op jit(solution)/shard_map/reshape | solution.py:146
  43.3 14.4 %shard_map.64 = (bf16[128,64,128]{2,1,0:T(8,128)(2,1)}, f32[4,64,128]{2,1,0:T(8,128)}) custom-call(s32[256]{0:T(256)} %bitcast.19, s32[256]{0:T(256)} %bitcast.21, s32[1]{0:T(128)} %bitcast.10.count_ref, bf16[256,64,64]{2,1,0:T(8,128)(2,1)} %copy.9.adj_ref, bf16[32,64,128]{2,1,0:T(8,128)(2,1)} %bitcast.13), custom_call_target="tpu_custom_call" | custom-call | flops 268435456 | bytes 4194304 | tf_op jit(solution)/shard_map/pallas_call | solution.py:124
  57.7 0.0 copy-start
  57.7 59.5 %shard_map.65 = f32[256,128]{1,0:T(8,128)} custom-call(bf16[32,256,128]{2,1,0:T(8,128)(2,1)} %bitcast.16, f32[256,128]{1,0:T(8,128)} %bitcast.18), custom_call_target="tpu_custom_call" | custom-call | tf_op jit(solution)/shard_map/pallas_call | solution.py:78
  117.2 0.0 copy-done
  117.2 1.0 fusion.3
  118.3 31.1 %all_gather.7 = bf16[2048,128]{1,0:T(8,128)(2,1)} all-gather(bf16[256,128]{1,0:T(8,128)(2,1)S(1)} %fusion.3), channel_id=1, replica_groups=mesh['row'=8,'col'=32] {'row'}, dimensions={0}, use_global_device_ids=true | all-gather | bytes 589824 | tf_op jit(solution)/shard_map/all_gather | solution.py:156
  149.4 14.4 %shard_map.66 = (bf16[128,64,128]{2,1,0:T(8,128)(2,1)}, f32[4,64,128]{2,1,0:T(8,128)}) custom-call(s32[256]{0:T(256)} %bitcast.20, s32[256]{0:T(256)} %bitcast.22, s32[1]{0:T(128)} %bitcast.11.count_ref, bf16[256,64,64]{2,1,0:T(8,128)(2,1)} %copy.9.adj_ref, bf16[32,64,128]{2,1,0:T(8,128)(2,1)} %bitcast.14), custom_call_target="tpu_custom_call" | custom-call | flops 268435456 | bytes 4194304 | tf_op jit(solution)/shard_map/pallas_call | solution.py:124
  163.8 59.6 %shard_map.67 = f32[256,128]{1,0:T(8,128)} custom-call(bf16[32,256,128]{2,1,0:T(8,128)(2,1)} %bitcast.15, f32[256,128]{1,0:T(8,128)} %bitcast.17), custom_call_target="tpu_custom_call" | custom-call | tf_op jit(solution)/shard_map/pallas_call | solution.py:78
  223.4 1.6 fusion.4
Async XLA Ops:
  57.7 59.5 %copy-start = (bf16[256,128]{1,0:T(8,128)(2,1)S(1)}, bf16[256,128]{1,0:T(8,128)(2,1)}, u32[]{:S(2)}) copy-start(bf16[256,128]{1,0:T(8,128)(2,1)} %param.6) | copy-start | bytes 196612

commit v4 on v3

--- a/solution.py
+++ b/solution.py
@@ -87,6 +87,60 @@
         ],
         compiler_params=pltpu.CompilerParams(collective_id=0, has_side_effects=True),
     )(pieces, own)
+
+
+def all_gather_kernel(n, src_ref, out_ref, send_sem, recv_sem):
+    me = lax.axis_index("row")
+    col = lax.axis_index("col")
+
+    barrier = pltpu.get_barrier_semaphore()
+
+    def greet(k, carry):
+        peer = lax.rem(me + k, n)
+        pl.semaphore_signal(barrier, inc=1, device_id=(peer, col), device_id_type=MESH)
+        return carry
+
+    lax.fori_loop(1, n, greet, 0)
+    pl.semaphore_wait(barrier, n - 1)
+
+    def copy(peer, slot):
+        return pltpu.make_async_remote_copy(
+            src_ref=src_ref,
+            dst_ref=out_ref.at[slot],
+            send_sem=send_sem.at[peer],
+            recv_sem=recv_sem.at[slot],
+            device_id=(peer, col),
+            device_id_type=MESH,
+        )
+
+    def start(k, carry):
+        copy(lax.rem(me + k, n), me).start()
+        return carry
+
+    lax.fori_loop(1, n, start, 0)
+    out_ref[me] = src_ref[...]
+
+    def finish(k, carry):
+        sender = lax.rem(me + n - k, n)
+        copy(sender, sender).wait_recv()
+        copy(lax.rem(me + k, n), me).wait_send()
+        return carry
+
+    lax.fori_loop(1, n, finish, 0)
+
+
+def row_all_gather(source):
+    n = lax.axis_size("row")
+    nodes_dev, feat_width = source.shape
+    vmem = pl.BlockSpec(memory_space=pltpu.VMEM)
+    return pl.pallas_call(
+        functools.partial(all_gather_kernel, n),
+        out_shape=jax.ShapeDtypeStruct((n, nodes_dev, feat_width), source.dtype),
+        in_specs=[vmem],
+        out_specs=vmem,
+        scratch_shapes=[pltpu.SemaphoreType.DMA((n,)), pltpu.SemaphoreType.DMA((n,))],
+        compiler_params=pltpu.CompilerParams(collective_id=1, has_side_effects=True),
+    )(source)
 
 
 def block_product_kernel(group, rows_ref, cols_ref, count_ref, adj_ref, panel_ref,
@@ -153,7 +207,7 @@
     current = features.astype(jnp.float32)
     for repeat in range(STEPS):
         source = (norm_scale * current).astype(jnp.bfloat16)
-        col_panel = lax.all_gather(source, "row", axis=0, tiled=True).reshape(-1, TILE, feat_width)
+        col_panel = row_all_gather(source).reshape(-1, TILE, feat_width)
         pieces, own = block_product(
             row_ids_all, col_ids_all, live_count, dev_tiles, col_panel, row_tiles, nodes_dev
         )

time: 228 us -> 192 us (0.84)
  blocking collectives: 62.2 us -> 0 us
  Pallas kernels: 148 us -> 174 us
    all_gather x2 -> x0, blocking collectives: 62.2 us -> none  [shards(): lax.all_gather(source, 'row', axis=0, tiled=True)]
    pallas_call x0 -> x2, Pallas kernels: none -> 26.9 us  [row_all_gather(): pl.pallas_call(functools.partial(all_gather_kernel, n), out_shape=jax.Sha...]
where the time goes in v4:
time: 192 us; the launch traced here: 191 us
  Pallas kernels  174 us (91%)
  local copies, waits for them, and re-layouts  9.98 us (5%)
  other arithmetic  5.58 us (3%)
    pallas_call x2, Pallas kernels, col_reduce_scatter(): pl.pallas_call(functools.partial(reduce_scatter_kernel, n), out_shape=jax...  119 us
    pallas_call x2, Pallas kernels, block_product(): pl.pallas_call(functools.partial(block_product_kernel, group), out_shape=...  28.8 us
    pallas_call x2, Pallas kernels, row_all_gather(): pl.pallas_call(functools.partial(all_gather_kernel, n), out_shape=jax.Sha...  26.9 us
    reshape x1, local copies, waits for them, and re-layouts, shards(): dev_tiles = adj_tiles.reshape(tile_slots, TILE, TILE)  6.7 us

profile of v4, /device:TPU:8, one launch (start us, length us, event | category | flops | bytes accessed | tf_op | source)
XLA Modules:
  0.0 190.6 jit_solution(16488587519012371907)
XLA Ops:
  0.7 0.7 broadcast_multiply_fusion
  1.3 1.6 fusion.5.src_ref
  2.9 13.3 %shard_map.64 = bf16[8,256,128]{2,1,0:T(8,128)(2,1)} custom-call(bf16[256,128]{1,0:T(8,128)(2,1)} %fusion.5.src_ref), custom_call_target="tpu_custom_call" | custom-call | tf_op jit(solution)/shard_map/pallas_call | solution.py:136
  16.3 3.3 %copy.7 = bf16[1,1,256,4096]{2,3,1,0:T(8,128)(2,1)S(1)} copy(bf16[1,1,256,4096]{3,2,1,0:T(8,128)(2,1)} %param.8) | data formatting | bytes 4194304 | tf_op args[2]
  19.5 6.7 %copy.9.adj_ref = bf16[256,64,64]{2,1,0:T(8,128)(2,1)} copy(bf16[256,64,64]{0,2,1:T(8,128)(2,1)S(1)} %bitcast.12) | data formatting | bytes 4194304 | tf_op jit(solution)/shard_map/reshape | solution.py:200
  26.2 14.4 %shard_map.65 = (bf16[128,64,128]{2,1,0:T(8,128)(2,1)}, f32[4,64,128]{2,1,0:T(8,128)}) custom-call(s32[256]{0:T(256)} %bitcast.19, s32[256]{0:T(256)} %bitcast.21, s32[1]{0:T(128)} %bitcast.10.count_ref, bf16[256,64,64]{2,1,0:T(8,128)(2,1)} %copy.9.adj_ref, bf16[32,64,128]{2,1,0:T(8,128)(2,1)} %bitcast.13), custom_call_target="tpu_custom_call" | custom-call | flops 268435456 | bytes 4194304 | tf_op jit(solution)/shard_map/pallas_call | solution.py:178
  40.6 0.0 copy-start
  40.6 59.2 %shard_map.66 = f32[256,128]{1,0:T(8,128)} custom-call(bf16[32,256,128]{2,1,0:T(8,128)(2,1)} %bitcast.16, f32[256,128]{1,0:T(8,128)} %bitcast.18), custom_call_target="tpu_custom_call" | custom-call | tf_op jit(solution)/shard_map/pallas_call | solution.py:78
  99.9 0.0 copy-done
  99.9 1.7 fusion.3.src_ref
  101.6 13.5 %shard_map.67 = bf16[8,256,128]{2,1,0:T(8,128)(2,1)} custom-call(bf16[256,128]{1,0:T(8,128)(2,1)} %fusion.3.src_ref), custom_call_target="tpu_custom_call" | custom-call | tf_op jit(solution)/shard_map/pallas_call | solution.py:136
  115.1 14.4 %shard_map.68 = (bf16[128,64,128]{2,1,0:T(8,128)(2,1)}, f32[4,64,128]{2,1,0:T(8,128)}) custom-call(s32[256]{0:T(256)} %bitcast.20, s32[256]{0:T(256)} %bitcast.22, s32[1]{0:T(128)} %bitcast.11.count_ref, bf16[256,64,64]{2,1,0:T(8,128)(2,1)} %copy.9.adj_ref, bf16[32,64,128]{2,1,0:T(8,128)(2,1)} %bitcast.14), custom_call_target="tpu_custom_call" | custom-call | flops 268435456 | bytes 4194304 | tf_op jit(solution)/shard_map/pallas_call | solution.py:178
  129.5 59.5 %shard_map.69 = f32[256,128]{1,0:T(8,128)} custom-call(bf16[32,256,128]{2,1,0:T(8,128)(2,1)} %bitcast.15, f32[256,128]{1,0:T(8,128)} %bitcast.17), custom_call_target="tpu_custom_call" | custom-call | tf_op jit(solution)/shard_map/pallas_call | solution.py:78
  189.0 1.6 fusion.4
Async XLA Ops:
  40.6 59.2 %copy-start = (bf16[256,128]{1,0:T(8,128)(2,1)S(1)}, bf16[256,128]{1,0:T(8,128)(2,1)}, u32[]{:S(2)}) copy-start(bf16[256,128]{1,0:T(8,128)(2,1)} %param.6) | copy-start | bytes 196612

commit v5 on v4

--- a/solution.py
+++ b/solution.py
@@ -16,77 +16,100 @@
 ALPHA = 0.1
 
 
-def reduce_scatter_kernel(n, part_ref, own_ref, out_ref, recv, send_sem, recv_sem):
-    me = lax.axis_index("col")
+CORES = 2
+Z_RING = 8
+
+
+def reduce_scatter_kernel(n_z, x_ref, out_ref, ra, sa, cw_recv, ccw_recv, cw_send, ccw_send,
+                          fin, y_recv, a_sems, cw_sems, ccw_sems, y_sems):
+    c = lax.axis_index("col")
     row = lax.axis_index("row")
+    core = lax.rem(c, CORES)
+    z = lax.rem(c // CORES, n_z)
+    yh = c // (CORES * n_z)
+
+    def dev(yh_, z_, core_):
+        return (row, (yh_ * n_z + z_) * CORES + core_)
+
+    partner = dev(yh, z, 1 - core)
+    right = dev(yh, lax.rem(z + 1, n_z), core)
+    left = dev(yh, lax.rem(z + n_z - 1, n_z), core)
+    y_partner = dev(1 - yh, z, core)
 
     barrier = pltpu.get_barrier_semaphore()
-
-    def greet(k, carry):
-        peer = lax.rem(me + k, n)
-        pl.semaphore_signal(barrier, inc=1, device_id=(row, peer), device_id_type=MESH)
-        return carry
-
-    lax.fori_loop(1, n, greet, 0)
-    pl.semaphore_wait(barrier, n - 1)
-
-    def send(peer):
+    for peer in (partner, right, left, y_partner):
+        pl.semaphore_signal(barrier, inc=1, device_id=peer, device_id_type=MESH)
+    pl.semaphore_wait(barrier, 4)
+
+    def rcopy(src, dst, sems, k, peer):
         return pltpu.make_async_remote_copy(
-            src_ref=part_ref.at[peer],
-            dst_ref=recv.at[me],
-            send_sem=send_sem.at[peer],
-            recv_sem=recv_sem.at[me],
-            device_id=(row, peer),
-            device_id_type=MESH,
+            src_ref=src, dst_ref=dst, send_sem=sems.at[0, k], recv_sem=sems.at[1, k],
+            device_id=peer, device_id_type=MESH,
         )
 
-    def arrival(sender):
-        return pltpu.make_async_remote_copy(
-            src_ref=part_ref.at[sender],
-            dst_ref=recv.at[sender],
-            send_sem=send_sem.at[sender],
-            recv_sem=recv_sem.at[sender],
-            device_id=(row, sender),
-            device_id_type=MESH,
-        )
-
-    def start(k, carry):
-        send(lax.rem(me + k, n)).start()
-        return carry
-
-    lax.fori_loop(1, n, start, 0)
-
-    out_ref[...] = own_ref[...]
-
-    def finish(k, carry):
-        sender = lax.rem(me + n - k, n)
-        arrival(sender).wait_recv()
-        out_ref[...] += recv[sender].astype(jnp.float32)
-        return carry
-
-    lax.fori_loop(1, n, finish, 0)
-
-    def drain(k, carry):
-        send(lax.rem(me + k, n)).wait_send()
-        return carry
-
-    lax.fori_loop(1, n, drain, 0)
-
-
-def col_reduce_scatter(pieces, own):
-    n, nodes_dev, feat_width = pieces.shape
+    copy_a = rcopy(x_ref.at[1 - core], ra, a_sems, 0, partner)
+    copy_a.start()
+    copy_a.wait_recv()
+    sa[...] = x_ref[core] + ra[...]
+
+    sends = [copy_a]
+    for s in range(n_z - 1):
+        g_cw = lax.rem(z + (n_z - s - 1), n_z)
+        g_ccw = lax.rem(z + s + 1, n_z)
+        src_cw = sa.at[g_cw, 0] if s == 0 else cw_send.at[s - 1]
+        src_ccw = sa.at[g_ccw, 1] if s == 0 else ccw_send.at[s - 1]
+        copy_cw = rcopy(src_cw, cw_recv.at[s], cw_sems, s, right)
+        copy_ccw = rcopy(src_ccw, ccw_recv.at[s], ccw_sems, s, left)
+        copy_cw.start()
+        copy_ccw.start()
+        sends += [copy_cw, copy_ccw]
+        got_cw = lax.rem(z + (2 * n_z - s - 2), n_z)
+        got_ccw = lax.rem(z + s + 2, n_z)
+        copy_cw.wait_recv()
+        if s < n_z - 2:
+            cw_send[s] = cw_recv[s] + sa[got_cw, 0]
+        else:
+            fin[0] = cw_recv[s] + sa[got_cw, 0]
+        copy_ccw.wait_recv()
+        if s < n_z - 2:
+            ccw_send[s] = ccw_recv[s] + sa[got_ccw, 1]
+        else:
+            fin[1] = ccw_recv[s] + sa[got_ccw, 1]
+
+    copy_y = rcopy(fin.at[1 - yh], y_recv, y_sems, 0, y_partner)
+    copy_y.start()
+    sends.append(copy_y)
+    copy_y.wait_recv()
+    out_ref[...] = fin[yh] + y_recv[...]
+    for cp in sends:
+        cp.wait_send()
+
+
+def col_reduce_scatter(pieces):
+    cores, n_z, n_y, nodes_dev, feat_width = pieces.shape
+    piece = (nodes_dev, feat_width)
+    vmem = pl.BlockSpec(memory_space=pltpu.VMEM)
     return pl.pallas_call(
-        functools.partial(reduce_scatter_kernel, n),
-        out_shape=jax.ShapeDtypeStruct((nodes_dev, feat_width), jnp.float32),
-        in_specs=[pl.BlockSpec(memory_space=pltpu.VMEM)] * 2,
-        out_specs=pl.BlockSpec(memory_space=pltpu.VMEM),
+        functools.partial(reduce_scatter_kernel, n_z),
+        out_shape=jax.ShapeDtypeStruct(piece, jnp.float32),
+        in_specs=[vmem],
+        out_specs=vmem,
         scratch_shapes=[
-            pltpu.VMEM((n, nodes_dev, feat_width), jnp.bfloat16),
-            pltpu.SemaphoreType.DMA((n,)),
-            pltpu.SemaphoreType.DMA((n,)),
+            pltpu.VMEM((n_z, n_y) + piece, jnp.float32),
+            pltpu.VMEM((n_z, n_y) + piece, jnp.float32),
+            pltpu.VMEM((n_z - 1,) + piece, jnp.float32),
+            pltpu.VMEM((n_z - 1,) + piece, jnp.float32),
+            pltpu.VMEM((n_z - 1,) + piece, jnp.float32),
+            pltpu.VMEM((n_z - 1,) + piece, jnp.float32),
+            pltpu.VMEM((n_y,) + piece, jnp.float32),
+            pltpu.VMEM(piece, jnp.float32),
+            pltpu.SemaphoreType.DMA((2, 1)),
+            pltpu.SemaphoreType.DMA((2, n_z - 1)),
+            pltpu.SemaphoreType.DMA((2, n_z - 1)),
+            pltpu.SemaphoreType.DMA((2, 1)),
         ],
         compiler_params=pltpu.CompilerParams(collective_id=0, has_side_effects=True),
-    )(pieces, own)
+    )(pieces)
 
 
 def all_gather_kernel(n, src_ref, out_ref, send_sem, recv_sem):
@@ -144,7 +167,7 @@
 
 
 def block_product_kernel(group, rows_ref, cols_ref, count_ref, adj_ref, panel_ref,
-                         pieces_ref, own_ref, acc_ref):
+                         pieces_ref, acc_ref):
     acc_ref[...] = jnp.zeros_like(acc_ref)
     count = count_ref[0]
     slots = adj_ref.shape[0]
@@ -162,10 +185,10 @@
         return carry
 
     lax.fori_loop(0, slots // group, body, 0)
-    pieces_ref[...] = acc_ref[...].astype(pieces_ref.dtype)
-    per_piece = own_ref.shape[0]
-    me = lax.axis_index("col")
-    own_ref[...] = acc_ref[pl.ds(me * per_piece, per_piece)]
+    cores, n_z, n_y, per_piece = pieces_ref.shape[:4]
+    for j in range(cores * n_z * n_y):
+        core_j, z_j, yh_j = j % cores, (j // cores) % n_z, j // (cores * n_z)
+        pieces_ref[core_j, z_j, yh_j] = acc_ref[j * per_piece:(j + 1) * per_piece]
 
 
 def block_product(row_ids, col_ids, count, dev_tiles, col_panel, row_tiles, nodes_dev):
@@ -177,16 +200,16 @@
     vmem = pl.BlockSpec(memory_space=pltpu.VMEM)
     return pl.pallas_call(
         functools.partial(block_product_kernel, group),
-        out_shape=(
-            jax.ShapeDtypeStruct((row_tiles, TILE, feat_width), jnp.bfloat16),
-            jax.ShapeDtypeStruct((per_piece, TILE, feat_width), jnp.float32),
+        out_shape=jax.ShapeDtypeStruct(
+            (CORES, Z_RING, row_tiles // (per_piece * CORES * Z_RING), per_piece, TILE, feat_width),
+            jnp.float32,
         ),
         in_specs=[smem, smem, smem, vmem, vmem],
-        out_specs=(vmem, vmem),
+        out_specs=vmem,
         scratch_shapes=[pltpu.VMEM((row_tiles, TILE, feat_width), jnp.float32)],
         cost_estimate=pl.CostEstimate(
             flops=2 * slots * TILE * TILE * feat_width,
-            bytes_accessed=slots * TILE * TILE * 2 + row_tiles * TILE * feat_width * 2,
+            bytes_accessed=slots * TILE * TILE * 2 + row_tiles * TILE * feat_width * 4,
             transcendentals=0,
         ),
     )(row_ids, col_ids, count, dev_tiles, col_panel)
@@ -208,12 +231,10 @@
     for repeat in range(STEPS):
         source = (norm_scale * current).astype(jnp.bfloat16)
         col_panel = row_all_gather(source).reshape(-1, TILE, feat_width)
-        pieces, own = block_product(
+        pieces = block_product(
             row_ids_all, col_ids_all, live_count, dev_tiles, col_panel, row_tiles, nodes_dev
         )
-        own_rows = col_reduce_scatter(
-            pieces.reshape(col_count, nodes_dev, feat_width), own.reshape(nodes_dev, feat_width)
-        )
+        own_rows = col_reduce_scatter(pieces.reshape(pieces.shape[:3] + (nodes_dev, feat_width)))
         current = (1.0 - ALPHA) * norm_scale * own_rows + teleport
     return current.astype(jnp.bfloat16)
 

time: 192 us -> 173 us (0.901)
  Pallas kernels: 174 us -> 156 us
    pallas_call x2, Pallas kernels: 119 us -> 102 us  [col_reduce_scatter(): pl.pallas_call(functools.partial(reduce_scatter_kernel, n_z), out_shape=j...]
    pallas_call x2, Pallas kernels: 26.9 us -> 24 us  [row_all_gather(): pl.pallas_call(functools.partial(all_gather_kernel, n), out_shape=jax.Sha...]
where the time goes in v5:
time: 173 us
  Pallas kernels  156 us (90%)
  local copies, waits for them, and re-layouts  9.97 us (6%)
  other arithmetic  5.58 us (3%)
    pallas_call x2, Pallas kernels, col_reduce_scatter(): pl.pallas_call(functools.partial(reduce_scatter_kernel, n_z), out_shape=j...  102 us
    pallas_call x2, Pallas kernels, block_product(): pl.pallas_call(functools.partial(block_product_kernel, group), out_shape=...  30.1 us
    pallas_call x2, Pallas kernels, row_all_gather(): pl.pallas_call(functools.partial(all_gather_kernel, n), out_shape=jax.Sha...  24 us
    reshape x1, local copies, waits for them, and re-layouts, shards(): dev_tiles = adj_tiles.reshape(tile_slots, TILE, TILE)  6.69 us

profile of v5, /device:TPU:8, one launch (start us, length us, event | category | flops | bytes accessed | tf_op | source)
XLA Modules:
  0.0 172.7 jit_solution(7054842870860344198)
XLA Ops:
  0.7 0.7 broadcast_multiply_fusion
  1.3 1.6 fusion.5.src_ref
  2.9 13.4 %shard_map.64 = bf16[8,256,128]{2,1,0:T(8,128)(2,1)} custom-call(bf16[256,128]{1,0:T(8,128)(2,1)} %fusion.5.src_ref), custom_call_target="tpu_custom_call" | custom-call | tf_op jit(solution)/shard_map/pallas_call | solution.py:159
  16.3 3.3 %copy.7 = bf16[1,1,256,4096]{2,3,1,0:T(8,128)(2,1)S(1)} copy(bf16[1,1,256,4096]{3,2,1,0:T(8,128)(2,1)} %param.8) | data formatting | bytes 4194304 | tf_op args[2]
  19.6 6.7 %copy.9.adj_ref = bf16[256,64,64]{2,1,0:T(8,128)(2,1)} copy(bf16[256,64,64]{0,2,1:T(8,128)(2,1)S(1)} %bitcast.12) | data formatting | bytes 4194304 | tf_op jit(solution)/shard_map/reshape | solution.py:223
  26.3 15.1 %shard_map.65 = f32[2,8,2,4,64,128]{5,4,3,2,1,0:T(8,128)} custom-call(s32[256]{0:T(256)} %bitcast.15, s32[256]{0:T(256)} %bitcast.17, s32[1]{0:T(128)} %bitcast.8.count_ref, bf16[256,64,64]{2,1,0:T(8,128)(2,1)} %copy.9.adj_ref, bf16[32,64,128]{2,1,0:T(8,128)(2,1)} %bitcast.13), custom_call_target="tpu_custom_call" | custom-call | flops 268435456 | bytes 6291456 | tf_op jit(solution)/shard_map/pallas_call | solution.py:201
  41.3 0.0 copy-start
  41.3 53.3 %shard_map.66 = f32[256,128]{1,0:T(8,128)} custom-call(f32[2,8,2,256,128]{4,3,2,1,0:T(8,128)} %bitcast.11), custom_call_target="tpu_custom_call" | custom-call | tf_op jit(solution)/shard_map/pallas_call | solution.py:92
  94.6 0.0 copy-done
  94.6 1.7 fusion.3.src_ref
  96.3 10.6 %shard_map.67 = bf16[8,256,128]{2,1,0:T(8,128)(2,1)} custom-call(bf16[256,128]{1,0:T(8,128)(2,1)} %fusion.3.src_ref), custom_call_target="tpu_custom_call" | custom-call | tf_op jit(solution)/shard_map/pallas_call | solution.py:159
  106.9 15.1 %shard_map.68 = f32[2,8,2,4,64,128]{5,4,3,2,1,0:T(8,128)} custom-call(s32[256]{0:T(256)} %bitcast.16, s32[256]{0:T(256)} %bitcast.18, s32[1]{0:T(128)} %bitcast.9.count_ref, bf16[256,64,64]{2,1,0:T(8,128)(2,1)} %copy.9.adj_ref, bf16[32,64,128]{2,1,0:T(8,128)(2,1)} %bitcast.14), custom_call_target="tpu_custom_call" | custom-call | flops 268435456 | bytes 6291456 | tf_op jit(solution)/shard_map/pallas_call | solution.py:201
  122.0 49.1 %shard_map.69 = f32[256,128]{1,0:T(8,128)} custom-call(f32[2,8,2,256,128]{4,3,2,1,0:T(8,128)} %bitcast.10), custom_call_target="tpu_custom_call" | custom-call | tf_op jit(solution)/shard_map/pallas_call | solution.py:92
  171.1 1.6 fusion.4
Async XLA Ops:
  41.3 53.3 %copy-start = (bf16[256,128]{1,0:T(8,128)(2,1)S(1)}, bf16[256,128]{1,0:T(8,128)(2,1)}, u32[]{:S(2)}) copy-start(bf16[256,128]{1,0:T(8,128)(2,1)} %param.6) | copy-start | bytes 196612

commit v6 on v5

--- a/solution.py
+++ b/solution.py
@@ -20,7 +20,7 @@
 Z_RING = 8
 
 
-def reduce_scatter_kernel(n_z, x_ref, out_ref, ra, sa, cw_recv, ccw_recv, cw_send, ccw_send,
+def reduce_scatter_kernel(n_z, chunks, x_ref, out_ref, ra, recv_cw, recv_ccw, send_cw, send_ccw,
                           fin, y_recv, a_sems, cw_sems, ccw_sems, y_sems):
     c = lax.axis_index("col")
     row = lax.axis_index("row")
@@ -41,42 +41,67 @@
         pl.semaphore_signal(barrier, inc=1, device_id=peer, device_id_type=MESH)
     pl.semaphore_wait(barrier, 4)
 
-    def rcopy(src, dst, sems, k, peer):
+    def rcopy(src, dst, sems, idx, peer):
         return pltpu.make_async_remote_copy(
-            src_ref=src, dst_ref=dst, send_sem=sems.at[0, k], recv_sem=sems.at[1, k],
+            src_ref=src, dst_ref=dst, send_sem=sems.at[(0,) + idx], recv_sem=sems.at[(1,) + idx],
             device_id=peer, device_id_type=MESH,
         )
 
-    copy_a = rcopy(x_ref.at[1 - core], ra, a_sems, 0, partner)
-    copy_a.start()
-    copy_a.wait_recv()
-    sa[...] = x_ref[core] + ra[...]
-
-    sends = [copy_a]
+    def first(d):
+        return lax.rem(z + (n_z - 1 if d == 0 else 1), n_z)
+
+    def got(d, s):
+        return lax.rem(z + ((2 * n_z - s - 2) if d == 0 else (s + 2)), n_z)
+
+    need = [(first(0), 0), (first(1), 1)]
     for s in range(n_z - 1):
-        g_cw = lax.rem(z + (n_z - s - 1), n_z)
-        g_ccw = lax.rem(z + s + 1, n_z)
-        src_cw = sa.at[g_cw, 0] if s == 0 else cw_send.at[s - 1]
-        src_ccw = sa.at[g_ccw, 1] if s == 0 else ccw_send.at[s - 1]
-        copy_cw = rcopy(src_cw, cw_recv.at[s], cw_sems, s, right)
-        copy_ccw = rcopy(src_ccw, ccw_recv.at[s], ccw_sems, s, left)
-        copy_cw.start()
-        copy_ccw.start()
-        sends += [copy_cw, copy_ccw]
-        got_cw = lax.rem(z + (2 * n_z - s - 2), n_z)
-        got_ccw = lax.rem(z + s + 2, n_z)
-        copy_cw.wait_recv()
-        if s < n_z - 2:
-            cw_send[s] = cw_recv[s] + sa[got_cw, 0]
-        else:
-            fin[0] = cw_recv[s] + sa[got_cw, 0]
-        copy_ccw.wait_recv()
-        if s < n_z - 2:
-            ccw_send[s] = ccw_recv[s] + sa[got_ccw, 1]
-        else:
-            fin[1] = ccw_recv[s] + sa[got_ccw, 1]
-
-    copy_y = rcopy(fin.at[1 - yh], y_recv, y_sems, 0, y_partner)
+        need += [(got(0, s), 0), (got(1, s), 1)]
+    copies_a = []
+    for k, (g, h) in enumerate(need):
+        cp = rcopy(x_ref.at[1 - core, g, h], ra.at[g, h], a_sems, (k,), partner)
+        cp.start()
+        copies_a.append(cp)
+
+    def ready(d, s):
+        copies_a[d if s < 0 else 2 + 2 * s + d].wait_recv()
+
+    size = x_ref.shape[3] // chunks
+    recv = (recv_cw, recv_ccw)
+    send = (send_cw, send_ccw)
+    sems = (cw_sems, ccw_sems)
+    to = (right, left)
+    sends = list(copies_a)
+
+    def ring_copy(d, s, i):
+        part = pl.ds(i * size, size)
+        return rcopy(send[d].at[s, part], recv[d].at[s, part], sems[d], (s, i), to[d])
+
+    for d in range(2):
+        ready(d, -1)
+        g = first(d)
+        send[d][0] = x_ref[core, g, d] + ra[g, d]
+        for i in range(chunks):
+            cp = ring_copy(d, 0, i)
+            cp.start()
+            sends.append(cp)
+    for s in range(n_z - 1):
+        for d in range(2):
+            ready(d, s)
+        for i in range(chunks):
+            part = pl.ds(i * size, size)
+            for d in range(2):
+                g = got(d, s)
+                ring_copy(d, s, i).wait_recv()
+                val = recv[d][s, part] + x_ref[core, g, d, part] + ra[g, d, part]
+                if s < n_z - 2:
+                    send[d][s + 1, part] = val
+                    cp = ring_copy(d, s + 1, i)
+                    cp.start()
+                    sends.append(cp)
+                else:
+                    fin[d, part] = val
+
+    copy_y = rcopy(fin.at[1 - yh], y_recv, y_sems, (0,), y_partner)
     copy_y.start()
     sends.append(copy_y)
     copy_y.wait_recv()
@@ -87,25 +112,25 @@
 
 def col_reduce_scatter(pieces):
     cores, n_z, n_y, nodes_dev, feat_width = pieces.shape
+    chunks = 4
     piece = (nodes_dev, feat_width)
     vmem = pl.BlockSpec(memory_space=pltpu.VMEM)
     return pl.pallas_call(
-        functools.partial(reduce_scatter_kernel, n_z),
+        functools.partial(reduce_scatter_kernel, n_z, chunks),
         out_shape=jax.ShapeDtypeStruct(piece, jnp.float32),
         in_specs=[vmem],
         out_specs=vmem,
         scratch_shapes=[
             pltpu.VMEM((n_z, n_y) + piece, jnp.float32),
-            pltpu.VMEM((n_z, n_y) + piece, jnp.float32),
             pltpu.VMEM((n_z - 1,) + piece, jnp.float32),
             pltpu.VMEM((n_z - 1,) + piece, jnp.float32),
             pltpu.VMEM((n_z - 1,) + piece, jnp.float32),
             pltpu.VMEM((n_z - 1,) + piece, jnp.float32),
             pltpu.VMEM((n_y,) + piece, jnp.float32),
             pltpu.VMEM(piece, jnp.float32),
-            pltpu.SemaphoreType.DMA((2, 1)),
-            pltpu.SemaphoreType.DMA((2, n_z - 1)),
-            pltpu.SemaphoreType.DMA((2, n_z - 1)),
+            pltpu.SemaphoreType.DMA((2, 2 * n_z)),
+            pltpu.SemaphoreType.DMA((2, n_z - 1, chunks)),
+            pltpu.SemaphoreType.DMA((2, n_z - 1, chunks)),
             pltpu.SemaphoreType.DMA((2, 1)),
         ],
         compiler_params=pltpu.CompilerParams(collective_id=0, has_side_effects=True),

time: 173 us -> 149 us (0.86)
  Pallas kernels: 156 us -> 132 us
    pallas_call x2, Pallas kernels: 102 us -> 78 us  [col_reduce_scatter(): pl.pallas_call(functools.partial(reduce_scatter_kernel, n_z, chunks), out...]
where the time goes in v6:
time: 149 us
  Pallas kernels  132 us (89%)
  local copies, waits for them, and re-layouts  9.97 us (7%)
  other arithmetic  5.58 us (4%)
    pallas_call x2, Pallas kernels, col_reduce_scatter(): pl.pallas_call(functools.partial(reduce_scatter_kernel, n_z, chunks), out...  78 us
    pallas_call x2, Pallas kernels, block_product(): pl.pallas_call(functools.partial(block_product_kernel, group), out_shape=...  30.1 us
    pallas_call x2, Pallas kernels, row_all_gather(): pl.pallas_call(functools.partial(all_gather_kernel, n), out_shape=jax.Sha...  24.1 us
    reshape x1, local copies, waits for them, and re-layouts, shards(): dev_tiles = adj_tiles.reshape(tile_slots, TILE, TILE)  6.69 us
    unnamed x3, local copies, waits for them, and re-layouts  3.28 us
    convert_element_type x2, other arithmetic, shards(): source = (norm_scale * current).astype(jnp.bfloat16)  3.25 us

profile of v6, /device:TPU:8, one launch (start us, length us, event | category | flops | bytes accessed | tf_op | source)
XLA Modules:
  0.0 148.5 jit_solution(3344101993155210619)
XLA Ops:
  0.7 0.7 broadcast_multiply_fusion
  1.3 1.6 %fusion.5.src_ref = bf16[256,128]{1,0:T(8,128)(2,1)} fusion(bf16[256,128]{1,0:T(8,128)(2,1)} %param.6, f32[256]{0:T(256)S(1)} %get-tuple-element.6), kind=kLoop, calls=%fused_computation.7 | loop fusion | flops 98304 | bytes 132096 | tf_op jit(solution)/shard_map/convert_element_type | solution.py:257
  2.9 13.4 %shard_map.64 = bf16[8,256,128]{2,1,0:T(8,128)(2,1)} custom-call(bf16[256,128]{1,0:T(8,128)(2,1)} %fusion.5.src_ref), custom_call_target="tpu_custom_call" | custom-call | tf_op jit(solution)/shard_map/pallas_call | solution.py:184
  16.3 3.3 %copy.7 = bf16[1,1,256,4096]{2,3,1,0:T(8,128)(2,1)S(1)} copy(bf16[1,1,256,4096]{3,2,1,0:T(8,128)(2,1)} %param.8) | data formatting | bytes 4194304 | tf_op args[2]
  19.6 6.7 %copy.9.adj_ref = bf16[256,64,64]{2,1,0:T(8,128)(2,1)} copy(bf16[256,64,64]{0,2,1:T(8,128)(2,1)S(1)} %bitcast.12) | data formatting | bytes 4194304 | tf_op jit(solution)/shard_map/reshape | solution.py:248
  26.3 15.1 %shard_map.65 = f32[2,8,2,4,64,128]{5,4,3,2,1,0:T(8,128)} custom-call(s32[256]{0:T(256)} %bitcast.15, s32[256]{0:T(256)} %bitcast.17, s32[1]{0:T(128)} %bitcast.8.count_ref, bf16[256,64,64]{2,1,0:T(8,128)(2,1)} %copy.9.adj_ref, bf16[32,64,128]{2,1,0:T(8,128)(2,1)} %bitcast.13), custom_call_target="tpu_custom_call" | custom-call | flops 268435456 | bytes 6291456 | tf_op jit(solution)/shard_map/pallas_call | solution.py:226
  41.3 0.0 copy-start
  41.3 40.9 %shard_map.66 = f32[256,128]{1,0:T(8,128)} custom-call(f32[2,8,2,256,128]{4,3,2,1,0:T(8,128)} %bitcast.11), custom_call_target="tpu_custom_call" | custom-call | tf_op jit(solution)/shard_map/pallas_call | solution.py:118
  82.2 0.0 copy-done
  82.3 1.7 %fusion.3.src_ref = bf16[256,128]{1,0:T(8,128)(2,1)} fusion(bf16[256,128]{1,0:T(8,128)(2,1)S(1)} %copy-done, f32[256,128]{1,0:T(8,128)} %shard_map.66, f32[256]{0:T(256)S(1)} %get-tuple-element.6, f32[256]{0:T(256)S(1)} %get-tuple-element.5), kind=kLoop, calls=%fused_computation.5 | loop fusion | flops 196608 | bytes 264192 | tf_op jit(solution)/shard_map/convert_element_type | solution.py:257
  83.9 10.8 %shard_map.67 = bf16[8,256,128]{2,1,0:T(8,128)(2,1)} custom-call(bf16[256,128]{1,0:T(8,128)(2,1)} %fusion.3.src_ref), custom_call_target="tpu_custom_call" | custom-call | tf_op jit(solution)/shard_map/pallas_call | solution.py:184
  94.7 15.1 %shard_map.68 = f32[2,8,2,4,64,128]{5,4,3,2,1,0:T(8,128)} custom-call(s32[256]{0:T(256)} %bitcast.16, s32[256]{0:T(256)} %bitcast.18, s32[1]{0:T(128)} %bitcast.9.count_ref, bf16[256,64,64]{2,1,0:T(8,128)(2,1)} %copy.9.adj_ref, bf16[32,64,128]{2,1,0:T(8,128)(2,1)} %bitcast.14), custom_call_target="tpu_custom_call" | custom-call | flops 268435456 | bytes 6291456 | tf_op jit(solution)/shard_map/pallas_call | solution.py:226
  109.7 37.1 %shard_map.69 = f32[256,128]{1,0:T(8,128)} custom-call(f32[2,8,2,256,128]{4,3,2,1,0:T(8,128)} %bitcast.10), custom_call_target="tpu_custom_call" | custom-call | tf_op jit(solution)/shard_map/pallas_call | solution.py:118
  146.9 1.6 %fusion.4 = bf16[256,128]{1,0:T(8,128)(2,1)} fusion(bf16[256,128]{1,0:T(8,128)(2,1)S(1)} %copy-done, f32[256,128]{1,0:T(8,128)} %shard_map.69, f32[256]{0:T(256)S(1)} %get-tuple-element.5), kind=kLoop, calls=%fused_computation.6 | loop fusion | flops 163840 | bytes 263168 | tf_op jit(solution)/shard_map/convert_element_type | solution.py:264
Async XLA Ops:
  41.3 40.9 %copy-start = (bf16[256,128]{1,0:T(8,128)(2,1)S(1)}, bf16[256,128]{1,0:T(8,128)(2,1)}, u32[]{:S(2)}) copy-start(bf16[256,128]{1,0:T(8,128)(2,1)} %param.6) | copy-start | bytes 196612

commit v7 on v6

--- a/solution.py
+++ b/solution.py
@@ -75,6 +75,10 @@
     def ring_copy(d, s, i):
         part = pl.ds(i * size, size)
         return rcopy(send[d].at[s, part], recv[d].at[s, part], sems[d], (s, i), to[d])
+
+    def y_copy(i):
+        part = pl.ds(i * size, size)
+        return rcopy(fin.at[1 - yh, part], y_recv.at[part], y_sems, (i,), y_partner)
 
     for d in range(2):
         ready(d, -1)
@@ -100,19 +104,25 @@
                     sends.append(cp)
                 else:
                     fin[d, part] = val
-
-    copy_y = rcopy(fin.at[1 - yh], y_recv, y_sems, (0,), y_partner)
-    copy_y.start()
-    sends.append(copy_y)
-    copy_y.wait_recv()
-    out_ref[...] = fin[yh] + y_recv[...]
+            if s == n_z - 2:
+                cp = y_copy(i)
+                cp.start()
+                sends.append(cp)
+
+    for i in range(chunks):
+        part = pl.ds(i * size, size)
+        y_copy(i).wait_recv()
+        out_ref[part] = fin[yh, part] + y_recv[part]
     for cp in sends:
         cp.wait_send()
 
 
+RS_CHUNKS = 4
+
+
 def col_reduce_scatter(pieces):
     cores, n_z, n_y, nodes_dev, feat_width = pieces.shape
-    chunks = 4
+    chunks = RS_CHUNKS
     piece = (nodes_dev, feat_width)
     vmem = pl.BlockSpec(memory_space=pltpu.VMEM)
     return pl.pallas_call(
@@ -131,7 +141,7 @@
             pltpu.SemaphoreType.DMA((2, 2 * n_z)),
             pltpu.SemaphoreType.DMA((2, n_z - 1, chunks)),
             pltpu.SemaphoreType.DMA((2, n_z - 1, chunks)),
-            pltpu.SemaphoreType.DMA((2, 1)),
+            pltpu.SemaphoreType.DMA((2, chunks)),
         ],
         compiler_params=pltpu.CompilerParams(collective_id=0, has_side_effects=True),
     )(pieces)

time: 149 us -> 147 us (0.987)
  Pallas kernels: 132 us -> 130 us
    pallas_call x2, Pallas kernels: 78 us -> 76 us  [col_reduce_scatter(): pl.pallas_call(functools.partial(reduce_scatter_kernel, n_z, chunks), out...]
where the time goes in v7:
time: 147 us
  Pallas kernels  130 us (88%)
  local copies, waits for them, and re-layouts  9.97 us (7%)
  other arithmetic  5.58 us (4%)
    pallas_call x2, Pallas kernels, col_reduce_scatter(): pl.pallas_call(functools.partial(reduce_scatter_kernel, n_z, chunks), out...  76 us
    pallas_call x2, Pallas kernels, block_product(): pl.pallas_call(functools.partial(block_product_kernel, group), out_shape=...  30.1 us
    pallas_call x2, Pallas kernels, row_all_gather(): pl.pallas_call(functools.partial(all_gather_kernel, n), out_shape=jax.Sha...  24.1 us
    reshape x1, local copies, waits for them, and re-layouts, shards(): dev_tiles = adj_tiles.reshape(tile_slots, TILE, TILE)  6.69 us
    unnamed x3, local copies, waits for them, and re-layouts  3.28 us
    convert_element_type x2, other arithmetic, shards(): source = (norm_scale * current).astype(jnp.bfloat16)  3.25 us

profile of v7, /device:TPU:8, one launch (start us, length us, event | category | flops | bytes accessed | tf_op | source)
XLA Modules:
  0.0 146.5 jit_solution(7158994260083872203)
XLA Ops:
  0.7 0.7 broadcast_multiply_fusion
  1.3 1.6 %fusion.5.src_ref = bf16[256,128]{1,0:T(8,128)(2,1)} fusion(bf16[256,128]{1,0:T(8,128)(2,1)} %param.6, f32[256]{0:T(256)S(1)} %get-tuple-element.6), kind=kLoop, calls=%fused_computation.7 | loop fusion | flops 98304 | bytes 132096 | tf_op jit(solution)/shard_map/convert_element_type | solution.py:267
  2.9 13.4 %shard_map.64 = bf16[8,256,128]{2,1,0:T(8,128)(2,1)} custom-call(bf16[256,128]{1,0:T(8,128)(2,1)} %fusion.5.src_ref), custom_call_target="tpu_custom_call" | custom-call | tf_op jit(solution)/shard_map/pallas_call | solution.py:194
  16.3 3.3 %copy.7 = bf16[1,1,256,4096]{2,3,1,0:T(8,128)(2,1)S(1)} copy(bf16[1,1,256,4096]{3,2,1,0:T(8,128)(2,1)} %param.8) | data formatting | bytes 4194304 | tf_op args[2]
  19.6 6.7 %copy.9.adj_ref = bf16[256,64,64]{2,1,0:T(8,128)(2,1)} copy(bf16[256,64,64]{0,2,1:T(8,128)(2,1)S(1)} %bitcast.12) | data formatting | bytes 4194304 | tf_op jit(solution)/shard_map/reshape | solution.py:258
  26.3 15.1 %shard_map.65 = f32[2,8,2,4,64,128]{5,4,3,2,1,0:T(8,128)} custom-call(s32[256]{0:T(256)} %bitcast.15, s32[256]{0:T(256)} %bitcast.17, s32[1]{0:T(128)} %bitcast.8.count_ref, bf16[256,64,64]{2,1,0:T(8,128)(2,1)} %copy.9.adj_ref, bf16[32,64,128]{2,1,0:T(8,128)(2,1)} %bitcast.13), custom_call_target="tpu_custom_call" | custom-call | flops 268435456 | bytes 6291456 | tf_op jit(solution)/shard_map/pallas_call | solution.py:236
  41.3 0.0 copy-start
  41.3 39.9 %shard_map.66 = f32[256,128]{1,0:T(8,128)} custom-call(f32[2,8,2,256,128]{4,3,2,1,0:T(8,128)} %bitcast.11), custom_call_target="tpu_custom_call" | custom-call | tf_op jit(solution)/shard_map/pallas_call | solution.py:128
  81.2 0.0 copy-done
  81.3 1.7 %fusion.3.src_ref = bf16[256,128]{1,0:T(8,128)(2,1)} fusion(bf16[256,128]{1,0:T(8,128)(2,1)S(1)} %copy-done, f32[256,128]{1,0:T(8,128)} %shard_map.66, f32[256]{0:T(256)S(1)} %get-tuple-element.6, f32[256]{0:T(256)S(1)} %get-tuple-element.5), kind=kLoop, calls=%fused_computation.5 | loop fusion | flops 196608 | bytes 264192 | tf_op jit(solution)/shard_map/convert_element_type | solution.py:267
  82.9 10.8 %shard_map.67 = bf16[8,256,128]{2,1,0:T(8,128)(2,1)} custom-call(bf16[256,128]{1,0:T(8,128)(2,1)} %fusion.3.src_ref), custom_call_target="tpu_custom_call" | custom-call | tf_op jit(solution)/shard_map/pallas_call | solution.py:194
  93.7 15.1 %shard_map.68 = f32[2,8,2,4,64,128]{5,4,3,2,1,0:T(8,128)} custom-call(s32[256]{0:T(256)} %bitcast.16, s32[256]{0:T(256)} %bitcast.18, s32[1]{0:T(128)} %bitcast.9.count_ref, bf16[256,64,64]{2,1,0:T(8,128)(2,1)} %copy.9.adj_ref, bf16[32,64,128]{2,1,0:T(8,128)(2,1)} %bitcast.14), custom_call_target="tpu_custom_call" | custom-call | flops 268435456 | bytes 6291456 | tf_op jit(solution)/shard_map/pallas_call | solution.py:236
  108.7 36.1 %shard_map.69 = f32[256,128]{1,0:T(8,128)} custom-call(f32[2,8,2,256,128]{4,3,2,1,0:T(8,128)} %bitcast.10), custom_call_target="tpu_custom_call" | custom-call | tf_op jit(solution)/shard_map/pallas_call | solution.py:128
  144.9 1.6 %fusion.4 = bf16[256,128]{1,0:T(8,128)(2,1)} fusion(bf16[256,128]{1,0:T(8,128)(2,1)S(1)} %copy-done, f32[256,128]{1,0:T(8,128)} %shard_map.69, f32[256]{0:T(256)S(1)} %get-tuple-element.5), kind=kLoop, calls=%fused_computation.6 | loop fusion | flops 163840 | bytes 263168 | tf_op jit(solution)/shard_map/convert_element_type | solution.py:274
Async XLA Ops:
  41.3 39.9 %copy-start = (bf16[256,128]{1,0:T(8,128)(2,1)S(1)}, bf16[256,128]{1,0:T(8,128)(2,1)}, u32[]{:S(2)}) copy-start(bf16[256,128]{1,0:T(8,128)(2,1)} %param.6) | copy-start | bytes 196612

commit v8 on v7

--- a/solution.py
+++ b/solution.py
@@ -202,8 +202,9 @@
 
 
 def block_product_kernel(group, rows_ref, cols_ref, count_ref, adj_ref, panel_ref,
-                         pieces_ref, acc_ref):
-    acc_ref[...] = jnp.zeros_like(acc_ref)
+                         pieces_ref):
+    cores, n_z, n_y, per_piece = pieces_ref.shape[:4]
+    pieces_ref[...] = jnp.zeros_like(pieces_ref)
     count = count_ref[0]
     slots = adj_ref.shape[0]
 
@@ -216,14 +217,12 @@
             prods.append(jnp.where(t < count, p, jnp.zeros_like(p)))
         for i in range(group):
             r = rows_ref[base + i]
-            acc_ref[r] += prods[i]
+            j = r // per_piece
+            at = (lax.rem(j, cores), lax.rem(j // cores, n_z), j // (cores * n_z), lax.rem(r, per_piece))
+            pieces_ref[at] += prods[i]
         return carry
 
     lax.fori_loop(0, slots // group, body, 0)
-    cores, n_z, n_y, per_piece = pieces_ref.shape[:4]
-    for j in range(cores * n_z * n_y):
-        core_j, z_j, yh_j = j % cores, (j // cores) % n_z, j // (cores * n_z)
-        pieces_ref[core_j, z_j, yh_j] = acc_ref[j * per_piece:(j + 1) * per_piece]
 
 
 def block_product(row_ids, col_ids, count, dev_tiles, col_panel, row_tiles, nodes_dev):
@@ -241,7 +240,6 @@
         ),
         in_specs=[smem, smem, smem, vmem, vmem],
         out_specs=vmem,
-        scratch_shapes=[pltpu.VMEM((row_tiles, TILE, feat_width), jnp.float32)],
         cost_estimate=pl.CostEstimate(
             flops=2 * slots * TILE * TILE * feat_width,
             bytes_accessed=slots * TILE * TILE * 2 + row_tiles * TILE * feat_width * 4,

time: 147 us -> 146 us (level)
  no operation moved by 1% of the time
where the time goes in v8:
time: 146 us
  Pallas kernels  130 us (89%)
  local copies, waits for them, and re-layouts  9.97 us (7%)
  other arithmetic  5.58 us (4%)
    pallas_call x2, Pallas kernels, col_reduce_scatter(): pl.pallas_call(functools.partial(reduce_scatter_kernel, n_z, chunks), out...  76 us
    pallas_call x2, Pallas kernels, block_product(): pl.pallas_call(functools.partial(block_product_kernel, group), out_shape=...  29.6 us
    pallas_call x2, Pallas kernels, row_all_gather(): pl.pallas_call(functools.partial(all_gather_kernel, n), out_shape=jax.Sha...  24.1 us
    reshape x1, local copies, waits for them, and re-layouts, shards(): dev_tiles = adj_tiles.reshape(tile_slots, TILE, TILE)  6.69 us
    unnamed x3, local copies, waits for them, and re-layouts  3.28 us
    convert_element_type x2, other arithmetic, shards(): source = (norm_scale * current).astype(jnp.bfloat16)  3.25 us

profile of v8, /device:TPU:8, one launch (start us, length us, event | category | flops | bytes accessed | tf_op | source)
XLA Modules:
  0.0 146.0 jit_solution(18398369028491936459)
XLA Ops:
  0.7 0.7 broadcast_multiply_fusion
  1.3 1.6 %fusion.5.src_ref = bf16[256,128]{1,0:T(8,128)(2,1)} fusion(bf16[256,128]{1,0:T(8,128)(2,1)} %param.6, f32[256]{0:T(256)S(1)} %get-tuple-element.6), kind=kLoop, calls=%fused_computation.7 | loop fusion | flops 98304 | bytes 132096 | tf_op jit(solution)/shard_map/convert_element_type | solution.py:265
  2.9 13.4 %shard_map.64 = bf16[8,256,128]{2,1,0:T(8,128)(2,1)} custom-call(bf16[256,128]{1,0:T(8,128)(2,1)} %fusion.5.src_ref), custom_call_target="tpu_custom_call" | custom-call | tf_op jit(solution)/shard_map/pallas_call | solution.py:194
  16.3 3.3 %copy.7 = bf16[1,1,256,4096]{2,3,1,0:T(8,128)(2,1)S(1)} copy(bf16[1,1,256,4096]{3,2,1,0:T(8,128)(2,1)} %param.8) | data formatting | bytes 4194304 | tf_op args[2]
  19.6 6.7 %copy.9.adj_ref = bf16[256,64,64]{2,1,0:T(8,128)(2,1)} copy(bf16[256,64,64]{0,2,1:T(8,128)(2,1)S(1)} %bitcast.12) | data formatting | bytes 4194304 | tf_op jit(solution)/shard_map/reshape | solution.py:256
  26.3 14.8 %shard_map.65 = f32[2,8,2,4,64,128]{5,4,3,2,1,0:T(8,128)} custom-call(s32[256]{0:T(256)} %bitcast.15, s32[256]{0:T(256)} %bitcast.17, s32[1]{0:T(128)} %bitcast.8.count_ref, bf16[256,64,64]{2,1,0:T(8,128)(2,1)} %copy.9.adj_ref, bf16[32,64,128]{2,1,0:T(8,128)(2,1)} %bitcast.13), custom_call_target="tpu_custom_call" | custom-call | flops 268435456 | bytes 6291456 | tf_op jit(solution)/shard_map/pallas_call | solution.py:235
  41.1 0.0 copy-start
  41.1 39.9 %shard_map.66 = f32[256,128]{1,0:T(8,128)} custom-call(f32[2,8,2,256,128]{4,3,2,1,0:T(8,128)} %bitcast.11), custom_call_target="tpu_custom_call" | custom-call | tf_op jit(solution)/shard_map/pallas_call | solution.py:128
  81.0 0.0 copy-done
  81.0 1.7 %fusion.3.src_ref = bf16[256,128]{1,0:T(8,128)(2,1)} fusion(bf16[256,128]{1,0:T(8,128)(2,1)S(1)} %copy-done, f32[256,128]{1,0:T(8,128)} %shard_map.66, f32[256]{0:T(256)S(1)} %get-tuple-element.6, f32[256]{0:T(256)S(1)} %get-tuple-element.5), kind=kLoop, calls=%fused_computation.5 | loop fusion | flops 196608 | bytes 264192 | tf_op jit(solution)/shard_map/convert_element_type | solution.py:265
  82.7 10.8 %shard_map.67 = bf16[8,256,128]{2,1,0:T(8,128)(2,1)} custom-call(bf16[256,128]{1,0:T(8,128)(2,1)} %fusion.3.src_ref), custom_call_target="tpu_custom_call" | custom-call | tf_op jit(solution)/shard_map/pallas_call | solution.py:194
  93.4 14.8 %shard_map.68 = f32[2,8,2,4,64,128]{5,4,3,2,1,0:T(8,128)} custom-call(s32[256]{0:T(256)} %bitcast.16, s32[256]{0:T(256)} %bitcast.18, s32[1]{0:T(128)} %bitcast.9.count_ref, bf16[256,64,64]{2,1,0:T(8,128)(2,1)} %copy.9.adj_ref, bf16[32,64,128]{2,1,0:T(8,128)(2,1)} %bitcast.14), custom_call_target="tpu_custom_call" | custom-call | flops 268435456 | bytes 6291456 | tf_op jit(solution)/shard_map/pallas_call | solution.py:235
  108.2 36.1 %shard_map.69 = f32[256,128]{1,0:T(8,128)} custom-call(f32[2,8,2,256,128]{4,3,2,1,0:T(8,128)} %bitcast.10), custom_call_target="tpu_custom_call" | custom-call | tf_op jit(solution)/shard_map/pallas_call | solution.py:128
  144.3 1.6 %fusion.4 = bf16[256,128]{1,0:T(8,128)(2,1)} fusion(bf16[256,128]{1,0:T(8,128)(2,1)S(1)} %copy-done, f32[256,128]{1,0:T(8,128)} %shard_map.69, f32[256]{0:T(256)S(1)} %get-tuple-element.5), kind=kLoop, calls=%fused_computation.6 | loop fusion | flops 163840 | bytes 263168 | tf_op jit(solution)/shard_map/convert_element_type | solution.py:272
Async XLA Ops:
  41.1 39.9 %copy-start = (bf16[256,128]{1,0:T(8,128)(2,1)S(1)}, bf16[256,128]{1,0:T(8,128)(2,1)}, u32[]{:S(2)}) copy-start(bf16[256,128]{1,0:T(8,128)(2,1)} %param.6) | copy-start | bytes 196612

commit v9 on v8

--- a/solution.py
+++ b/solution.py
@@ -20,8 +20,9 @@
 Z_RING = 8
 
 
-def reduce_scatter_kernel(n_z, chunks, x_ref, out_ref, ra, recv_cw, recv_ccw, send_cw, send_ccw,
-                          fin, y_recv, a_sems, cw_sems, ccw_sems, y_sems):
+def reduce_scatter_kernel(n_z, chunks, last, x_ref, s9_ref, scale_ref, tele_ref, out_ref, ra,
+                          recv_cw, recv_ccw, send_cw, send_ccw, fin, y_recv,
+                          a_sems, cw_sems, ccw_sems, y_sems, *ag_sems):
     c = lax.axis_index("col")
     row = lax.axis_index("row")
     core = lax.rem(c, CORES)
@@ -36,10 +37,18 @@
     left = dev(yh, lax.rem(z + n_z - 1, n_z), core)
     y_partner = dev(1 - yh, z, core)
 
+    n_row = lax.axis_size("row")
     barrier = pltpu.get_barrier_semaphore()
     for peer in (partner, right, left, y_partner):
         pl.semaphore_signal(barrier, inc=1, device_id=peer, device_id_type=MESH)
-    pl.semaphore_wait(barrier, 4)
+    if not last:
+        def greet(k, carry):
+            pl.semaphore_signal(barrier, inc=1, device_id=(lax.rem(row + k, n_row), c),
+                                device_id_type=MESH)
+            return carry
+
+        lax.fori_loop(1, n_row, greet, 0)
+    pl.semaphore_wait(barrier, 4 if last else 3 + n_row)
 
     def rcopy(src, dst, sems, idx, peer):
         return pltpu.make_async_remote_copy(
@@ -112,7 +121,34 @@
     for i in range(chunks):
         part = pl.ds(i * size, size)
         y_copy(i).wait_recv()
-        out_ref[part] = fin[yh, part] + y_recv[part]
+        own = fin[yh, part] + y_recv[part]
+        current = s9_ref[part] * own + tele_ref[part]
+        if last:
+            out_ref[part] = current.astype(out_ref.dtype)
+        else:
+            out_ref[row, part] = (scale_ref[part] * current).astype(out_ref.dtype)
+    if not last:
+        ag_send, ag_recv = ag_sems
+
+        def ag_copy(peer, slot):
+            return pltpu.make_async_remote_copy(
+                src_ref=out_ref.at[row], dst_ref=out_ref.at[slot], send_sem=ag_send.at[peer],
+                recv_sem=ag_recv.at[slot], device_id=(peer, c), device_id_type=MESH,
+            )
+
+        def ag_start(k, carry):
+            ag_copy(lax.rem(row + k, n_row), row).start()
+            return carry
+
+        lax.fori_loop(1, n_row, ag_start, 0)
+
+        def ag_finish(k, carry):
+            sender = lax.rem(row + n_row - k, n_row)
+            ag_copy(sender, sender).wait_recv()
+            ag_copy(lax.rem(row + k, n_row), row).wait_send()
+            return carry
+
+        lax.fori_loop(1, n_row, ag_finish, 0)
     for cp in sends:
         cp.wait_send()
 
@@ -120,15 +156,18 @@
 RS_CHUNKS = 4
 
 
-def col_reduce_scatter(pieces):
+def col_reduce_scatter(pieces, s9, scale, tele, last):
     cores, n_z, n_y, nodes_dev, feat_width = pieces.shape
+    n_row = lax.axis_size("row")
     chunks = RS_CHUNKS
     piece = (nodes_dev, feat_width)
     vmem = pl.BlockSpec(memory_space=pltpu.VMEM)
+    out_shape = piece if last else (n_row,) + piece
+    ag_sems = [] if last else [pltpu.SemaphoreType.DMA((n_row,))] * 2
     return pl.pallas_call(
-        functools.partial(reduce_scatter_kernel, n_z, chunks),
-        out_shape=jax.ShapeDtypeStruct(piece, jnp.float32),
-        in_specs=[vmem],
+        functools.partial(reduce_scatter_kernel, n_z, chunks, last),
+        out_shape=jax.ShapeDtypeStruct(out_shape, jnp.bfloat16),
+        in_specs=[vmem] * 4,
         out_specs=vmem,
         scratch_shapes=[
             pltpu.VMEM((n_z, n_y) + piece, jnp.float32),
@@ -142,9 +181,9 @@
             pltpu.SemaphoreType.DMA((2, n_z - 1, chunks)),
             pltpu.SemaphoreType.DMA((2, n_z - 1, chunks)),
             pltpu.SemaphoreType.DMA((2, chunks)),
-        ],
-        compiler_params=pltpu.CompilerParams(collective_id=0, has_side_effects=True),
-    )(pieces)
+        ] + ag_sems,
+        compiler_params=pltpu.CompilerParams(collective_id=2 if last else 0, has_side_effects=True),
+    )(pieces, s9, scale, tele)
 
 
 def all_gather_kernel(n, src_ref, out_ref, send_sem, recv_sem):
@@ -260,16 +299,20 @@
     row_tiles = nodes_dev * col_count // TILE
     norm_scale = jnp.sqrt(KNN / degrees.astype(jnp.float32))[:, None]
     teleport = ALPHA * features.astype(jnp.float32)
-    current = features.astype(jnp.float32)
+    scale9 = jnp.broadcast_to((1.0 - ALPHA) * norm_scale, features.shape)
+    scale = jnp.broadcast_to(norm_scale, features.shape)
+    source = (norm_scale * features.astype(jnp.float32)).astype(jnp.bfloat16)
+    gathered = row_all_gather(source)
     for repeat in range(STEPS):
-        source = (norm_scale * current).astype(jnp.bfloat16)
-        col_panel = row_all_gather(source).reshape(-1, TILE, feat_width)
+        col_panel = gathered.reshape(-1, TILE, feat_width)
         pieces = block_product(
             row_ids_all, col_ids_all, live_count, dev_tiles, col_panel, row_tiles, nodes_dev
         )
-        own_rows = col_reduce_scatter(pieces.reshape(pieces.shape[:3] + (nodes_dev, feat_width)))
-        current = (1.0 - ALPHA) * norm_scale * own_rows + teleport
-    return current.astype(jnp.bfloat16)
+        gathered = col_reduce_scatter(
+            pieces.reshape(pieces.shape[:3] + (nodes_dev, feat_width)),
+            scale9, scale, teleport, repeat == STEPS - 1,
+        )
+    return gathered
 
 
 def solution(mesh):

time: 146 us -> 145 us (level)
  other arithmetic: 5.58 us -> 2.26 us
  local copies, waits for them, and re-layouts: 9.97 us -> 12.9 us
    pallas_call x2 -> x1, Pallas kernels: 24.1 us -> 13.4 us  [row_all_gather(): pl.pallas_call(functools.partial(all_gather_kernel, n), out_shape=jax.Sha...]
    pallas_call x2, Pallas kernels: 76 us -> 85.8 us  [col_reduce_scatter(): pl.pallas_call(functools.partial(reduce_scatter_kernel, n_z, chunks, last...]
    convert_element_type x3 -> x0, other arithmetic: 4.89 us -> none  [the longest x2 3.25 us: shards(): source = (norm_scale * current).astype(jnp.bfloat16)]
    mul x1 -> x2, other arithmetic: 0.69 us -> 2.26 us  [the longest x1 1.57 us: shards(): teleport = ALPHA * features.astype(jnp.float32)]
    unnamed x3 -> x2, local copies, waits for them, and re-layouts: 3.28 us -> 4.75 us
where the time goes in v9:
time: 145 us
  Pallas kernels  129 us (89%)
  local copies, waits for them, and re-layouts  12.9 us (9%)
  other arithmetic  2.26 us (2%)
    pallas_call x2, Pallas kernels, col_reduce_scatter(): pl.pallas_call(functools.partial(reduce_scatter_kernel, n_z, chunks, last...  85.8 us
    pallas_call x2, Pallas kernels, block_product(): pl.pallas_call(functools.partial(block_product_kernel, group), out_shape=...  29.5 us
    pallas_call x1, Pallas kernels, row_all_gather(): pl.pallas_call(functools.partial(all_gather_kernel, n), out_shape=jax.Sha...  13.4 us
    reshape x1, local copies, waits for them, and re-layouts, shards(): dev_tiles = adj_tiles.reshape(tile_slots, TILE, TILE)  6.68 us
    unnamed x2, local copies, waits for them, and re-layouts  4.75 us

profile of v9, /device:TPU:8, one launch (start us, length us, event | category | flops | bytes accessed | tf_op | source)
XLA Modules:
  0.0 144.6 jit_solution(12211397895034197327)
XLA Ops:
  0.7 0.7 broadcast_multiply_fusion
  1.3 0.8 broadcast_in_dim.2.s9_ref
  2.1 0.8 mul.21.scale_ref
  2.9 1.6 %convert_multiply_fusion = (f32[256,128]{1,0:T(8,128)}, bf16[256,128]{1,0:T(8,128)(2,1)}) fusion(bf16[256,128]{1,0:T(8,128)(2,1)} %param.6, f32[256]{0:T(256)S(1)} %get-tuple-element.6), kind=kLoop, calls=%fused_computation | loop fusion | flops 131072 | bytes 263168 | tf_op jit(solution)/shard_map/mul | solution.py:301
  4.4 13.4 %shard_map.64 = bf16[8,256,128]{2,1,0:T(8,128)(2,1)} custom-call(bf16[256,128]{1,0:T(8,128)(2,1)} %get-tuple-element.8.src_ref), custom_call_target="tpu_custom_call" | custom-call | tf_op jit(solution)/shard_map/pallas_call | solution.py:233
  17.8 3.3 %copy.7 = bf16[1,1,256,4096]{2,3,1,0:T(8,128)(2,1)S(1)} copy(bf16[1,1,256,4096]{3,2,1,0:T(8,128)(2,1)} %param.8) | data formatting | bytes 4194304 | tf_op args[2]
  21.1 6.7 %copy.9.adj_ref = bf16[256,64,64]{2,1,0:T(8,128)(2,1)} copy(bf16[256,64,64]{0,2,1:T(8,128)(2,1)S(1)} %bitcast.12) | data formatting | bytes 4194304 | tf_op jit(solution)/shard_map/reshape | solution.py:295
  27.8 14.8 %shard_map.65 = f32[2,8,2,4,64,128]{5,4,3,2,1,0:T(8,128)} custom-call(s32[256]{0:T(256)} %bitcast.15, s32[256]{0:T(256)} %bitcast.17, s32[1]{0:T(128)} %bitcast.8.count_ref, bf16[256,64,64]{2,1,0:T(8,128)(2,1)} %copy.9.adj_ref, bf16[32,64,128]{2,1,0:T(8,128)(2,1)} %bitcast.14), custom_call_target="tpu_custom_call" | custom-call | flops 268435456 | bytes 6291456 | tf_op jit(solution)/shard_map/pallas_call | solution.py:274
  42.5 49.9 %shard_map.66 = bf16[8,256,128]{2,1,0:T(8,128)(2,1)} custom-call(f32[2,8,2,256,128]{4,3,2,1,0:T(8,128)} %bitcast.10, f32[256,128]{1,0:T(8,128)} %broadcast_in_dim.2.s9_ref, f32[256,128]{1,0:T(8,128)} %mul.21.scale_ref, f32[256,128]{1,0:T(8,128)} %get-tuple-element.7.tele_ref), custom_call_target="tpu_custom_call" | custom-call | tf_op jit(solution)/shard_map/pallas_call | solution.py:167
  92.5 14.8 %shard_map.67 = f32[2,8,2,4,64,128]{5,4,3,2,1,0:T(8,128)} custom-call(s32[256]{0:T(256)} %bitcast.16, s32[256]{0:T(256)} %bitcast.18, s32[1]{0:T(128)} %bitcast.9.count_ref, bf16[256,64,64]{2,1,0:T(8,128)(2,1)} %copy.9.adj_ref, bf16[32,64,128]{2,1,0:T(8,128)(2,1)} %bitcast.13), custom_call_target="tpu_custom_call" | custom-call | flops 268435456 | bytes 6291456 | tf_op jit(solution)/shard_map/pallas_call | solution.py:274
  107.2 35.9 %shard_map.68 = bf16[256,128]{1,0:T(8,128)(2,1)} custom-call(f32[2,8,2,256,128]{4,3,2,1,0:T(8,128)} %bitcast.11, f32[256,128]{1,0:T(8,128)} %broadcast_in_dim.2.s9_ref, f32[256,128]{1,0:T(8,128)} %mul.21.scale_ref, f32[256,128]{1,0:T(8,128)} %get-tuple-element.7.tele_ref), custom_call_target="tpu_custom_call" | custom-call | tf_op jit(solution)/shard_map/pallas_call | solution.py:167
  143.1 1.5 %copy.12 = bf16[256,128]{1,0:T(8,128)(2,1)} copy(bf16[256,128]{1,0:T(8,128)(2,1)} %shard_map.68) | data formatting | bytes 131072

commit v10 on v9

--- a/solution.py
+++ b/solution.py
@@ -268,7 +268,7 @@
     slots = dev_tiles.shape[0]
     feat_width = col_panel.shape[2]
     per_piece = nodes_dev // TILE
-    group = 4 if slots % 4 == 0 else 1
+    group = 16 if slots % 16 == 0 else 1
     smem = pl.BlockSpec(memory_space=pltpu.SMEM)
     vmem = pl.BlockSpec(memory_space=pltpu.VMEM)
     return pl.pallas_call(

time: 145 us -> 135 us (0.931)
  Pallas kernels: 129 us -> 119 us
    pallas_call x2, Pallas kernels: 29.5 us -> 19.4 us  [block_product(): pl.pallas_call(functools.partial(block_product_kernel, group), out_shape=...]
where the time goes in v10:
time: 135 us; the launch traced here: 134 us
  Pallas kernels  119 us (88%)
  local copies, waits for them, and re-layouts  12.9 us (10%)
  other arithmetic  2.26 us (2%)
    pallas_call x2, Pallas kernels, col_reduce_scatter(): pl.pallas_call(functools.partial(reduce_scatter_kernel, n_z, chunks, last...  85.8 us
    pallas_call x2, Pallas kernels, block_product(): pl.pallas_call(functools.partial(block_product_kernel, group), out_shape=...  19.4 us
    pallas_call x1, Pallas kernels, row_all_gather(): pl.pallas_call(functools.partial(all_gather_kernel, n), out_shape=jax.Sha...  13.4 us
    reshape x1, local copies, waits for them, and re-layouts, shards(): dev_tiles = adj_tiles.reshape(tile_slots, TILE, TILE)  6.68 us
    unnamed x2, local copies, waits for them, and re-layouts  4.75 us

profile of v10, /device:TPU:8, one launch (start us, length us, event | category | flops | bytes accessed | tf_op | source)
XLA Modules:
  0.0 134.5 jit_solution(9750700089569390495)
XLA Ops:
  0.7 0.7 broadcast_multiply_fusion
  1.3 0.8 broadcast_in_dim.2.s9_ref
  2.1 0.8 mul.21.scale_ref
  2.9 1.6 %convert_multiply_fusion = (f32[256,128]{1,0:T(8,128)}, bf16[256,128]{1,0:T(8,128)(2,1)}) fusion(bf16[256,128]{1,0:T(8,128)(2,1)} %param.6, f32[256]{0:T(256)S(1)} %get-tuple-element.6), kind=kLoop, calls=%fused_computation | loop fusion | flops 131072 | bytes 263168 | tf_op jit(solution)/shard_map/mul | solution.py:301
  4.4 13.4 %shard_map.64 = bf16[8,256,128]{2,1,0:T(8,128)(2,1)} custom-call(bf16[256,128]{1,0:T(8,128)(2,1)} %get-tuple-element.8.src_ref), custom_call_target="tpu_custom_call" | custom-call | tf_op jit(solution)/shard_map/pallas_call | solution.py:233
  17.8 3.3 %copy.7 = bf16[1,1,256,4096]{2,3,1,0:T(8,128)(2,1)S(1)} copy(bf16[1,1,256,4096]{3,2,1,0:T(8,128)(2,1)} %param.8) | data formatting | bytes 4194304 | tf_op args[2]
  21.1 6.7 %copy.9.adj_ref = bf16[256,64,64]{2,1,0:T(8,128)(2,1)} copy(bf16[256,64,64]{0,2,1:T(8,128)(2,1)S(1)} %bitcast.12) | data formatting | bytes 4194304 | tf_op jit(solution)/shard_map/reshape | solution.py:295
  27.8 9.7 %shard_map.65 = f32[2,8,2,4,64,128]{5,4,3,2,1,0:T(8,128)} custom-call(s32[256]{0:T(256)} %bitcast.15, s32[256]{0:T(256)} %bitcast.17, s32[1]{0:T(128)} %bitcast.8.count_ref, bf16[256,64,64]{2,1,0:T(8,128)(2,1)} %copy.9.adj_ref, bf16[32,64,128]{2,1,0:T(8,128)(2,1)} %bitcast.14), custom_call_target="tpu_custom_call" | custom-call | flops 268435456 | bytes 6291456 | tf_op jit(solution)/shard_map/pallas_call | solution.py:274
  37.5 49.9 %shard_map.66 = bf16[8,256,128]{2,1,0:T(8,128)(2,1)} custom-call(f32[2,8,2,256,128]{4,3,2,1,0:T(8,128)} %bitcast.10, f32[256,128]{1,0:T(8,128)} %broadcast_in_dim.2.s9_ref, f32[256,128]{1,0:T(8,128)} %mul.21.scale_ref, f32[256,128]{1,0:T(8,128)} %get-tuple-element.7.tele_ref), custom_call_target="tpu_custom_call" | custom-call | tf_op jit(solution)/shard_map/pallas_call | solution.py:167
  87.4 9.7 %shard_map.67 = f32[2,8,2,4,64,128]{5,4,3,2,1,0:T(8,128)} custom-call(s32[256]{0:T(256)} %bitcast.16, s32[256]{0:T(256)} %bitcast.18, s32[1]{0:T(128)} %bitcast.9.count_ref, bf16[256,64,64]{2,1,0:T(8,128)(2,1)} %copy.9.adj_ref, bf16[32,64,128]{2,1,0:T(8,128)(2,1)} %bitcast.13), custom_call_target="tpu_custom_call" | custom-call | flops 268435456 | bytes 6291456 | tf_op jit(solution)/shard_map/pallas_call | solution.py:274
  97.1 35.9 %shard_map.68 = bf16[256,128]{1,0:T(8,128)(2,1)} custom-call(f32[2,8,2,256,128]{4,3,2,1,0:T(8,128)} %bitcast.11, f32[256,128]{1,0:T(8,128)} %broadcast_in_dim.2.s9_ref, f32[256,128]{1,0:T(8,128)} %mul.21.scale_ref, f32[256,128]{1,0:T(8,128)} %get-tuple-element.7.tele_ref), custom_call_target="tpu_custom_call" | custom-call | tf_op jit(solution)/shard_map/pallas_call | solution.py:167
  133.0 1.5 %copy.12 = bf16[256,128]{1,0:T(8,128)(2,1)} copy(bf16[256,128]{1,0:T(8,128)(2,1)} %shard_map.68) | data formatting | bytes 131072

commit v11 on v10

--- a/solution.py
+++ b/solution.py
@@ -302,11 +302,20 @@
     scale9 = jnp.broadcast_to((1.0 - ALPHA) * norm_scale, features.shape)
     scale = jnp.broadcast_to(norm_scale, features.shape)
     source = (norm_scale * features.astype(jnp.float32)).astype(jnp.bfloat16)
-    gathered = row_all_gather(source)
+    n_row = lax.axis_size("row")
+    me_row = lax.axis_index("row")
+    gathered = jnp.stack([source] + [
+        lax.ppermute(source, "row", [(i, (i + k) % n_row) for i in range(n_row)])
+        for k in range(1, n_row)
+    ])
+    per_piece = nodes_dev // TILE
+    rotated_cols = lax.rem(me_row - col_ids_all // per_piece + n_row, n_row) * per_piece + lax.rem(
+        col_ids_all, per_piece)
     for repeat in range(STEPS):
         col_panel = gathered.reshape(-1, TILE, feat_width)
         pieces = block_product(
-            row_ids_all, col_ids_all, live_count, dev_tiles, col_panel, row_tiles, nodes_dev
+            row_ids_all, rotated_cols if repeat == 0 else col_ids_all, live_count, dev_tiles,
+            col_panel, row_tiles, nodes_dev,
         )
         gathered = col_reduce_scatter(
             pieces.reshape(pieces.shape[:3] + (nodes_dev, feat_width)),

time: 135 us -> 140 us (1.037)
  Pallas kernels: 119 us -> 105 us
  starting transfers between devices: 0 us -> 12.3 us
  waiting for transfers between devices: 0 us -> 2.82 us
  other arithmetic: 2.26 us -> 4.39 us
    pallas_call x1 -> x0, Pallas kernels: 13.4 us -> none  [row_all_gather(): pl.pallas_call(functools.partial(all_gather_kernel, n), out_shape=jax.Sha...]
    ppermute x0 -> x7, starting transfers between devices: none -> 12.3 us  [shards(): lax.ppermute(source, 'row', [(i, (i + k) % n_row) for i in range(n_row)])]
    ppermute x0 -> x7, waiting for transfers between devices: none -> 2.82 us  [shards(): lax.ppermute(source, 'row', [(i, (i + k) % n_row) for i in range(n_row)])]
    unnamed x2 -> x10, local copies, waits for them, and re-layouts: 4.75 us -> 5.66 us
  transfers between devices with their start and end apart: 0 -> 7, of which waited for: 0 -> 2; matrix products, arithmetic and copies ran while one was open for 0% -> 9% of each run, Pallas kernels for 0% -> 0%
where the time goes in v11:
time: 140 us; the launch traced here: 139 us
  Pallas kernels  105 us (75%)
  local copies, waits for them, and re-layouts  13.8 us (10%)
  starting transfers between devices  12.3 us (9%)
  other arithmetic  4.39 us (3%)
  waiting for transfers between devices  2.82 us (2%)
    pallas_call x2, Pallas kernels, col_reduce_scatter(): pl.pallas_call(functools.partial(reduce_scatter_kernel, n_z, chunks, last...  85.7 us
    pallas_call x2, Pallas kernels, block_product(): pl.pallas_call(functools.partial(block_product_kernel, group), out_shape=...  19.5 us
    ppermute x7, starting transfers between devices, shards(): lax.ppermute(source, 'row', [(i, (i + k) % n_row) for i in range(n_row)])  12.3 us
    reshape x1, local copies, waits for them, and re-layouts, shards(): dev_tiles = adj_tiles.reshape(tile_slots, TILE, TILE)  6.68 us
    unnamed x10, local copies, waits for them, and re-layouts  5.66 us
    ppermute x7, waiting for transfers between devices, shards(): lax.ppermute(source, 'row', [(i, (i + k) % n_row) for i in range(n_row)])  2.82 us
  transfers between devices with their start and end apart: 7, of which 2 were waited for; matrix products, arithmetic and copies ran while one was open for 9% of the time, Pallas kernels for 0%

profile of v11, /device:TPU:8, one launch (start us, length us, event | category | flops | bytes accessed | tf_op | source)
XLA Modules:
  0.0 139.3 jit_solution(1667380163610752422)
XLA Ops:
  0.0 0.7 broadcast_multiply_fusion
  0.7 0.9 bitcast_dynamic-update-slice_fusion.7
  1.6 1.5 %collective-permute-start = (bf16[256,128]{1,0:T(8,128)(2,1)S(1)}, bf16[256,128]{1,0:T(8,128)(2,1)S(1)}, u32[]{:S(2)}, u32[]{:S(2)}) collective-permute-start(bf16[256,128]{1,0:T(8,128)(2,1)S(1)} %get-tuple-element.8), channel_id=1, source_target_pairs={{0,32},{32,64},{64,96},{96,128},{128,160},{160,192},{192,224},{224... | collective-permute-start | bytes 196616 | tf_op jit(solution)/shard_map/ppermute | solution.py:308
  3.1 1.5 %collective-permute-start.1 = (bf16[256,128]{1,0:T(8,128)(2,1)S(1)}, bf16[256,128]{1,0:T(8,128)(2,1)S(1)}, u32[]{:S(2)}, u32[]{:S(2)}) collective-permute-start(bf16[256,128]{1,0:T(8,128)(2,1)S(1)} %get-tuple-element.8), channel_id=1, source_target_pairs={{0,64},{32,96},{64,128},{96,160},{128,192},{160,224},{192,0},{224,... | collective-permute-start | bytes 196616 | tf_op jit(solution)/shard_map/ppermute | solution.py:308
  4.6 2.8 %collective-permute-start.2 = (bf16[256,128]{1,0:T(8,128)(2,1)S(1)}, bf16[256,128]{1,0:T(8,128)(2,1)S(1)}, u32[]{:S(2)}, u32[]{:S(2)}) collective-permute-start(bf16[256,128]{1,0:T(8,128)(2,1)S(1)} %get-tuple-element.8), channel_id=1, source_target_pairs={{0,96},{32,128},{64,160},{96,192},{128,224},{160,0},{192,32},{224,... | collective-permute-start | bytes 196616 | tf_op jit(solution)/shard_map/ppermute | solution.py:308
  7.4 0.8 collective-permute-start.3
  8.2 3.4 %collective-permute-start.4 = (bf16[256,128]{1,0:T(8,128)(2,1)S(1)}, bf16[256,128]{1,0:T(8,128)(2,1)S(1)}, u32[]{:S(2)}, u32[]{:S(2)}) collective-permute-start(bf16[256,128]{1,0:T(8,128)(2,1)S(1)} %get-tuple-element.8), channel_id=1, source_target_pairs={{0,160},{32,192},{64,224},{96,0},{128,32},{160,64},{192,96},{224,1... | collective-permute-start | bytes 196616 | tf_op jit(solution)/shard_map/ppermute | solution.py:308
  11.6 1.5 %convert_multiply_fusion.tele_ref = f32[256,128]{1,0:T(8,128)} fusion(bf16[256,128]{1,0:T(8,128)(2,1)} %param.6), kind=kLoop, calls=%fused_computation | loop fusion | flops 65536 | bytes 196608 | tf_op jit(solution)/shard_map/mul | solution.py:301
  13.1 1.3 fusion.3.cols_ref
  14.3 3.3 %copy.7 = bf16[1,1,256,4096]{2,3,1,0:T(8,128)(2,1)S(1)} copy(bf16[1,1,256,4096]{3,2,1,0:T(8,128)(2,1)} %param.8) | data formatting | bytes 4194304 | tf_op args[2]
  17.6 6.7 %copy.9.adj_ref = bf16[256,64,64]{2,1,0:T(8,128)(2,1)} copy(bf16[256,64,64]{0,2,1:T(8,128)(2,1)S(1)} %bitcast.28) | data formatting | bytes 4194304 | tf_op jit(solution)/shard_map/reshape | solution.py:295
  24.9 0.0 collective-permute-done
  24.9 0.1 collective-permute-start.5
  25.1 2.3 %collective-permute-start.6 = (bf16[256,128]{1,0:T(8,128)(2,1)S(1)}, bf16[256,128]{1,0:T(8,128)(2,1)S(1)}, u32[]{:S(2)}, u32[]{:S(2)}) collective-permute-start(bf16[256,128]{1,0:T(8,128)(2,1)S(1)} %get-tuple-element.8), channel_id=1, source_target_pairs={{0,224},{32,0},{64,32},{96,64},{128,96},{160,128},{192,160},{224,1... | collective-permute-start | bytes 196616 | tf_op jit(solution)/shard_map/ppermute | solution.py:308
  27.5 1.8 %collective-permute-done.5 = bf16[256,128]{1,0:T(8,128)(2,1)S(1)} collective-permute-done((bf16[256,128]{1,0:T(8,128)(2,1)S(1)}, bf16[256,128]{1,0:T(8,128)(2,1)S(1)}, u32[]{:S(2)}, u32[]{:S(2)}) %collective-permute-start.5) | collective-permute-done | bytes 65568 | tf_op jit(solution)/shard_map/ppermute | solution.py:308
  29.3 1.0 collective-permute-done.6
  30.3 0.8 copy-done
  31.2 9.7 %shard_map.64 = f32[2,8,2,4,64,128]{5,4,3,2,1,0:T(8,128)} custom-call(s32[256]{0:T(256)} %bitcast.31, s32[256]{0:T(256)} %fusion.3.cols_ref, s32[1]{0:T(128)} %bitcast.24.count_ref, bf16[256,64,64]{2,1,0:T(8,128)(2,1)} %copy.9.adj_ref, bf16[32,64,128]{2,1,0:T(8,128)(2,1)} %bitcast.30), custom_call_target="tpu_custom_call" | custom-call | flops 268435456 | bytes 6291456 | tf_op jit(solution)/shard_map/pallas_call | solution.py:274
  40.9 0.7 mul.25.scale_ref
  41.6 0.8 broadcast_in_dim.2.s9_ref
  42.4 49.0 %shard_map.65 = bf16[8,256,128]{2,1,0:T(8,128)(2,1)} custom-call(f32[2,8,2,256,128]{4,3,2,1,0:T(8,128)} %bitcast.26, f32[256,128]{1,0:T(8,128)} %broadcast_in_dim.2.s9_ref, f32[256,128]{1,0:T(8,128)} %mul.25.scale_ref, f32[256,128]{1,0:T(8,128)} %convert_multiply_fusion.tele_ref), custom_call_target="tpu_custom_call" | custom-call | tf_op jit(solution)/shard_map/pallas_call | solution.py:167
  91.4 9.7 %shard_map.66 = f32[2,8,2,4,64,128]{5,4,3,2,1,0:T(8,128)} custom-call(s32[256]{0:T(256)} %bitcast.32, s32[256]{0:T(256)} %bitcast.34, s32[1]{0:T(128)} %bitcast.25.count_ref, bf16[256,64,64]{2,1,0:T(8,128)(2,1)} %copy.9.adj_ref, bf16[32,64,128]{2,1,0:T(8,128)(2,1)} %bitcast.29), custom_call_target="tpu_custom_call" | custom-call | flops 268435456 | bytes 6291456 | tf_op jit(solution)/shard_map/pallas_call | solution.py:274
  101.1 36.7 %shard_map.67 = bf16[256,128]{1,0:T(8,128)(2,1)} custom-call(f32[2,8,2,256,128]{4,3,2,1,0:T(8,128)} %bitcast.27, f32[256,128]{1,0:T(8,128)} %broadcast_in_dim.2.s9_ref, f32[256,128]{1,0:T(8,128)} %mul.25.scale_ref, f32[256,128]{1,0:T(8,128)} %convert_multiply_fusion.tele_ref), custom_call_target="tpu_custom_call" | custom-call | tf_op jit(solution)/shard_map/pallas_call | solution.py:167
  137.8 1.5 %copy.19 = bf16[256,128]{1,0:T(8,128)(2,1)} copy(bf16[256,128]{1,0:T(8,128)(2,1)} %shard_map.67) | data formatting | bytes 131072
  (12 shorter events, 0.1 us)
Async XLA Ops:
  1.6 23.3 %collective-permute-start = (bf16[256,128]{1,0:T(8,128)(2,1)S(1)}, bf16[256,128]{1,0:T(8,128)(2,1)S(1)}, u32[]{:S(2)}, u32[]{:S(2)}) collective-permute-start(bf16[256,128]{1,0:T(8,128)(2,1)S(1)} %get-tuple-element.8), channel_id=1, source_target_pairs={{0,32},{32,64},{64,96},{96,128},{128,160},{160,192},{192,224},{224... | collective-permute-start | bytes 196616 | tf_op jit(solution)/shard_map/ppermute | solution.py:308
  3.1 22.0 %collective-permute-start.1 = (bf16[256,128]{1,0:T(8,128)(2,1)S(1)}, bf16[256,128]{1,0:T(8,128)(2,1)S(1)}, u32[]{:S(2)}, u32[]{:S(2)}) collective-permute-start(bf16[256,128]{1,0:T(8,128)(2,1)S(1)} %get-tuple-element.8), channel_id=1, source_target_pairs={{0,64},{32,96},{64,128},{96,160},{128,192},{160,224},{192,0},{224,... | collective-permute-start | bytes 196616 | tf_op jit(solution)/shard_map/ppermute | solution.py:308
  4.6 22.8 %collective-permute-start.2 = (bf16[256,128]{1,0:T(8,128)(2,1)S(1)}, bf16[256,128]{1,0:T(8,128)(2,1)S(1)}, u32[]{:S(2)}, u32[]{:S(2)}) collective-permute-start(bf16[256,128]{1,0:T(8,128)(2,1)S(1)} %get-tuple-element.8), channel_id=1, source_target_pairs={{0,96},{32,128},{64,160},{96,192},{128,224},{160,0},{192,32},{224,... | collective-permute-start | bytes 196616 | tf_op jit(solution)/shard_map/ppermute | solution.py:308
  7.4 20.0 %collective-permute-start.3 = (bf16[256,128]{1,0:T(8,128)(2,1)S(1)}, bf16[256,128]{1,0:T(8,128)(2,1)S(1)}, u32[]{:S(2)}, u32[]{:S(2)}) collective-permute-start(bf16[256,128]{1,0:T(8,128)(2,1)S(1)} %get-tuple-element.8), channel_id=1, source_target_pairs={{0,128},{32,160},{64,192},{96,224},{128,0},{160,32},{192,64},{224,... | collective-permute-start | bytes 196616 | tf_op jit(solution)/shard_map/ppermute | solution.py:308
  8.2 19.3 %collective-permute-start.4 = (bf16[256,128]{1,0:T(8,128)(2,1)S(1)}, bf16[256,128]{1,0:T(8,128)(2,1)S(1)}, u32[]{:S(2)}, u32[]{:S(2)}) collective-permute-start(bf16[256,128]{1,0:T(8,128)(2,1)S(1)} %get-tuple-element.8), channel_id=1, source_target_pairs={{0,160},{32,192},{64,224},{96,0},{128,32},{160,64},{192,96},{224,1... | collective-permute-start | bytes 196616 | tf_op jit(solution)/shard_map/ppermute | solution.py:308
  24.9 4.3 %collective-permute-start.5 = (bf16[256,128]{1,0:T(8,128)(2,1)S(1)}, bf16[256,128]{1,0:T(8,128)(2,1)S(1)}, u32[]{:S(2)}, u32[]{:S(2)}) collective-permute-start(bf16[256,128]{1,0:T(8,128)(2,1)S(1)} %get-tuple-element.8), channel_id=1, source_target_pairs={{0,192},{32,224},{64,0},{96,32},{128,64},{160,96},{192,128},{224,1... | collective-permute-start | bytes 196616 | tf_op jit(solution)/shard_map/ppermute | solution.py:308
  25.1 5.2 %collective-permute-start.6 = (bf16[256,128]{1,0:T(8,128)(2,1)S(1)}, bf16[256,128]{1,0:T(8,128)(2,1)S(1)}, u32[]{:S(2)}, u32[]{:S(2)}) collective-permute-start(bf16[256,128]{1,0:T(8,128)(2,1)S(1)} %get-tuple-element.8), channel_id=1, source_target_pairs={{0,224},{32,0},{64,32},{96,64},{128,96},{160,128},{192,160},{224,1... | collective-permute-start | bytes 196616 | tf_op jit(solution)/shard_map/ppermute | solution.py:308
  30.3 0.8 copy-start

commit v12 on v10

--- a/solution.py
+++ b/solution.py
@@ -242,7 +242,6 @@
 
 def block_product_kernel(group, rows_ref, cols_ref, count_ref, adj_ref, panel_ref,
                          pieces_ref):
-    cores, n_z, n_y, per_piece = pieces_ref.shape[:4]
     pieces_ref[...] = jnp.zeros_like(pieces_ref)
     count = count_ref[0]
     slots = adj_ref.shape[0]
@@ -255,10 +254,8 @@
             p = jnp.dot(adj_ref[t], panel_ref[cols_ref[t]], preferred_element_type=jnp.float32)
             prods.append(jnp.where(t < count, p, jnp.zeros_like(p)))
         for i in range(group):
-            r = rows_ref[base + i]
-            j = r // per_piece
-            at = (lax.rem(j, cores), lax.rem(j // cores, n_z), j // (cores * n_z), lax.rem(r, per_piece))
-            pieces_ref[at] += prods[i]
+            slot = rows_ref[base + i]
+            pieces_ref[slot] += prods[i]
         return carry
 
     lax.fori_loop(0, slots // group, body, 0)
@@ -267,16 +264,12 @@
 def block_product(row_ids, col_ids, count, dev_tiles, col_panel, row_tiles, nodes_dev):
     slots = dev_tiles.shape[0]
     feat_width = col_panel.shape[2]
-    per_piece = nodes_dev // TILE
     group = 16 if slots % 16 == 0 else 1
     smem = pl.BlockSpec(memory_space=pltpu.SMEM)
     vmem = pl.BlockSpec(memory_space=pltpu.VMEM)
     return pl.pallas_call(
         functools.partial(block_product_kernel, group),
-        out_shape=jax.ShapeDtypeStruct(
-            (CORES, Z_RING, row_tiles // (per_piece * CORES * Z_RING), per_piece, TILE, feat_width),
-            jnp.float32,
-        ),
+        out_shape=jax.ShapeDtypeStruct((row_tiles, TILE, feat_width), jnp.float32),
         in_specs=[smem, smem, smem, vmem, vmem],
         out_specs=vmem,
         cost_estimate=pl.CostEstimate(
@@ -303,13 +296,18 @@
     scale = jnp.broadcast_to(norm_scale, features.shape)
     source = (norm_scale * features.astype(jnp.float32)).astype(jnp.bfloat16)
     gathered = row_all_gather(source)
+    per_piece = nodes_dev // TILE
+    n_y = col_count // (CORES * Z_RING)
+    piece_j = row_ids_all // per_piece
+    row_slots = (((piece_j % CORES) * Z_RING + (piece_j // CORES) % Z_RING) * n_y
+                 + piece_j // (CORES * Z_RING)) * per_piece + row_ids_all % per_piece
     for repeat in range(STEPS):
         col_panel = gathered.reshape(-1, TILE, feat_width)
         pieces = block_product(
-            row_ids_all, col_ids_all, live_count, dev_tiles, col_panel, row_tiles, nodes_dev
+            row_slots, col_ids_all, live_count, dev_tiles, col_panel, row_tiles, nodes_dev
         )
         gathered = col_reduce_scatter(
-            pieces.reshape(pieces.shape[:3] + (nodes_dev, feat_width)),
+            pieces.reshape(CORES, Z_RING, -1, nodes_dev, feat_width),
             scale9, scale, teleport, repeat == STEPS - 1,
         )
     return gathered

time: 135 us -> 134 us (level)
  Pallas kernels: 119 us -> 116 us
    pallas_call x2, Pallas kernels: 19.4 us -> 16.9 us  [block_product(): pl.pallas_call(functools.partial(block_product_kernel, group), out_shape=...]
where the time goes in v12:
time: 134 us; the launch traced here: 133 us
  Pallas kernels  116 us (87%)
  local copies, waits for them, and re-layouts  12.9 us (10%)
  other arithmetic  3.51 us (3%)
    pallas_call x2, Pallas kernels, col_reduce_scatter(): pl.pallas_call(functools.partial(reduce_scatter_kernel, n_z, chunks, last...  85.8 us
    pallas_call x2, Pallas kernels, block_product(): pl.pallas_call(functools.partial(block_product_kernel, group), out_shape=...  16.9 us
    pallas_call x1, Pallas kernels, row_all_gather(): pl.pallas_call(functools.partial(all_gather_kernel, n), out_shape=jax.Sha...  13.4 us
    reshape x1, local copies, waits for them, and re-layouts, shards(): dev_tiles = adj_tiles.reshape(tile_slots, TILE, TILE)  6.68 us
    unnamed x2, local copies, waits for them, and re-layouts  4.75 us

profile of v12, /device:TPU:8, one launch (start us, length us, event | category | flops | bytes accessed | tf_op | source)
XLA Modules:
  0.0 133.2 jit_solution(1438409566612813553)
XLA Ops:
  0.7 1.2 fusion.3.rows_ref
  1.9 0.7 broadcast_multiply_fusion
  2.6 0.8 broadcast_in_dim.2.s9_ref
  3.4 0.8 mul.39.scale_ref
  4.1 1.6 %convert_multiply_fusion = (f32[256,128]{1,0:T(8,128)}, bf16[256,128]{1,0:T(8,128)(2,1)}) fusion(bf16[256,128]{1,0:T(8,128)(2,1)} %param.6, f32[256]{0:T(256)S(1)} %get-tuple-element.6), kind=kLoop, calls=%fused_computation | loop fusion | flops 131072 | bytes 263168 | tf_op jit(solution)/shard_map/mul | solution.py:294
  5.7 13.4 %shard_map.64 = bf16[8,256,128]{2,1,0:T(8,128)(2,1)} custom-call(bf16[256,128]{1,0:T(8,128)(2,1)} %get-tuple-element.8.src_ref), custom_call_target="tpu_custom_call" | custom-call | tf_op jit(solution)/shard_map/pallas_call | solution.py:233
  19.1 3.3 %copy.7 = bf16[1,1,256,4096]{2,3,1,0:T(8,128)(2,1)S(1)} copy(bf16[1,1,256,4096]{3,2,1,0:T(8,128)(2,1)} %param.8) | data formatting | bytes 4194304 | tf_op args[2]
  22.4 6.7 %copy.9.adj_ref = bf16[256,64,64]{2,1,0:T(8,128)(2,1)} copy(bf16[256,64,64]{0,2,1:T(8,128)(2,1)S(1)} %bitcast.12) | data formatting | bytes 4194304 | tf_op jit(solution)/shard_map/reshape | solution.py:288
  29.0 8.4 %shard_map.65 = f32[128,64,128]{2,1,0:T(8,128)} custom-call(s32[256]{0:T(256)} %fusion.3.rows_ref, s32[256]{0:T(256)} %bitcast.15, s32[1]{0:T(128)} %bitcast.8.count_ref, bf16[256,64,64]{2,1,0:T(8,128)(2,1)} %copy.9.adj_ref, bf16[32,64,128]{2,1,0:T(8,128)(2,1)} %bitcast.14), custom_call_target="tpu_custom_call" | custom-call | flops 268435456 | bytes 6291456 | tf_op jit(solution)/shard_map/pallas_call | solution.py:270
  37.5 49.9 %shard_map.66 = bf16[8,256,128]{2,1,0:T(8,128)(2,1)} custom-call(f32[2,8,2,256,128]{4,3,2,1,0:T(8,128)} %bitcast.10, f32[256,128]{1,0:T(8,128)} %broadcast_in_dim.2.s9_ref, f32[256,128]{1,0:T(8,128)} %mul.39.scale_ref, f32[256,128]{1,0:T(8,128)} %get-tuple-element.7.tele_ref), custom_call_target="tpu_custom_call" | custom-call | tf_op jit(solution)/shard_map/pallas_call | solution.py:167
  87.4 8.4 %shard_map.67 = f32[128,64,128]{2,1,0:T(8,128)} custom-call(s32[256]{0:T(256)} %fusion.3.rows_ref, s32[256]{0:T(256)} %bitcast.16, s32[1]{0:T(128)} %bitcast.9.count_ref, bf16[256,64,64]{2,1,0:T(8,128)(2,1)} %copy.9.adj_ref, bf16[32,64,128]{2,1,0:T(8,128)(2,1)} %bitcast.13), custom_call_target="tpu_custom_call" | custom-call | flops 268435456 | bytes 6291456 | tf_op jit(solution)/shard_map/pallas_call | solution.py:270
  95.8 35.9 %shard_map.68 = bf16[256,128]{1,0:T(8,128)(2,1)} custom-call(f32[2,8,2,256,128]{4,3,2,1,0:T(8,128)} %bitcast.11, f32[256,128]{1,0:T(8,128)} %broadcast_in_dim.2.s9_ref, f32[256,128]{1,0:T(8,128)} %mul.39.scale_ref, f32[256,128]{1,0:T(8,128)} %get-tuple-element.7.tele_ref), custom_call_target="tpu_custom_call" | custom-call | tf_op jit(solution)/shard_map/pallas_call | solution.py:167
  131.7 1.5 %copy.12 = bf16[256,128]{1,0:T(8,128)(2,1)} copy(bf16[256,128]{1,0:T(8,128)(2,1)} %shard_map.68) | data formatting | bytes 131072

commit v13 on v12

--- a/solution.py
+++ b/solution.py
@@ -243,7 +243,6 @@
 def block_product_kernel(group, rows_ref, cols_ref, count_ref, adj_ref, panel_ref,
                          pieces_ref):
     pieces_ref[...] = jnp.zeros_like(pieces_ref)
-    count = count_ref[0]
     slots = adj_ref.shape[0]
 
     def body(g, carry):
@@ -251,8 +250,8 @@
         prods = []
         for i in range(group):
             t = base + i
-            p = jnp.dot(adj_ref[t], panel_ref[cols_ref[t]], preferred_element_type=jnp.float32)
-            prods.append(jnp.where(t < count, p, jnp.zeros_like(p)))
+            prods.append(
+                jnp.dot(adj_ref[t], panel_ref[cols_ref[t]], preferred_element_type=jnp.float32))
         for i in range(group):
             slot = rows_ref[base + i]
             pieces_ref[slot] += prods[i]
@@ -285,7 +284,9 @@
     nodes_dev = features.shape[0]
     feat_width = features.shape[1]
     tile_slots = adj_tiles.shape[2]
-    dev_tiles = adj_tiles.reshape(tile_slots, TILE, TILE)
+    live = jnp.arange(tile_slots, dtype=jnp.int32) < tile_counts.reshape(())
+    dev_tiles = jnp.where(live[:, None, None], adj_tiles.reshape(tile_slots, TILE, TILE),
+                          jnp.zeros((), adj_tiles.dtype))
     row_ids_all = tile_rows.reshape(tile_slots)
     col_ids_all = tile_cols.reshape(tile_slots)
     live_count = tile_counts.reshape(1)

time: 134 us -> 137 us (1.022)
  other arithmetic: 3.51 us -> 7.52 us
    select_n x0 -> x1, other arithmetic: none -> 4.01 us  [shards(): jnp.where(live[:, None, None], adj_tiles.reshape(tile_slots, TILE, TILE),...]
where the time goes in v13:
time: 137 us
  Pallas kernels  116 us (85%)
  local copies, waits for them, and re-layouts  12.9 us (9%)
  other arithmetic  7.52 us (5%)
    pallas_call x2, Pallas kernels, col_reduce_scatter(): pl.pallas_call(functools.partial(reduce_scatter_kernel, n_z, chunks, last...  85.6 us
    pallas_call x2, Pallas kernels, block_product(): pl.pallas_call(functools.partial(block_product_kernel, group), out_shape=...  16.7 us
    pallas_call x1, Pallas kernels, row_all_gather(): pl.pallas_call(functools.partial(all_gather_kernel, n), out_shape=jax.Sha...  13.4 us
    reshape x1, local copies, waits for them, and re-layouts, shards(): adj_tiles.reshape(tile_slots, TILE, TILE)  6.68 us
    unnamed x2, local copies, waits for them, and re-layouts  4.75 us
    select_n x1, other arithmetic, shards(): jnp.where(live[:, None, None], adj_tiles.reshape(tile_slots, TILE, TILE),...  4.01 us

profile of v13, /device:TPU:8, one launch (start us, length us, event | category | flops | bytes accessed | tf_op | source)
XLA Modules:
  0.0 136.8 jit_solution(4443969376103701746)
XLA Ops:
  0.7 1.3 fusion.3.rows_ref
  1.9 0.7 broadcast_multiply_fusion
  2.6 0.8 broadcast_in_dim.24.s9_ref
  3.4 0.8 mul.39.scale_ref
  4.1 1.6 %convert_multiply_fusion = (f32[256,128]{1,0:T(8,128)}, bf16[256,128]{1,0:T(8,128)(2,1)}) fusion(bf16[256,128]{1,0:T(8,128)(2,1)} %param.6, f32[256]{0:T(256)S(1)} %get-tuple-element.6), kind=kLoop, calls=%fused_computation.1 | loop fusion | flops 131072 | bytes 263168 | tf_op jit(solution)/shard_map/mul | solution.py:295
  5.7 13.4 %shard_map.64 = bf16[8,256,128]{2,1,0:T(8,128)(2,1)} custom-call(bf16[256,128]{1,0:T(8,128)(2,1)} %get-tuple-element.8.src_ref), custom_call_target="tpu_custom_call" | custom-call | tf_op jit(solution)/shard_map/pallas_call | solution.py:233
  19.1 3.3 %copy.7 = bf16[1,1,256,4096]{2,3,1,0:T(8,128)(2,1)S(1)} copy(bf16[1,1,256,4096]{3,2,1,0:T(8,128)(2,1)} %param.8) | data formatting | bytes 4194304 | tf_op args[2]
  22.4 6.7 %copy.8 = bf16[256,64,64]{2,1,0:T(8,128)(2,1)} copy(bf16[256,64,64]{0,2,1:T(8,128)(2,1)S(1)} %bitcast.14) | data formatting | bytes 4194304 | tf_op jit(solution)/shard_map/reshape | solution.py:288
  29.0 4.0 %broadcast_select_fusion.adj_ref = bf16[256,64,64]{2,1,0:T(8,128)(2,1)} fusion(bf16[256,64,64]{2,1,0:T(8,128)(2,1)} %copy.8, pred[256]{0:T(512)(128)(4,1)S(1)} %iota_compare_fusion), kind=kLoop, calls=%fused_computation | loop fusion | flops 1048576 | bytes 4194560 | tf_op jit(solution)/shard_map/jit(_where)/select_n | solution.py:288
  33.1 8.4 %shard_map.65 = f32[128,64,128]{2,1,0:T(8,128)} custom-call(s32[256]{0:T(256)} %fusion.3.rows_ref, s32[256]{0:T(256)} %bitcast.17, s32[1]{0:T(128)} %bitcast.9.count_ref, bf16[256,64,64]{2,1,0:T(8,128)(2,1)} %broadcast_select_fusion.adj_ref, bf16[32,64,128]{2,1,0:T(8,128)(2,1)} %bitcast.16), custom_call_target="tpu_custom_call" | custom-call | flops 268435456 | bytes 6291456 | tf_op jit(solution)/shard_map/pallas_call | solution.py:269
  41.4 49.9 %shard_map.66 = bf16[8,256,128]{2,1,0:T(8,128)(2,1)} custom-call(f32[2,8,2,256,128]{4,3,2,1,0:T(8,128)} %bitcast.12, f32[256,128]{1,0:T(8,128)} %broadcast_in_dim.24.s9_ref, f32[256,128]{1,0:T(8,128)} %mul.39.scale_ref, f32[256,128]{1,0:T(8,128)} %get-tuple-element.7.tele_ref), custom_call_target="tpu_custom_call" | custom-call | tf_op jit(solution)/shard_map/pallas_call | solution.py:167
  91.3 8.4 %shard_map.67 = f32[128,64,128]{2,1,0:T(8,128)} custom-call(s32[256]{0:T(256)} %fusion.3.rows_ref, s32[256]{0:T(256)} %bitcast.18, s32[1]{0:T(128)} %bitcast.10.count_ref, bf16[256,64,64]{2,1,0:T(8,128)(2,1)} %broadcast_select_fusion.adj_ref, bf16[32,64,128]{2,1,0:T(8,128)(2,1)} %bitcast.15), custom_call_target="tpu_custom_call" | custom-call | flops 268435456 | bytes 6291456 | tf_op jit(solution)/shard_map/pallas_call | solution.py:269
  99.7 35.6 %shard_map.68 = bf16[256,128]{1,0:T(8,128)(2,1)} custom-call(f32[2,8,2,256,128]{4,3,2,1,0:T(8,128)} %bitcast.13, f32[256,128]{1,0:T(8,128)} %broadcast_in_dim.24.s9_ref, f32[256,128]{1,0:T(8,128)} %mul.39.scale_ref, f32[256,128]{1,0:T(8,128)} %get-tuple-element.7.tele_ref), custom_call_target="tpu_custom_call" | custom-call | tf_op jit(solution)/shard_map/pallas_call | solution.py:167
  135.3 1.5 %copy.11 = bf16[256,128]{1,0:T(8,128)(2,1)} copy(bf16[256,128]{1,0:T(8,128)(2,1)} %shard_map.68) | data formatting | bytes 131072
  (1 shorter events, 0.0 us)

commit v14 on v12

--- a/solution.py
+++ b/solution.py
@@ -118,6 +118,17 @@
                 cp.start()
                 sends.append(cp)
 
+    if not last:
+        ag_send, ag_recv = ag_sems
+
+        def ag_copy(peer, slot, i):
+            part = pl.ds(i * size, size)
+            return pltpu.make_async_remote_copy(
+                src_ref=out_ref.at[row, part], dst_ref=out_ref.at[slot, part],
+                send_sem=ag_send.at[peer, i], recv_sem=ag_recv.at[slot, i],
+                device_id=(peer, c), device_id_type=MESH,
+            )
+
     for i in range(chunks):
         part = pl.ds(i * size, size)
         y_copy(i).wait_recv()
@@ -127,25 +138,17 @@
             out_ref[part] = current.astype(out_ref.dtype)
         else:
             out_ref[row, part] = (scale_ref[part] * current).astype(out_ref.dtype)
+
+            def ag_start(k, carry, i=i):
+                ag_copy(lax.rem(row + k, n_row), row, i).start()
+                return carry
+
+            lax.fori_loop(1, n_row, ag_start, 0)
     if not last:
-        ag_send, ag_recv = ag_sems
-
-        def ag_copy(peer, slot):
-            return pltpu.make_async_remote_copy(
-                src_ref=out_ref.at[row], dst_ref=out_ref.at[slot], send_sem=ag_send.at[peer],
-                recv_sem=ag_recv.at[slot], device_id=(peer, c), device_id_type=MESH,
-            )
-
-        def ag_start(k, carry):
-            ag_copy(lax.rem(row + k, n_row), row).start()
-            return carry
-
-        lax.fori_loop(1, n_row, ag_start, 0)
-
         def ag_finish(k, carry):
-            sender = lax.rem(row + n_row - k, n_row)
-            ag_copy(sender, sender).wait_recv()
-            ag_copy(lax.rem(row + k, n_row), row).wait_send()
+            for i in range(chunks):
+                ag_copy(lax.rem(row + n_row - k, n_row), lax.rem(row + n_row - k, n_row), i).wait_recv()
+                ag_copy(lax.rem(row + k, n_row), row, i).wait_send()
             return carry
 
         lax.fori_loop(1, n_row, ag_finish, 0)
@@ -163,7 +166,7 @@
     piece = (nodes_dev, feat_width)
     vmem = pl.BlockSpec(memory_space=pltpu.VMEM)
     out_shape = piece if last else (n_row,) + piece
-    ag_sems = [] if last else [pltpu.SemaphoreType.DMA((n_row,))] * 2
+    ag_sems = [] if last else [pltpu.SemaphoreType.DMA((n_row, chunks))] * 2
     return pl.pallas_call(
         functools.partial(reduce_scatter_kernel, n_z, chunks, last),
         out_shape=jax.ShapeDtypeStruct(out_shape, jnp.bfloat16),

time: 134 us -> 132 us (0.985)
  Pallas kernels: 116 us -> 114 us
    pallas_call x2, Pallas kernels: 85.8 us -> 84.3 us  [col_reduce_scatter(): pl.pallas_call(functools.partial(reduce_scatter_kernel, n_z, chunks, last...]
where the time goes in v14:
time: 132 us
  Pallas kernels  114 us (86%)
  local copies, waits for them, and re-layouts  12.9 us (10%)
  other arithmetic  3.51 us (3%)
    pallas_call x2, Pallas kernels, col_reduce_scatter(): pl.pallas_call(functools.partial(reduce_scatter_kernel, n_z, chunks, last...  84.3 us
    pallas_call x2, Pallas kernels, block_product(): pl.pallas_call(functools.partial(block_product_kernel, group), out_shape=...  16.8 us
    pallas_call x1, Pallas kernels, row_all_gather(): pl.pallas_call(functools.partial(all_gather_kernel, n), out_shape=jax.Sha...  13.4 us
    reshape x1, local copies, waits for them, and re-layouts, shards(): dev_tiles = adj_tiles.reshape(tile_slots, TILE, TILE)  6.68 us
    unnamed x2, local copies, waits for them, and re-layouts  4.75 us

profile of v14, /device:TPU:8, one launch (start us, length us, event | category | flops | bytes accessed | tf_op | source)
XLA Modules:
  0.0 131.6 jit_solution(9918028127309731276)
XLA Ops:
  0.7 1.2 fusion.3.rows_ref
  1.9 0.7 broadcast_multiply_fusion
  2.6 0.8 broadcast_in_dim.2.s9_ref
  3.4 0.8 mul.39.scale_ref
  4.1 1.6 %convert_multiply_fusion = (f32[256,128]{1,0:T(8,128)}, bf16[256,128]{1,0:T(8,128)(2,1)}) fusion(bf16[256,128]{1,0:T(8,128)(2,1)} %param.6, f32[256]{0:T(256)S(1)} %get-tuple-element.6), kind=kLoop, calls=%fused_computation | loop fusion | flops 131072 | bytes 263168 | tf_op jit(solution)/shard_map/mul | solution.py:297
  5.7 13.4 %shard_map.64 = bf16[8,256,128]{2,1,0:T(8,128)(2,1)} custom-call(bf16[256,128]{1,0:T(8,128)(2,1)} %get-tuple-element.8.src_ref), custom_call_target="tpu_custom_call" | custom-call | tf_op jit(solution)/shard_map/pallas_call | solution.py:236
  19.1 3.3 %copy.7 = bf16[1,1,256,4096]{2,3,1,0:T(8,128)(2,1)S(1)} copy(bf16[1,1,256,4096]{3,2,1,0:T(8,128)(2,1)} %param.8) | data formatting | bytes 4194304 | tf_op args[2]
  22.4 6.7 %copy.9.adj_ref = bf16[256,64,64]{2,1,0:T(8,128)(2,1)} copy(bf16[256,64,64]{0,2,1:T(8,128)(2,1)S(1)} %bitcast.12) | data formatting | bytes 4194304 | tf_op jit(solution)/shard_map/reshape | solution.py:291
  29.0 8.4 %shard_map.65 = f32[128,64,128]{2,1,0:T(8,128)} custom-call(s32[256]{0:T(256)} %fusion.3.rows_ref, s32[256]{0:T(256)} %bitcast.15, s32[1]{0:T(128)} %bitcast.8.count_ref, bf16[256,64,64]{2,1,0:T(8,128)(2,1)} %copy.9.adj_ref, bf16[32,64,128]{2,1,0:T(8,128)(2,1)} %bitcast.14), custom_call_target="tpu_custom_call" | custom-call | flops 268435456 | bytes 6291456 | tf_op jit(solution)/shard_map/pallas_call | solution.py:273
  37.5 48.5 %shard_map.66 = bf16[8,256,128]{2,1,0:T(8,128)(2,1)} custom-call(f32[2,8,2,256,128]{4,3,2,1,0:T(8,128)} %bitcast.10, f32[256,128]{1,0:T(8,128)} %broadcast_in_dim.2.s9_ref, f32[256,128]{1,0:T(8,128)} %mul.39.scale_ref, f32[256,128]{1,0:T(8,128)} %get-tuple-element.7.tele_ref), custom_call_target="tpu_custom_call" | custom-call | tf_op jit(solution)/shard_map/pallas_call | solution.py:170
  85.9 8.4 %shard_map.67 = f32[128,64,128]{2,1,0:T(8,128)} custom-call(s32[256]{0:T(256)} %fusion.3.rows_ref, s32[256]{0:T(256)} %bitcast.16, s32[1]{0:T(128)} %bitcast.9.count_ref, bf16[256,64,64]{2,1,0:T(8,128)(2,1)} %copy.9.adj_ref, bf16[32,64,128]{2,1,0:T(8,128)(2,1)} %bitcast.13), custom_call_target="tpu_custom_call" | custom-call | flops 268435456 | bytes 6291456 | tf_op jit(solution)/shard_map/pallas_call | solution.py:273
  94.4 35.8 %shard_map.68 = bf16[256,128]{1,0:T(8,128)(2,1)} custom-call(f32[2,8,2,256,128]{4,3,2,1,0:T(8,128)} %bitcast.11, f32[256,128]{1,0:T(8,128)} %broadcast_in_dim.2.s9_ref, f32[256,128]{1,0:T(8,128)} %mul.39.scale_ref, f32[256,128]{1,0:T(8,128)} %get-tuple-element.7.tele_ref), custom_call_target="tpu_custom_call" | custom-call | tf_op jit(solution)/shard_map/pallas_call | solution.py:170
  130.2 1.5 %copy.12 = bf16[256,128]{1,0:T(8,128)(2,1)} copy(bf16[256,128]{1,0:T(8,128)(2,1)} %shard_map.68) | data formatting | bytes 131072

commit v15 on v14

--- a/solution.py
+++ b/solution.py
@@ -156,7 +156,7 @@
         cp.wait_send()
 
 
-RS_CHUNKS = 4
+RS_CHUNKS = 8
 
 
 def col_reduce_scatter(pieces, s9, scale, tele, last):

time: 132 us -> 133 us (level)
  Pallas kernels: 114 us -> 116 us
where the time goes in v15:
time: 133 us
  Pallas kernels  116 us (87%)
  local copies, waits for them, and re-layouts  12.9 us (10%)
  other arithmetic  3.51 us (3%)
    pallas_call x2, Pallas kernels, col_reduce_scatter(): pl.pallas_call(functools.partial(reduce_scatter_kernel, n_z, chunks, last...  85.3 us
    pallas_call x2, Pallas kernels, block_product(): pl.pallas_call(functools.partial(block_product_kernel, group), out_shape=...  16.8 us
    pallas_call x1, Pallas kernels, row_all_gather(): pl.pallas_call(functools.partial(all_gather_kernel, n), out_shape=jax.Sha...  13.4 us
    reshape x1, local copies, waits for them, and re-layouts, shards(): dev_tiles = adj_tiles.reshape(tile_slots, TILE, TILE)  6.68 us
    unnamed x2, local copies, waits for them, and re-layouts  4.75 us

profile of v15, /device:TPU:8, one launch (start us, length us, event | category | flops | bytes accessed | tf_op | source)
XLA Modules:
  0.0 132.7 jit_solution(3378090760174930654)
XLA Ops:
  0.7 1.2 fusion.3.rows_ref
  1.9 0.7 broadcast_multiply_fusion
  2.6 0.8 broadcast_in_dim.2.s9_ref
  3.4 0.8 mul.39.scale_ref
  4.1 1.6 %convert_multiply_fusion = (f32[256,128]{1,0:T(8,128)}, bf16[256,128]{1,0:T(8,128)(2,1)}) fusion(bf16[256,128]{1,0:T(8,128)(2,1)} %param.6, f32[256]{0:T(256)S(1)} %get-tuple-element.6), kind=kLoop, calls=%fused_computation | loop fusion | flops 131072 | bytes 263168 | tf_op jit(solution)/shard_map/mul | solution.py:297
  5.7 13.4 %shard_map.64 = bf16[8,256,128]{2,1,0:T(8,128)(2,1)} custom-call(bf16[256,128]{1,0:T(8,128)(2,1)} %get-tuple-element.8.src_ref), custom_call_target="tpu_custom_call" | custom-call | tf_op jit(solution)/shard_map/pallas_call | solution.py:236
  19.1 3.3 %copy.7 = bf16[1,1,256,4096]{2,3,1,0:T(8,128)(2,1)S(1)} copy(bf16[1,1,256,4096]{3,2,1,0:T(8,128)(2,1)} %param.8) | data formatting | bytes 4194304 | tf_op args[2]
  22.4 6.7 %copy.9.adj_ref = bf16[256,64,64]{2,1,0:T(8,128)(2,1)} copy(bf16[256,64,64]{0,2,1:T(8,128)(2,1)S(1)} %bitcast.12) | data formatting | bytes 4194304 | tf_op jit(solution)/shard_map/reshape | solution.py:291
  29.0 8.4 %shard_map.65 = f32[128,64,128]{2,1,0:T(8,128)} custom-call(s32[256]{0:T(256)} %fusion.3.rows_ref, s32[256]{0:T(256)} %bitcast.15, s32[1]{0:T(128)} %bitcast.8.count_ref, bf16[256,64,64]{2,1,0:T(8,128)(2,1)} %copy.9.adj_ref, bf16[32,64,128]{2,1,0:T(8,128)(2,1)} %bitcast.14), custom_call_target="tpu_custom_call" | custom-call | flops 268435456 | bytes 6291456 | tf_op jit(solution)/shard_map/pallas_call | solution.py:273
  37.5 49.1 %shard_map.66 = bf16[8,256,128]{2,1,0:T(8,128)(2,1)} custom-call(f32[2,8,2,256,128]{4,3,2,1,0:T(8,128)} %bitcast.10, f32[256,128]{1,0:T(8,128)} %broadcast_in_dim.2.s9_ref, f32[256,128]{1,0:T(8,128)} %mul.39.scale_ref, f32[256,128]{1,0:T(8,128)} %get-tuple-element.7.tele_ref), custom_call_target="tpu_custom_call" | custom-call | tf_op jit(solution)/shard_map/pallas_call | solution.py:170
  86.6 8.4 %shard_map.67 = f32[128,64,128]{2,1,0:T(8,128)} custom-call(s32[256]{0:T(256)} %fusion.3.rows_ref, s32[256]{0:T(256)} %bitcast.16, s32[1]{0:T(128)} %bitcast.9.count_ref, bf16[256,64,64]{2,1,0:T(8,128)(2,1)} %copy.9.adj_ref, bf16[32,64,128]{2,1,0:T(8,128)(2,1)} %bitcast.13), custom_call_target="tpu_custom_call" | custom-call | flops 268435456 | bytes 6291456 | tf_op jit(solution)/shard_map/pallas_call | solution.py:273
  95.0 36.2 %shard_map.68 = bf16[256,128]{1,0:T(8,128)(2,1)} custom-call(f32[2,8,2,256,128]{4,3,2,1,0:T(8,128)} %bitcast.11, f32[256,128]{1,0:T(8,128)} %broadcast_in_dim.2.s9_ref, f32[256,128]{1,0:T(8,128)} %mul.39.scale_ref, f32[256,128]{1,0:T(8,128)} %get-tuple-element.7.tele_ref), custom_call_target="tpu_custom_call" | custom-call | tf_op jit(solution)/shard_map/pallas_call | solution.py:170
  131.2 1.5 %copy.12 = bf16[256,128]{1,0:T(8,128)(2,1)} copy(bf16[256,128]{1,0:T(8,128)(2,1)} %shard_map.68) | data formatting | bytes 131072

commit v16 on v14

--- a/solution.py
+++ b/solution.py
@@ -124,7 +124,7 @@
         def ag_copy(peer, slot, i):
             part = pl.ds(i * size, size)
             return pltpu.make_async_remote_copy(
-                src_ref=out_ref.at[row, part], dst_ref=out_ref.at[slot, part],
+                src_ref=out_ref.at[row * chunks + i], dst_ref=out_ref.at[slot * chunks + i],
                 send_sem=ag_send.at[peer, i], recv_sem=ag_recv.at[slot, i],
                 device_id=(peer, c), device_id_type=MESH,
             )
@@ -137,7 +137,7 @@
         if last:
             out_ref[part] = current.astype(out_ref.dtype)
         else:
-            out_ref[row, part] = (scale_ref[part] * current).astype(out_ref.dtype)
+            out_ref[row * chunks + i] = (scale_ref[part] * current).astype(out_ref.dtype)
 
             def ag_start(k, carry, i=i):
                 ag_copy(lax.rem(row + k, n_row), row, i).start()
@@ -145,6 +145,8 @@
 
             lax.fori_loop(1, n_row, ag_start, 0)
     if not last:
+        out_ref[n_row * chunks] = jnp.zeros(out_ref.shape[1:], out_ref.dtype)
+
         def ag_finish(k, carry):
             for i in range(chunks):
                 ag_copy(lax.rem(row + n_row - k, n_row), lax.rem(row + n_row - k, n_row), i).wait_recv()
@@ -162,10 +164,10 @@
 def col_reduce_scatter(pieces, s9, scale, tele, last):
     cores, n_z, n_y, nodes_dev, feat_width = pieces.shape
     n_row = lax.axis_size("row")
-    chunks = RS_CHUNKS
+    chunks = nodes_dev // TILE
     piece = (nodes_dev, feat_width)
     vmem = pl.BlockSpec(memory_space=pltpu.VMEM)
-    out_shape = piece if last else (n_row,) + piece
+    out_shape = piece if last else (n_row * chunks + 1, TILE, feat_width)
     ag_sems = [] if last else [pltpu.SemaphoreType.DMA((n_row, chunks))] * 2
     return pl.pallas_call(
         functools.partial(reduce_scatter_kernel, n_z, chunks, last),
@@ -192,6 +194,7 @@
 def all_gather_kernel(n, src_ref, out_ref, send_sem, recv_sem):
     me = lax.axis_index("row")
     col = lax.axis_index("col")
+    per_piece = src_ref.shape[0]
 
     barrier = pltpu.get_barrier_semaphore()
 
@@ -206,7 +209,7 @@
     def copy(peer, slot):
         return pltpu.make_async_remote_copy(
             src_ref=src_ref,
-            dst_ref=out_ref.at[slot],
+            dst_ref=out_ref.at[pl.ds(slot * per_piece, per_piece)],
             send_sem=send_sem.at[peer],
             recv_sem=recv_sem.at[slot],
             device_id=(peer, col),
@@ -218,7 +221,8 @@
         return carry
 
     lax.fori_loop(1, n, start, 0)
-    out_ref[me] = src_ref[...]
+    out_ref[pl.ds(me * per_piece, per_piece)] = src_ref[...]
+    out_ref[n * per_piece] = jnp.zeros(out_ref.shape[1:], out_ref.dtype)
 
     def finish(k, carry):
         sender = lax.rem(me + n - k, n)
@@ -232,21 +236,21 @@
 def row_all_gather(source):
     n = lax.axis_size("row")
     nodes_dev, feat_width = source.shape
+    per_piece = nodes_dev // TILE
     vmem = pl.BlockSpec(memory_space=pltpu.VMEM)
     return pl.pallas_call(
         functools.partial(all_gather_kernel, n),
-        out_shape=jax.ShapeDtypeStruct((n, nodes_dev, feat_width), source.dtype),
+        out_shape=jax.ShapeDtypeStruct((n * per_piece + 1, TILE, feat_width), source.dtype),
         in_specs=[vmem],
         out_specs=vmem,
         scratch_shapes=[pltpu.SemaphoreType.DMA((n,)), pltpu.SemaphoreType.DMA((n,))],
         compiler_params=pltpu.CompilerParams(collective_id=1, has_side_effects=True),
-    )(source)
-
-
-def block_product_kernel(group, rows_ref, cols_ref, count_ref, adj_ref, panel_ref,
+    )(source.reshape(per_piece, TILE, feat_width))
+
+
+def block_product_kernel(group, rows_ref, cols_ref, adj_ref, panel_ref,
                          pieces_ref):
     pieces_ref[...] = jnp.zeros_like(pieces_ref)
-    count = count_ref[0]
     slots = adj_ref.shape[0]
 
     def body(g, carry):
@@ -255,7 +259,7 @@
         for i in range(group):
             t = base + i
             p = jnp.dot(adj_ref[t], panel_ref[cols_ref[t]], preferred_element_type=jnp.float32)
-            prods.append(jnp.where(t < count, p, jnp.zeros_like(p)))
+            prods.append(p)
         for i in range(group):
             slot = rows_ref[base + i]
             pieces_ref[slot] += prods[i]
@@ -264,7 +268,7 @@
     lax.fori_loop(0, slots // group, body, 0)
 
 
-def block_product(row_ids, col_ids, count, dev_tiles, col_panel, row_tiles, nodes_dev):
+def block_product(row_ids, col_ids, dev_tiles, col_panel, row_tiles):
     slots = dev_tiles.shape[0]
     feat_width = col_panel.shape[2]
     group = 16 if slots % 16 == 0 else 1
@@ -273,14 +277,14 @@
     return pl.pallas_call(
         functools.partial(block_product_kernel, group),
         out_shape=jax.ShapeDtypeStruct((row_tiles, TILE, feat_width), jnp.float32),
-        in_specs=[smem, smem, smem, vmem, vmem],
+        in_specs=[smem, smem, vmem, vmem],
         out_specs=vmem,
         cost_estimate=pl.CostEstimate(
             flops=2 * slots * TILE * TILE * feat_width,
             bytes_accessed=slots * TILE * TILE * 2 + row_tiles * TILE * feat_width * 4,
             transcendentals=0,
         ),
-    )(row_ids, col_ids, count, dev_tiles, col_panel)
+    )(row_ids, col_ids, dev_tiles, col_panel)
 
 
 def shards(features, degrees, adj_tiles, tile_rows, tile_cols, tile_counts):
@@ -290,8 +294,9 @@
     tile_slots = adj_tiles.shape[2]
     dev_tiles = adj_tiles.reshape(tile_slots, TILE, TILE)
     row_ids_all = tile_rows.reshape(tile_slots)
-    col_ids_all = tile_cols.reshape(tile_slots)
-    live_count = tile_counts.reshape(1)
+    live = jnp.arange(tile_slots, dtype=jnp.int32) < tile_counts.reshape(())
+    panel_tiles = lax.axis_size("row") * (nodes_dev // TILE)
+    col_ids_all = jnp.where(live, tile_cols.reshape(tile_slots), panel_tiles)
     row_tiles = nodes_dev * col_count // TILE
     norm_scale = jnp.sqrt(KNN / degrees.astype(jnp.float32))[:, None]
     teleport = ALPHA * features.astype(jnp.float32)
@@ -305,10 +310,7 @@
     row_slots = (((piece_j % CORES) * Z_RING + (piece_j // CORES) % Z_RING) * n_y
                  + piece_j // (CORES * Z_RING)) * per_piece + row_ids_all % per_piece
     for repeat in range(STEPS):
-        col_panel = gathered.reshape(-1, TILE, feat_width)
-        pieces = block_product(
-            row_slots, col_ids_all, live_count, dev_tiles, col_panel, row_tiles, nodes_dev
-        )
+        pieces = block_product(row_slots, col_ids_all, dev_tiles, gathered, row_tiles)
         gathered = col_reduce_scatter(
             pieces.reshape(CORES, Z_RING, -1, nodes_dev, feat_width),
             scale9, scale, teleport, repeat == STEPS - 1,

time: 132 us -> 132 us (level)
  no operation moved by 1% of the time
where the time goes in v16:
time: 132 us
  Pallas kernels  114 us (86%)
  local copies, waits for them, and re-layouts  12.9 us (10%)
  other arithmetic  3.56 us (3%)
    pallas_call x2, Pallas kernels, col_reduce_scatter(): pl.pallas_call(functools.partial(reduce_scatter_kernel, n_z, chunks, last...  84.4 us
    pallas_call x2, Pallas kernels, block_product(): pl.pallas_call(functools.partial(block_product_kernel, group), out_shape=...  16.7 us
    pallas_call x1, Pallas kernels, row_all_gather(): pl.pallas_call(functools.partial(all_gather_kernel, n), out_shape=jax.Sha...  13.4 us
    reshape x1, local copies, waits for them, and re-layouts, shards(): dev_tiles = adj_tiles.reshape(tile_slots, TILE, TILE)  6.68 us
    unnamed x2, local copies, waits for them, and re-layouts  4.75 us

profile of v16, /device:TPU:8, one launch (start us, length us, event | category | flops | bytes accessed | tf_op | source)
XLA Modules:
  0.0 131.7 jit_solution(2661581749194284308)
XLA Ops:
  0.7 1.3 compare_select_fusion.2
  2.0 0.7 broadcast_multiply_fusion
  2.6 0.8 broadcast_in_dim.7.s9_ref
  3.4 0.8 mul.39.scale_ref
  4.2 1.6 %convert_multiply_fusion = (f32[256,128]{1,0:T(8,128)}, bf16[256,128]{1,0:T(8,128)(2,1)}) fusion(bf16[256,128]{1,0:T(8,128)(2,1)} %param.6, f32[256]{0:T(256)S(1)} %get-tuple-element.6), kind=kLoop, calls=%fused_computation | loop fusion | flops 131072 | bytes 263168 | tf_op jit(solution)/shard_map/mul | solution.py:302
  5.7 13.4 %shard_map.64.panel_ref = bf16[33,64,128]{2,1,0:T(8,128)(2,1)} custom-call(bf16[4,64,128]{2,1,0:T(8,128)(2,1)} %bitcast.11), custom_call_target="tpu_custom_call" | custom-call | tf_op jit(solution)/shard_map/pallas_call | solution.py:241
  19.1 3.3 %copy.7 = bf16[1,1,256,4096]{2,3,1,0:T(8,128)(2,1)S(1)} copy(bf16[1,1,256,4096]{3,2,1,0:T(8,128)(2,1)} %param.8) | data formatting | bytes 4194304 | tf_op args[2]
  22.4 6.7 %copy.9.adj_ref = bf16[256,64,64]{2,1,0:T(8,128)(2,1)} copy(bf16[256,64,64]{0,2,1:T(8,128)(2,1)S(1)} %bitcast.10) | data formatting | bytes 4194304 | tf_op jit(solution)/shard_map/reshape | solution.py:295
  29.1 8.3 %shard_map.65 = f32[128,64,128]{2,1,0:T(8,128)} custom-call(s32[256]{0:T(256)} %get-tuple-element.10.rows_ref, s32[256]{0:T(256)} %get-tuple-element.9.cols_ref, bf16[256,64,64]{2,1,0:T(8,128)(2,1)} %copy.9.adj_ref, bf16[33,64,128]{2,1,0:T(8,128)(2,1)} %shard_map.64.panel_ref), custom_call_target="tpu_custom_call" | custom-call | flops 268435456 | bytes 6291456 | tf_op jit(solution)/shard_map/pallas_call | solution.py:277
  37.4 48.5 %shard_map.66.panel_ref = bf16[33,64,128]{2,1,0:T(8,128)(2,1)} custom-call(f32[2,8,2,256,128]{4,3,2,1,0:T(8,128)} %bitcast.8, f32[256,128]{1,0:T(8,128)} %broadcast_in_dim.7.s9_ref, f32[256,128]{1,0:T(8,128)} %mul.39.scale_ref, f32[256,128]{1,0:T(8,128)} %get-tuple-element.7.tele_ref), custom_call_target="tpu_custom_call" | custom-call | tf_op jit(solution)/shard_map/pallas_call | solution.py:172
  86.0 8.4 %shard_map.67 = f32[128,64,128]{2,1,0:T(8,128)} custom-call(s32[256]{0:T(256)} %get-tuple-element.10.rows_ref, s32[256]{0:T(256)} %get-tuple-element.9.cols_ref, bf16[256,64,64]{2,1,0:T(8,128)(2,1)} %copy.9.adj_ref, bf16[33,64,128]{2,1,0:T(8,128)(2,1)} %shard_map.66.panel_ref), custom_call_target="tpu_custom_call" | custom-call | flops 268435456 | bytes 6291456 | tf_op jit(solution)/shard_map/pallas_call | solution.py:277
  94.3 35.9 %shard_map.68 = bf16[256,128]{1,0:T(8,128)(2,1)} custom-call(f32[2,8,2,256,128]{4,3,2,1,0:T(8,128)} %bitcast.9, f32[256,128]{1,0:T(8,128)} %broadcast_in_dim.7.s9_ref, f32[256,128]{1,0:T(8,128)} %mul.39.scale_ref, f32[256,128]{1,0:T(8,128)} %get-tuple-element.7.tele_ref), custom_call_target="tpu_custom_call" | custom-call | tf_op jit(solution)/shard_map/pallas_call | solution.py:172
  130.2 1.5 %copy.12 = bf16[256,128]{1,0:T(8,128)(2,1)} copy(bf16[256,128]{1,0:T(8,128)(2,1)} %shard_map.68) | data formatting | bytes 131072

commit v17 on v16

--- a/solution.py
+++ b/solution.py
@@ -191,7 +191,7 @@
     )(pieces, s9, scale, tele)
 
 
-def all_gather_kernel(n, src_ref, out_ref, send_sem, recv_sem):
+def all_gather_kernel(n, src_ref, adj_ref, out_ref, tiles_ref, send_sem, recv_sem):
     me = lax.axis_index("row")
     col = lax.axis_index("col")
     per_piece = src_ref.shape[0]
@@ -224,6 +224,15 @@
     out_ref[pl.ds(me * per_piece, per_piece)] = src_ref[...]
     out_ref[n * per_piece] = jnp.zeros(out_ref.shape[1:], out_ref.dtype)
 
+    rows = 16
+
+    def shape_tiles(g, carry):
+        at = pl.ds(pl.multiple_of(g * rows, rows), rows)
+        tiles_ref[at] = adj_ref[at].reshape((rows,) + tiles_ref.shape[1:])
+        return carry
+
+    lax.fori_loop(0, adj_ref.shape[0] // rows, shape_tiles, 0)
+
     def finish(k, carry):
         sender = lax.rem(me + n - k, n)
         copy(sender, sender).wait_recv()
@@ -233,19 +242,22 @@
     lax.fori_loop(1, n, finish, 0)
 
 
-def row_all_gather(source):
+def row_all_gather(source, adj_flat):
     n = lax.axis_size("row")
     nodes_dev, feat_width = source.shape
     per_piece = nodes_dev // TILE
     vmem = pl.BlockSpec(memory_space=pltpu.VMEM)
     return pl.pallas_call(
         functools.partial(all_gather_kernel, n),
-        out_shape=jax.ShapeDtypeStruct((n * per_piece + 1, TILE, feat_width), source.dtype),
-        in_specs=[vmem],
-        out_specs=vmem,
+        out_shape=(
+            jax.ShapeDtypeStruct((n * per_piece + 1, TILE, feat_width), source.dtype),
+            jax.ShapeDtypeStruct((adj_flat.shape[0], TILE, TILE), adj_flat.dtype),
+        ),
+        in_specs=[vmem, vmem],
+        out_specs=(vmem, vmem),
         scratch_shapes=[pltpu.SemaphoreType.DMA((n,)), pltpu.SemaphoreType.DMA((n,))],
         compiler_params=pltpu.CompilerParams(collective_id=1, has_side_effects=True),
-    )(source.reshape(per_piece, TILE, feat_width))
+    )(source.reshape(per_piece, TILE, feat_width), adj_flat)
 
 
 def block_product_kernel(group, rows_ref, cols_ref, adj_ref, panel_ref,
@@ -292,7 +304,6 @@
     nodes_dev = features.shape[0]
     feat_width = features.shape[1]
     tile_slots = adj_tiles.shape[2]
-    dev_tiles = adj_tiles.reshape(tile_slots, TILE, TILE)
     row_ids_all = tile_rows.reshape(tile_slots)
     live = jnp.arange(tile_slots, dtype=jnp.int32) < tile_counts.reshape(())
     panel_tiles = lax.axis_size("row") * (nodes_dev // TILE)
@@ -303,7 +314,7 @@
     scale9 = jnp.broadcast_to((1.0 - ALPHA) * norm_scale, features.shape)
     scale = jnp.broadcast_to(norm_scale, features.shape)
     source = (norm_scale * features.astype(jnp.float32)).astype(jnp.bfloat16)
-    gathered = row_all_gather(source)
+    gathered, dev_tiles = row_all_gather(source, adj_tiles.reshape(tile_slots, TILE * TILE))
     per_piece = nodes_dev // TILE
     n_y = col_count // (CORES * Z_RING)
     piece_j = row_ids_all // per_piece

time: 132 us -> 124 us (0.939)
  local copies, waits for them, and re-layouts: 12.9 us -> 2.99 us
  Pallas kernels: 114 us -> 117 us
    reshape x1 -> x0, local copies, waits for them, and re-layouts: 6.68 us -> none  [shards(): dev_tiles = adj_tiles.reshape(tile_slots, TILE, TILE)]
    unnamed x2 -> x1, local copies, waits for them, and re-layouts: 4.75 us -> 1.47 us
    pallas_call x1, Pallas kernels: 13.4 us -> 15.5 us  [row_all_gather(): pl.pallas_call(functools.partial(all_gather_kernel, n), out_shape=(jax.Sh...]
where the time goes in v17:
time: 124 us
  Pallas kernels  117 us (94%)
  other arithmetic  3.57 us (3%)
  local copies, waits for them, and re-layouts  2.99 us (2%)
    pallas_call x2, Pallas kernels, col_reduce_scatter(): pl.pallas_call(functools.partial(reduce_scatter_kernel, n_z, chunks, last...  84.6 us
    pallas_call x2, Pallas kernels, block_product(): pl.pallas_call(functools.partial(block_product_kernel, group), out_shape=...  16.7 us
    pallas_call x1, Pallas kernels, row_all_gather(): pl.pallas_call(functools.partial(all_gather_kernel, n), out_shape=(jax.Sh...  15.5 us

profile of v17, /device:TPU:8, one launch (start us, length us, event | category | flops | bytes accessed | tf_op | source)
XLA Modules:
  0.0 124.0 jit_solution(14903622338507860699)
XLA Ops:
  0.7 1.3 %compare_select_fusion.2 = (s32[256]{0:T(256)}, s32[256]{0:T(256)}) fusion(s32[256]{0:T(256)} %bitcast.12, s32[]{:T(128)} %bitcast.7, s32[256]{0:T(256)} %bitcast.13), kind=kLoop, calls=%fused_computation.5 | loop fusion | flops 17152 | bytes 4100 | tf_op jit(solution)/shard_map/jit(_where)/select_n | solution.py:310
  2.0 0.7 broadcast_multiply_fusion
  2.6 0.8 broadcast_in_dim.7.s9_ref
  3.4 0.8 mul.39.scale_ref
  4.2 1.6 %convert_multiply_fusion = (f32[256,128]{1,0:T(8,128)}, bf16[256,128]{1,0:T(8,128)(2,1)}) fusion(bf16[256,128]{1,0:T(8,128)(2,1)} %param.6, f32[256]{0:T(256)S(1)} %get-tuple-element.10), kind=kLoop, calls=%fused_computation | loop fusion | flops 131072 | bytes 263168 | tf_op jit(solution)/shard_map/mul | solution.py:313
  5.7 15.5 %shard_map.64 = (bf16[33,64,128]{2,1,0:T(8,128)(2,1)}, bf16[256,64,64]{2,1,0:T(8,128)(2,1)}) custom-call(bf16[4,64,128]{2,1,0:T(8,128)(2,1)} %bitcast.11, bf16[256,4096]{1,0:T(8,128)(2,1)} %bitcast.10), custom_call_target="tpu_custom_call" | custom-call | tf_op jit(solution)/shard_map/pallas_call | solution.py:250
  21.2 8.4 %shard_map.65 = f32[128,64,128]{2,1,0:T(8,128)} custom-call(s32[256]{0:T(256)} %get-tuple-element.14.rows_ref, s32[256]{0:T(256)} %get-tuple-element.13.cols_ref, bf16[256,64,64]{2,1,0:T(8,128)(2,1)} %get-tuple-element.7.adj_ref, bf16[33,64,128]{2,1,0:T(8,128)(2,1)} %get-tuple-element.8.panel_ref), custom_call_target="tpu_custom_call" | custom-call | flops 268435456 | bytes 6291456 | tf_op jit(solution)/shard_map/pallas_call | solution.py:289
  29.6 48.7 %shard_map.66.panel_ref = bf16[33,64,128]{2,1,0:T(8,128)(2,1)} custom-call(f32[2,8,2,256,128]{4,3,2,1,0:T(8,128)} %bitcast.8, f32[256,128]{1,0:T(8,128)} %broadcast_in_dim.7.s9_ref, f32[256,128]{1,0:T(8,128)} %mul.39.scale_ref, f32[256,128]{1,0:T(8,128)} %get-tuple-element.11.tele_ref), custom_call_target="tpu_custom_call" | custom-call | tf_op jit(solution)/shard_map/pallas_call | solution.py:172
  78.3 8.4 %shard_map.67 = f32[128,64,128]{2,1,0:T(8,128)} custom-call(s32[256]{0:T(256)} %get-tuple-element.14.rows_ref, s32[256]{0:T(256)} %get-tuple-element.13.cols_ref, bf16[256,64,64]{2,1,0:T(8,128)(2,1)} %get-tuple-element.7.adj_ref, bf16[33,64,128]{2,1,0:T(8,128)(2,1)} %shard_map.66.panel_ref), custom_call_target="tpu_custom_call" | custom-call | flops 268435456 | bytes 6291456 | tf_op jit(solution)/shard_map/pallas_call | solution.py:289
  86.7 35.9 %shard_map.68 = bf16[256,128]{1,0:T(8,128)(2,1)} custom-call(f32[2,8,2,256,128]{4,3,2,1,0:T(8,128)} %bitcast.9, f32[256,128]{1,0:T(8,128)} %broadcast_in_dim.7.s9_ref, f32[256,128]{1,0:T(8,128)} %mul.39.scale_ref, f32[256,128]{1,0:T(8,128)} %get-tuple-element.11.tele_ref), custom_call_target="tpu_custom_call" | custom-call | tf_op jit(solution)/shard_map/pallas_call | solution.py:172
  122.6 1.5 %copy.9 = bf16[256,128]{1,0:T(8,128)(2,1)} copy(bf16[256,128]{1,0:T(8,128)(2,1)} %shard_map.68) | data formatting | bytes 131072

commit v18 on v17

--- a/solution.py
+++ b/solution.py
@@ -171,7 +171,7 @@
     ag_sems = [] if last else [pltpu.SemaphoreType.DMA((n_row, chunks))] * 2
     return pl.pallas_call(
         functools.partial(reduce_scatter_kernel, n_z, chunks, last),
-        out_shape=jax.ShapeDtypeStruct(out_shape, jnp.bfloat16),
+        out_shape=jax.ShapeDtypeStruct(out_shape, jnp.float32 if last else jnp.bfloat16),
         in_specs=[vmem] * 4,
         out_specs=vmem,
         scratch_shapes=[
@@ -326,7 +326,7 @@
             pieces.reshape(CORES, Z_RING, -1, nodes_dev, feat_width),
             scale9, scale, teleport, repeat == STEPS - 1,
         )
-    return gathered
+    return gathered.astype(jnp.bfloat16)
 
 
 def solution(mesh):

time: 124 us -> 124 us (level)
  other arithmetic: 3.57 us -> 5.11 us
  local copies, waits for them, and re-layouts: 2.99 us -> 1.52 us
    convert_element_type x0 -> x1, other arithmetic: none -> 1.54 us  [shards(): return gathered.astype(jnp.bfloat16)]
    unnamed x1 -> x0, local copies, waits for them, and re-layouts: 1.47 us -> none
where the time goes in v18:
time: 124 us
  Pallas kernels  117 us (94%)
  other arithmetic  5.11 us (4%)
  local copies, waits for them, and re-layouts  1.52 us (1%)
    pallas_call x2, Pallas kernels, col_reduce_scatter(): pl.pallas_call(functools.partial(reduce_scatter_kernel, n_z, chunks, last...  84.6 us
    pallas_call x2, Pallas kernels, block_product(): pl.pallas_call(functools.partial(block_product_kernel, group), out_shape=...  16.7 us
    pallas_call x1, Pallas kernels, row_all_gather(): pl.pallas_call(functools.partial(all_gather_kernel, n), out_shape=(jax.Sh...  15.5 us

profile of v18, /device:TPU:8, one launch (start us, length us, event | category | flops | bytes accessed | tf_op | source)
XLA Modules:
  0.0 124.1 jit_solution(6592329310156498445)
XLA Ops:
  0.7 1.3 %compare_select_fusion.2 = (s32[256]{0:T(256)}, s32[256]{0:T(256)}) fusion(s32[256]{0:T(256)} %bitcast.12, s32[]{:T(128)} %bitcast.7, s32[256]{0:T(256)} %bitcast.13), kind=kLoop, calls=%fused_computation.5 | loop fusion | flops 17152 | bytes 4100 | tf_op jit(solution)/shard_map/jit(_where)/select_n | solution.py:310
  2.0 0.7 broadcast_multiply_fusion
  2.6 0.8 broadcast_in_dim.7.s9_ref
  3.4 0.8 mul.39.scale_ref
  4.2 1.6 %convert_multiply_fusion = (f32[256,128]{1,0:T(8,128)}, bf16[256,128]{1,0:T(8,128)(2,1)}) fusion(bf16[256,128]{1,0:T(8,128)(2,1)} %param.6, f32[256]{0:T(256)S(1)} %get-tuple-element.10), kind=kLoop, calls=%fused_computation | loop fusion | flops 131072 | bytes 263168 | tf_op jit(solution)/shard_map/mul | solution.py:313
  5.7 15.5 %shard_map.64 = (bf16[33,64,128]{2,1,0:T(8,128)(2,1)}, bf16[256,64,64]{2,1,0:T(8,128)(2,1)}) custom-call(bf16[4,64,128]{2,1,0:T(8,128)(2,1)} %bitcast.11, bf16[256,4096]{1,0:T(8,128)(2,1)} %bitcast.10), custom_call_target="tpu_custom_call" | custom-call | tf_op jit(solution)/shard_map/pallas_call | solution.py:250
  21.2 8.4 %shard_map.65 = f32[128,64,128]{2,1,0:T(8,128)} custom-call(s32[256]{0:T(256)} %get-tuple-element.14.rows_ref, s32[256]{0:T(256)} %get-tuple-element.13.cols_ref, bf16[256,64,64]{2,1,0:T(8,128)(2,1)} %get-tuple-element.7.adj_ref, bf16[33,64,128]{2,1,0:T(8,128)(2,1)} %get-tuple-element.8.panel_ref), custom_call_target="tpu_custom_call" | custom-call | flops 268435456 | bytes 6291456 | tf_op jit(solution)/shard_map/pallas_call | solution.py:289
  29.6 48.5 %shard_map.66.panel_ref = bf16[33,64,128]{2,1,0:T(8,128)(2,1)} custom-call(f32[2,8,2,256,128]{4,3,2,1,0:T(8,128)} %bitcast.9, f32[256,128]{1,0:T(8,128)} %broadcast_in_dim.7.s9_ref, f32[256,128]{1,0:T(8,128)} %mul.39.scale_ref, f32[256,128]{1,0:T(8,128)} %get-tuple-element.11.tele_ref), custom_call_target="tpu_custom_call" | custom-call | tf_op jit(solution)/shard_map/pallas_call | solution.py:172
  78.1 8.4 %shard_map.67 = f32[128,64,128]{2,1,0:T(8,128)} custom-call(s32[256]{0:T(256)} %get-tuple-element.14.rows_ref, s32[256]{0:T(256)} %get-tuple-element.13.cols_ref, bf16[256,64,64]{2,1,0:T(8,128)(2,1)} %get-tuple-element.7.adj_ref, bf16[33,64,128]{2,1,0:T(8,128)(2,1)} %shard_map.66.panel_ref), custom_call_target="tpu_custom_call" | custom-call | flops 268435456 | bytes 6291456 | tf_op jit(solution)/shard_map/pallas_call | solution.py:289
  86.5 36.1 %shard_map.68 = f32[256,128]{1,0:T(8,128)} custom-call(f32[2,8,2,256,128]{4,3,2,1,0:T(8,128)} %bitcast.8, f32[256,128]{1,0:T(8,128)} %broadcast_in_dim.7.s9_ref, f32[256,128]{1,0:T(8,128)} %mul.39.scale_ref, f32[256,128]{1,0:T(8,128)} %get-tuple-element.11.tele_ref), custom_call_target="tpu_custom_call" | custom-call | tf_op jit(solution)/shard_map/pallas_call | solution.py:172
  122.5 1.5 %convert_element_type.16 = bf16[256,128]{1,0:T(8,128)(2,1)} convert(f32[256,128]{1,0:T(8,128)} %shard_map.68) | non-fusion elementwise | flops 32768 | bytes 196608 | tf_op jit(solution)/shard_map/convert_element_type | solution.py:329

commit v19 on v18

--- a/solution.py
+++ b/solution.py
@@ -20,7 +20,7 @@
 Z_RING = 8
 
 
-def reduce_scatter_kernel(n_z, chunks, last, x_ref, s9_ref, scale_ref, tele_ref, out_ref, ra,
+def reduce_scatter_kernel(n_z, chunks, last, x_ref, scale_ref, feat_ref, out_ref, ra,
                           recv_cw, recv_ccw, send_cw, send_ccw, fin, y_recv,
                           a_sems, cw_sems, ccw_sems, y_sems, *ag_sems):
     c = lax.axis_index("col")
@@ -133,7 +133,7 @@
         part = pl.ds(i * size, size)
         y_copy(i).wait_recv()
         own = fin[yh, part] + y_recv[part]
-        current = s9_ref[part] * own + tele_ref[part]
+        current = ((1.0 - ALPHA) * scale_ref[part]) * own + ALPHA * feat_ref[part].astype(jnp.float32)
         if last:
             out_ref[part] = current.astype(out_ref.dtype)
         else:
@@ -161,7 +161,7 @@
 RS_CHUNKS = 4
 
 
-def col_reduce_scatter(pieces, s9, scale, tele, last):
+def col_reduce_scatter(pieces, scale, features, last):
     cores, n_z, n_y, nodes_dev, feat_width = pieces.shape
     n_row = lax.axis_size("row")
     chunks = nodes_dev // TILE
@@ -172,7 +172,7 @@
     return pl.pallas_call(
         functools.partial(reduce_scatter_kernel, n_z, chunks, last),
         out_shape=jax.ShapeDtypeStruct(out_shape, jnp.float32 if last else jnp.bfloat16),
-        in_specs=[vmem] * 4,
+        in_specs=[vmem] * 3,
         out_specs=vmem,
         scratch_shapes=[
             pltpu.VMEM((n_z, n_y) + piece, jnp.float32),
@@ -188,13 +188,15 @@
             pltpu.SemaphoreType.DMA((2, chunks)),
         ] + ag_sems,
         compiler_params=pltpu.CompilerParams(collective_id=2 if last else 0, has_side_effects=True),
-    )(pieces, s9, scale, tele)
-
-
-def all_gather_kernel(n, src_ref, adj_ref, out_ref, tiles_ref, send_sem, recv_sem):
+    )(pieces, scale, features)
+
+
+def all_gather_kernel(n, feat_ref, scale_ref, adj_ref, out_ref, tiles_ref, src_ref, send_sem,
+                      recv_sem):
     me = lax.axis_index("row")
     col = lax.axis_index("col")
     per_piece = src_ref.shape[0]
+    src_ref[...] = (scale_ref[...] * feat_ref[...].astype(jnp.float32)).astype(src_ref.dtype)
 
     barrier = pltpu.get_barrier_semaphore()
 
@@ -242,22 +244,27 @@
     lax.fori_loop(1, n, finish, 0)
 
 
-def row_all_gather(source, adj_flat):
+def row_all_gather(features, scale, adj_flat):
     n = lax.axis_size("row")
-    nodes_dev, feat_width = source.shape
+    nodes_dev, feat_width = features.shape
     per_piece = nodes_dev // TILE
     vmem = pl.BlockSpec(memory_space=pltpu.VMEM)
     return pl.pallas_call(
         functools.partial(all_gather_kernel, n),
         out_shape=(
-            jax.ShapeDtypeStruct((n * per_piece + 1, TILE, feat_width), source.dtype),
+            jax.ShapeDtypeStruct((n * per_piece + 1, TILE, feat_width), jnp.bfloat16),
             jax.ShapeDtypeStruct((adj_flat.shape[0], TILE, TILE), adj_flat.dtype),
         ),
-        in_specs=[vmem, vmem],
+        in_specs=[vmem, vmem, vmem],
         out_specs=(vmem, vmem),
-        scratch_shapes=[pltpu.SemaphoreType.DMA((n,)), pltpu.SemaphoreType.DMA((n,))],
+        scratch_shapes=[
+            pltpu.VMEM((per_piece, TILE, feat_width), jnp.bfloat16),
+            pltpu.SemaphoreType.DMA((n,)),
+            pltpu.SemaphoreType.DMA((n,)),
+        ],
         compiler_params=pltpu.CompilerParams(collective_id=1, has_side_effects=True),
-    )(source.reshape(per_piece, TILE, feat_width), adj_flat)
+    )(features.reshape(per_piece, TILE, feat_width), scale.reshape(per_piece, TILE, feat_width),
+      adj_flat)
 
 
 def block_product_kernel(group, rows_ref, cols_ref, adj_ref, panel_ref,
@@ -310,11 +317,8 @@
     col_ids_all = jnp.where(live, tile_cols.reshape(tile_slots), panel_tiles)
     row_tiles = nodes_dev * col_count // TILE
     norm_scale = jnp.sqrt(KNN / degrees.astype(jnp.float32))[:, None]
-    teleport = ALPHA * features.astype(jnp.float32)
-    scale9 = jnp.broadcast_to((1.0 - ALPHA) * norm_scale, features.shape)
     scale = jnp.broadcast_to(norm_scale, features.shape)
-    source = (norm_scale * features.astype(jnp.float32)).astype(jnp.bfloat16)
-    gathered, dev_tiles = row_all_gather(source, adj_tiles.reshape(tile_slots, TILE * TILE))
+    gathered, dev_tiles = row_all_gather(features, scale, adj_tiles.reshape(tile_slots, TILE * TILE))
     per_piece = nodes_dev // TILE
     n_y = col_count // (CORES * Z_RING)
     piece_j = row_ids_all // per_piece
@@ -324,7 +328,7 @@
         pieces = block_product(row_slots, col_ids_all, dev_tiles, gathered, row_tiles)
         gathered = col_reduce_scatter(
             pieces.reshape(CORES, Z_RING, -1, nodes_dev, feat_width),
-            scale9, scale, teleport, repeat == STEPS - 1,
+            scale, features, repeat == STEPS - 1,
         )
     return gathered.astype(jnp.bfloat16)
 

time: 124 us -> 122 us (0.984)
  other arithmetic: 5.11 us -> 3.54 us
    mul x2 -> x0, other arithmetic: 2.26 us -> none  [the longest x1 1.57 us: shards(): teleport = ALPHA * features.astype(jnp.float32)]
where the time goes in v19:
time: 122 us
  Pallas kernels  116 us (95%)
  other arithmetic  3.54 us (3%)
  local copies, waits for them, and re-layouts  1.57 us (1%)
    pallas_call x2, Pallas kernels, col_reduce_scatter(): pl.pallas_call(functools.partial(reduce_scatter_kernel, n_z, chunks, last...  84 us
    pallas_call x2, Pallas kernels, block_product(): pl.pallas_call(functools.partial(block_product_kernel, group), out_shape=...  16.8 us
    pallas_call x1, Pallas kernels, row_all_gather(): pl.pallas_call(functools.partial(all_gather_kernel, n), out_shape=(jax.Sh...  15.6 us

profile of v19, /device:TPU:8, one launch (start us, length us, event | category | flops | bytes accessed | tf_op | source)
XLA Modules:
  0.0 122.1 jit_solution(14344999863088806643)
XLA Ops:
  0.7 0.7 divide_sqrt_fusion
  1.3 1.3 %compare_select_fusion.2 = (s32[256]{0:T(256)}, s32[256]{0:T(256)}) fusion(s32[256]{0:T(256)} %bitcast.12, s32[]{:T(128)} %bitcast.7, s32[256]{0:T(256)} %bitcast.13), kind=kLoop, calls=%fused_computation.2 | loop fusion | flops 17152 | bytes 4100 | tf_op jit(solution)/shard_map/jit(_where)/select_n | solution.py:317
  2.6 0.1 broadcast_in_dim.15
  2.7 0.7 broadcast_in_dim.16.scale_ref
  3.5 0.7 broadcast_in_dim.17.scale_ref
  4.2 15.6 %shard_map.64 = (bf16[33,64,128]{2,1,0:T(8,128)(2,1)}, bf16[256,64,64]{2,1,0:T(8,128)(2,1)}) custom-call(bf16[4,64,128]{2,1,0:T(8,128)(2,1)} %bitcast.11, f32[4,64,128]{2,1,0:T(8,128)} %broadcast_in_dim.16.scale_ref, bf16[256,4096]{1,0:T(8,128)(2,1)} %bitcast.10), custom_call_target="tpu_custom_call" | custom-call | tf_op jit(solution)/shard_map/pallas_call | solution.py:252
  19.8 8.4 %shard_map.65 = f32[128,64,128]{2,1,0:T(8,128)} custom-call(s32[256]{0:T(256)} %get-tuple-element.10.rows_ref, s32[256]{0:T(256)} %get-tuple-element.9.cols_ref, bf16[256,64,64]{2,1,0:T(8,128)(2,1)} %get-tuple-element.7.adj_ref, bf16[33,64,128]{2,1,0:T(8,128)(2,1)} %get-tuple-element.8.panel_ref), custom_call_target="tpu_custom_call" | custom-call | flops 268435456 | bytes 6291456 | tf_op jit(solution)/shard_map/pallas_call | solution.py:296
  28.2 48.7 %shard_map.66.panel_ref = bf16[33,64,128]{2,1,0:T(8,128)(2,1)} custom-call(f32[2,8,2,256,128]{4,3,2,1,0:T(8,128)} %bitcast.8, f32[256,128]{1,0:T(8,128)} %broadcast_in_dim.17.scale_ref, bf16[256,128]{1,0:T(8,128)(2,1)} %feat_ref.3), custom_call_target="tpu_custom_call" | custom-call | tf_op jit(solution)/shard_map/pallas_call | solution.py:172
  76.9 8.4 %shard_map.67 = f32[128,64,128]{2,1,0:T(8,128)} custom-call(s32[256]{0:T(256)} %get-tuple-element.10.rows_ref, s32[256]{0:T(256)} %get-tuple-element.9.cols_ref, bf16[256,64,64]{2,1,0:T(8,128)(2,1)} %get-tuple-element.7.adj_ref, bf16[33,64,128]{2,1,0:T(8,128)(2,1)} %shard_map.66.panel_ref), custom_call_target="tpu_custom_call" | custom-call | flops 268435456 | bytes 6291456 | tf_op jit(solution)/shard_map/pallas_call | solution.py:296
  85.3 35.3 %shard_map.68 = f32[256,128]{1,0:T(8,128)} custom-call(f32[2,8,2,256,128]{4,3,2,1,0:T(8,128)} %bitcast.9, f32[256,128]{1,0:T(8,128)} %broadcast_in_dim.17.scale_ref, bf16[256,128]{1,0:T(8,128)(2,1)} %feat_ref.3), custom_call_target="tpu_custom_call" | custom-call | tf_op jit(solution)/shard_map/pallas_call | solution.py:172
  120.6 1.5 %convert_element_type.7 = bf16[256,128]{1,0:T(8,128)(2,1)} convert(f32[256,128]{1,0:T(8,128)} %shard_map.68) | non-fusion elementwise | flops 32768 | bytes 196608 | tf_op jit(solution)/shard_map/convert_element_type | solution.py:333

commit v20 on v19

--- a/solution.py
+++ b/solution.py
@@ -133,11 +133,11 @@
         part = pl.ds(i * size, size)
         y_copy(i).wait_recv()
         own = fin[yh, part] + y_recv[part]
-        current = ((1.0 - ALPHA) * scale_ref[part]) * own + ALPHA * feat_ref[part].astype(jnp.float32)
+        current = ((1.0 - ALPHA) * scale_ref[i]) * own + ALPHA * feat_ref[i].astype(jnp.float32)
         if last:
             out_ref[part] = current.astype(out_ref.dtype)
         else:
-            out_ref[row * chunks + i] = (scale_ref[part] * current).astype(out_ref.dtype)
+            out_ref[row * chunks + i] = (scale_ref[i] * current).astype(out_ref.dtype)
 
             def ag_start(k, carry, i=i):
                 ag_copy(lax.rem(row + k, n_row), row, i).start()
@@ -246,7 +246,7 @@
 
 def row_all_gather(features, scale, adj_flat):
     n = lax.axis_size("row")
-    nodes_dev, feat_width = features.shape
+    nodes_dev, feat_width = features.shape[0] * TILE, features.shape[2]
     per_piece = nodes_dev // TILE
     vmem = pl.BlockSpec(memory_space=pltpu.VMEM)
     return pl.pallas_call(
@@ -263,8 +263,7 @@
             pltpu.SemaphoreType.DMA((n,)),
         ],
         compiler_params=pltpu.CompilerParams(collective_id=1, has_side_effects=True),
-    )(features.reshape(per_piece, TILE, feat_width), scale.reshape(per_piece, TILE, feat_width),
-      adj_flat)
+    )(features, scale, adj_flat)
 
 
 def block_product_kernel(group, rows_ref, cols_ref, adj_ref, panel_ref,
@@ -317,7 +316,8 @@
     col_ids_all = jnp.where(live, tile_cols.reshape(tile_slots), panel_tiles)
     row_tiles = nodes_dev * col_count // TILE
     norm_scale = jnp.sqrt(KNN / degrees.astype(jnp.float32))[:, None]
-    scale = jnp.broadcast_to(norm_scale, features.shape)
+    scale = jnp.broadcast_to(norm_scale, features.shape).reshape(-1, TILE, feat_width)
+    features = features.reshape(-1, TILE, feat_width)
     gathered, dev_tiles = row_all_gather(features, scale, adj_tiles.reshape(tile_slots, TILE * TILE))
     per_piece = nodes_dev // TILE
     n_y = col_count // (CORES * Z_RING)

time: 122 us -> 122 us (level)
  no operation moved by 1% of the time
where the time goes in v20:
time: 122 us; the launch traced here: 121 us
  Pallas kernels  116 us (95%)
  other arithmetic  3.54 us (3%)
    pallas_call x2, Pallas kernels, col_reduce_scatter(): pl.pallas_call(functools.partial(reduce_scatter_kernel, n_z, chunks, last...  84.1 us
    pallas_call x2, Pallas kernels, block_product(): pl.pallas_call(functools.partial(block_product_kernel, group), out_shape=...  16.8 us
    pallas_call x1, Pallas kernels, row_all_gather(): pl.pallas_call(functools.partial(all_gather_kernel, n), out_shape=(jax.Sh...  15.6 us

profile of v20, /device:TPU:8, one launch (start us, length us, event | category | flops | bytes accessed | tf_op | source)
XLA Modules:
  0.0 121.4 jit_solution(9834966702572480508)
XLA Ops:
  0.7 0.7 divide_sqrt_fusion
  1.3 0.1 broadcast_in_dim.13
  1.4 1.3 %compare_select_fusion.2 = (s32[256]{0:T(256)}, s32[256]{0:T(256)}) fusion(s32[256]{0:T(256)} %bitcast.14, s32[]{:T(128)} %bitcast.7, s32[256]{0:T(256)} %bitcast.15), kind=kLoop, calls=%fused_computation.2 | loop fusion | flops 17152 | bytes 4100 | tf_op jit(solution)/shard_map/jit(_where)/select_n | solution.py:316
  2.7 0.7 broadcast_in_dim.14.scale_ref
  3.5 15.6 %shard_map.64 = (bf16[33,64,128]{2,1,0:T(8,128)(2,1)}, bf16[256,64,64]{2,1,0:T(8,128)(2,1)}) custom-call(bf16[4,64,128]{2,1,0:T(8,128)(2,1)} %bitcast.11, f32[4,64,128]{2,1,0:T(8,128)} %broadcast_in_dim.14.scale_ref, bf16[256,4096]{1,0:T(8,128)(2,1)} %bitcast.10), custom_call_target="tpu_custom_call" | custom-call | tf_op jit(solution)/shard_map/pallas_call | solution.py:252
  19.0 8.4 %shard_map.65 = f32[128,64,128]{2,1,0:T(8,128)} custom-call(s32[256]{0:T(256)} %get-tuple-element.10.rows_ref, s32[256]{0:T(256)} %get-tuple-element.9.cols_ref, bf16[256,64,64]{2,1,0:T(8,128)(2,1)} %get-tuple-element.7.adj_ref, bf16[33,64,128]{2,1,0:T(8,128)(2,1)} %get-tuple-element.8.panel_ref), custom_call_target="tpu_custom_call" | custom-call | flops 268435456 | bytes 6291456 | tf_op jit(solution)/shard_map/pallas_call | solution.py:295
  27.4 48.5 %shard_map.66.panel_ref = bf16[33,64,128]{2,1,0:T(8,128)(2,1)} custom-call(f32[2,8,2,256,128]{4,3,2,1,0:T(8,128)} %bitcast.8, f32[4,64,128]{2,1,0:T(8,128)} %broadcast_in_dim.14.scale_ref, bf16[4,64,128]{2,1,0:T(8,128)(2,1)} %bitcast.12), custom_call_target="tpu_custom_call" | custom-call | tf_op jit(solution)/shard_map/pallas_call | solution.py:172
  76.0 8.4 %shard_map.67 = f32[128,64,128]{2,1,0:T(8,128)} custom-call(s32[256]{0:T(256)} %get-tuple-element.10.rows_ref, s32[256]{0:T(256)} %get-tuple-element.9.cols_ref, bf16[256,64,64]{2,1,0:T(8,128)(2,1)} %get-tuple-element.7.adj_ref, bf16[33,64,128]{2,1,0:T(8,128)(2,1)} %shard_map.66.panel_ref), custom_call_target="tpu_custom_call" | custom-call | flops 268435456 | bytes 6291456 | tf_op jit(solution)/shard_map/pallas_call | solution.py:295
  84.3 35.5 %shard_map.68 = f32[256,128]{1,0:T(8,128)} custom-call(f32[2,8,2,256,128]{4,3,2,1,0:T(8,128)} %bitcast.9, f32[4,64,128]{2,1,0:T(8,128)} %broadcast_in_dim.14.scale_ref, bf16[4,64,128]{2,1,0:T(8,128)(2,1)} %bitcast.13), custom_call_target="tpu_custom_call" | custom-call | tf_op jit(solution)/shard_map/pallas_call | solution.py:172
  119.9 1.5 %convert_element_type.7 = bf16[256,128]{1,0:T(8,128)(2,1)} convert(f32[256,128]{1,0:T(8,128)} %shard_map.68) | non-fusion elementwise | flops 32768 | bytes 196608 | tf_op jit(solution)/shard_map/convert_element_type | solution.py:333

commit v21 on v20

--- a/solution.py
+++ b/solution.py
@@ -226,7 +226,7 @@
     out_ref[pl.ds(me * per_piece, per_piece)] = src_ref[...]
     out_ref[n * per_piece] = jnp.zeros(out_ref.shape[1:], out_ref.dtype)
 
-    rows = 16
+    rows = 32
 
     def shape_tiles(g, carry):
         at = pl.ds(pl.multiple_of(g * rows, rows), rows)

time: 122 us -> 121 us (level)
  no operation moved by 1% of the time
where the time goes in v21:
time: 121 us
  Pallas kernels  116 us (96%)
  other arithmetic  3.54 us (3%)
    pallas_call x2, Pallas kernels, col_reduce_scatter(): pl.pallas_call(functools.partial(reduce_scatter_kernel, n_z, chunks, last...  84 us
    pallas_call x2, Pallas kernels, block_product(): pl.pallas_call(functools.partial(block_product_kernel, group), out_shape=...  16.8 us
    pallas_call x1, Pallas kernels, row_all_gather(): pl.pallas_call(functools.partial(all_gather_kernel, n), out_shape=(jax.Sh...  15.6 us

profile of v21, /device:TPU:8, one launch (start us, length us, event | category | flops | bytes accessed | tf_op | source)
XLA Modules:
  0.0 121.3 jit_solution(6687280094292642085)
XLA Ops:
  0.7 0.7 divide_sqrt_fusion
  1.3 0.1 broadcast_in_dim.13
  1.4 1.3 %compare_select_fusion.2 = (s32[256]{0:T(256)}, s32[256]{0:T(256)}) fusion(s32[256]{0:T(256)} %bitcast.14, s32[]{:T(128)} %bitcast.7, s32[256]{0:T(256)} %bitcast.15), kind=kLoop, calls=%fused_computation.2 | loop fusion | flops 17152 | bytes 4100 | tf_op jit(solution)/shard_map/jit(_where)/select_n | solution.py:316
  2.7 0.7 broadcast_in_dim.14.scale_ref
  3.5 15.6 %shard_map.64 = (bf16[33,64,128]{2,1,0:T(8,128)(2,1)}, bf16[256,64,64]{2,1,0:T(8,128)(2,1)}) custom-call(bf16[4,64,128]{2,1,0:T(8,128)(2,1)} %bitcast.11, f32[4,64,128]{2,1,0:T(8,128)} %broadcast_in_dim.14.scale_ref, bf16[256,4096]{1,0:T(8,128)(2,1)} %bitcast.10), custom_call_target="tpu_custom_call" | custom-call | tf_op jit(solution)/shard_map/pallas_call | solution.py:252
  19.0 8.4 %shard_map.65 = f32[128,64,128]{2,1,0:T(8,128)} custom-call(s32[256]{0:T(256)} %get-tuple-element.10.rows_ref, s32[256]{0:T(256)} %get-tuple-element.9.cols_ref, bf16[256,64,64]{2,1,0:T(8,128)(2,1)} %get-tuple-element.7.adj_ref, bf16[33,64,128]{2,1,0:T(8,128)(2,1)} %get-tuple-element.8.panel_ref), custom_call_target="tpu_custom_call" | custom-call | flops 268435456 | bytes 6291456 | tf_op jit(solution)/shard_map/pallas_call | solution.py:295
  27.4 48.5 %shard_map.66.panel_ref = bf16[33,64,128]{2,1,0:T(8,128)(2,1)} custom-call(f32[2,8,2,256,128]{4,3,2,1,0:T(8,128)} %bitcast.8, f32[4,64,128]{2,1,0:T(8,128)} %broadcast_in_dim.14.scale_ref, bf16[4,64,128]{2,1,0:T(8,128)(2,1)} %bitcast.12), custom_call_target="tpu_custom_call" | custom-call | tf_op jit(solution)/shard_map/pallas_call | solution.py:172
  75.9 8.4 %shard_map.67 = f32[128,64,128]{2,1,0:T(8,128)} custom-call(s32[256]{0:T(256)} %get-tuple-element.10.rows_ref, s32[256]{0:T(256)} %get-tuple-element.9.cols_ref, bf16[256,64,64]{2,1,0:T(8,128)(2,1)} %get-tuple-element.7.adj_ref, bf16[33,64,128]{2,1,0:T(8,128)(2,1)} %shard_map.66.panel_ref), custom_call_target="tpu_custom_call" | custom-call | flops 268435456 | bytes 6291456 | tf_op jit(solution)/shard_map/pallas_call | solution.py:295
  84.3 35.5 %shard_map.68 = f32[256,128]{1,0:T(8,128)} custom-call(f32[2,8,2,256,128]{4,3,2,1,0:T(8,128)} %bitcast.9, f32[4,64,128]{2,1,0:T(8,128)} %broadcast_in_dim.14.scale_ref, bf16[4,64,128]{2,1,0:T(8,128)(2,1)} %bitcast.13), custom_call_target="tpu_custom_call" | custom-call | tf_op jit(solution)/shard_map/pallas_call | solution.py:172
  119.8 1.5 %convert_element_type.7 = bf16[256,128]{1,0:T(8,128)(2,1)} convert(f32[256,128]{1,0:T(8,128)} %shard_map.68) | non-fusion elementwise | flops 32768 | bytes 196608 | tf_op jit(solution)/shard_map/convert_element_type | solution.py:333

commit v22 on v21

--- a/solution.py
+++ b/solution.py
@@ -226,7 +226,7 @@
     out_ref[pl.ds(me * per_piece, per_piece)] = src_ref[...]
     out_ref[n * per_piece] = jnp.zeros(out_ref.shape[1:], out_ref.dtype)
 
-    rows = 32
+    rows = 64
 
     def shape_tiles(g, carry):
         at = pl.ds(pl.multiple_of(g * rows, rows), rows)

time: 121 us -> 122 us (level)
  no operation moved by 1% of the time
where the time goes in v22:
time: 122 us; the launch traced here: 121 us
  Pallas kernels  116 us (95%)
  other arithmetic  3.54 us (3%)
    pallas_call x2, Pallas kernels, col_reduce_scatter(): pl.pallas_call(functools.partial(reduce_scatter_kernel, n_z, chunks, last...  84 us
    pallas_call x2, Pallas kernels, block_product(): pl.pallas_call(functools.partial(block_product_kernel, group), out_shape=...  16.8 us
    pallas_call x1, Pallas kernels, row_all_gather(): pl.pallas_call(functools.partial(all_gather_kernel, n), out_shape=(jax.Sh...  15.6 us

profile of v22, /device:TPU:8, one launch (start us, length us, event | category | flops | bytes accessed | tf_op | source)
XLA Modules:
  0.0 121.4 jit_solution(15314883808046905015)
XLA Ops:
  0.7 0.7 divide_sqrt_fusion
  1.3 0.1 broadcast_in_dim.13
  1.4 1.3 %compare_select_fusion.2 = (s32[256]{0:T(256)}, s32[256]{0:T(256)}) fusion(s32[256]{0:T(256)} %bitcast.14, s32[]{:T(128)} %bitcast.7, s32[256]{0:T(256)} %bitcast.15), kind=kLoop, calls=%fused_computation.2 | loop fusion | flops 17152 | bytes 4100 | tf_op jit(solution)/shard_map/jit(_where)/select_n | solution.py:316
  2.7 0.7 broadcast_in_dim.14.scale_ref
  3.5 15.6 %shard_map.64 = (bf16[33,64,128]{2,1,0:T(8,128)(2,1)}, bf16[256,64,64]{2,1,0:T(8,128)(2,1)}) custom-call(bf16[4,64,128]{2,1,0:T(8,128)(2,1)} %bitcast.11, f32[4,64,128]{2,1,0:T(8,128)} %broadcast_in_dim.14.scale_ref, bf16[256,4096]{1,0:T(8,128)(2,1)} %bitcast.10), custom_call_target="tpu_custom_call" | custom-call | tf_op jit(solution)/shard_map/pallas_call | solution.py:252
  19.0 8.4 %shard_map.65 = f32[128,64,128]{2,1,0:T(8,128)} custom-call(s32[256]{0:T(256)} %get-tuple-element.10.rows_ref, s32[256]{0:T(256)} %get-tuple-element.9.cols_ref, bf16[256,64,64]{2,1,0:T(8,128)(2,1)} %get-tuple-element.7.adj_ref, bf16[33,64,128]{2,1,0:T(8,128)(2,1)} %get-tuple-element.8.panel_ref), custom_call_target="tpu_custom_call" | custom-call | flops 268435456 | bytes 6291456 | tf_op jit(solution)/shard_map/pallas_call | solution.py:295
  27.4 48.6 %shard_map.66.panel_ref = bf16[33,64,128]{2,1,0:T(8,128)(2,1)} custom-call(f32[2,8,2,256,128]{4,3,2,1,0:T(8,128)} %bitcast.8, f32[4,64,128]{2,1,0:T(8,128)} %broadcast_in_dim.14.scale_ref, bf16[4,64,128]{2,1,0:T(8,128)(2,1)} %bitcast.12), custom_call_target="tpu_custom_call" | custom-call | tf_op jit(solution)/shard_map/pallas_call | solution.py:172
  76.0 8.4 %shard_map.67 = f32[128,64,128]{2,1,0:T(8,128)} custom-call(s32[256]{0:T(256)} %get-tuple-element.10.rows_ref, s32[256]{0:T(256)} %get-tuple-element.9.cols_ref, bf16[256,64,64]{2,1,0:T(8,128)(2,1)} %get-tuple-element.7.adj_ref, bf16[33,64,128]{2,1,0:T(8,128)(2,1)} %shard_map.66.panel_ref), custom_call_target="tpu_custom_call" | custom-call | flops 268435456 | bytes 6291456 | tf_op jit(solution)/shard_map/pallas_call | solution.py:295
  84.4 35.5 %shard_map.68 = f32[256,128]{1,0:T(8,128)} custom-call(f32[2,8,2,256,128]{4,3,2,1,0:T(8,128)} %bitcast.9, f32[4,64,128]{2,1,0:T(8,128)} %broadcast_in_dim.14.scale_ref, bf16[4,64,128]{2,1,0:T(8,128)(2,1)} %bitcast.13), custom_call_target="tpu_custom_call" | custom-call | tf_op jit(solution)/shard_map/pallas_call | solution.py:172
  119.9 1.5 %convert_element_type.7 = bf16[256,128]{1,0:T(8,128)(2,1)} convert(f32[256,128]{1,0:T(8,128)} %shard_map.68) | non-fusion elementwise | flops 32768 | bytes 196608 | tf_op jit(solution)/shard_map/convert_element_type | solution.py:333

commit v23 on v22

--- a/solution.py
+++ b/solution.py
@@ -226,7 +226,7 @@
     out_ref[pl.ds(me * per_piece, per_piece)] = src_ref[...]
     out_ref[n * per_piece] = jnp.zeros(out_ref.shape[1:], out_ref.dtype)
 
-    rows = 64
+    rows = 128
 
     def shape_tiles(g, carry):
         at = pl.ds(pl.multiple_of(g * rows, rows), rows)

time: 122 us -> 121 us (level)
  no operation moved by 1% of the time
where the time goes in v23:
time: 121 us
  Pallas kernels  116 us (96%)
  other arithmetic  3.54 us (3%)
    pallas_call x2, Pallas kernels, col_reduce_scatter(): pl.pallas_call(functools.partial(reduce_scatter_kernel, n_z, chunks, last...  84 us
    pallas_call x2, Pallas kernels, block_product(): pl.pallas_call(functools.partial(block_product_kernel, group), out_shape=...  16.8 us
    pallas_call x1, Pallas kernels, row_all_gather(): pl.pallas_call(functools.partial(all_gather_kernel, n), out_shape=(jax.Sh...  15.6 us

profile of v23, /device:TPU:8, one launch (start us, length us, event | category | flops | bytes accessed | tf_op | source)
XLA Modules:
  0.0 121.4 jit_solution(7689702809034308322)
XLA Ops:
  0.7 0.7 divide_sqrt_fusion
  1.3 0.1 broadcast_in_dim.13
  1.4 1.3 %compare_select_fusion.2 = (s32[256]{0:T(256)}, s32[256]{0:T(256)}) fusion(s32[256]{0:T(256)} %bitcast.14, s32[]{:T(128)} %bitcast.7, s32[256]{0:T(256)} %bitcast.15), kind=kLoop, calls=%fused_computation.2 | loop fusion | flops 17152 | bytes 4100 | tf_op jit(solution)/shard_map/jit(_where)/select_n | solution.py:316
  2.7 0.7 broadcast_in_dim.14.scale_ref
  3.5 15.6 %shard_map.64 = (bf16[33,64,128]{2,1,0:T(8,128)(2,1)}, bf16[256,64,64]{2,1,0:T(8,128)(2,1)}) custom-call(bf16[4,64,128]{2,1,0:T(8,128)(2,1)} %bitcast.11, f32[4,64,128]{2,1,0:T(8,128)} %broadcast_in_dim.14.scale_ref, bf16[256,4096]{1,0:T(8,128)(2,1)} %bitcast.10), custom_call_target="tpu_custom_call" | custom-call | tf_op jit(solution)/shard_map/pallas_call | solution.py:252
  19.0 8.4 %shard_map.65 = f32[128,64,128]{2,1,0:T(8,128)} custom-call(s32[256]{0:T(256)} %get-tuple-element.10.rows_ref, s32[256]{0:T(256)} %get-tuple-element.9.cols_ref, bf16[256,64,64]{2,1,0:T(8,128)(2,1)} %get-tuple-element.7.adj_ref, bf16[33,64,128]{2,1,0:T(8,128)(2,1)} %get-tuple-element.8.panel_ref), custom_call_target="tpu_custom_call" | custom-call | flops 268435456 | bytes 6291456 | tf_op jit(solution)/shard_map/pallas_call | solution.py:295
  27.4 48.3 %shard_map.66.panel_ref = bf16[33,64,128]{2,1,0:T(8,128)(2,1)} custom-call(f32[2,8,2,256,128]{4,3,2,1,0:T(8,128)} %bitcast.8, f32[4,64,128]{2,1,0:T(8,128)} %broadcast_in_dim.14.scale_ref, bf16[4,64,128]{2,1,0:T(8,128)(2,1)} %bitcast.12), custom_call_target="tpu_custom_call" | custom-call | tf_op jit(solution)/shard_map/pallas_call | solution.py:172
  75.7 8.4 %shard_map.67 = f32[128,64,128]{2,1,0:T(8,128)} custom-call(s32[256]{0:T(256)} %get-tuple-element.10.rows_ref, s32[256]{0:T(256)} %get-tuple-element.9.cols_ref, bf16[256,64,64]{2,1,0:T(8,128)(2,1)} %get-tuple-element.7.adj_ref, bf16[33,64,128]{2,1,0:T(8,128)(2,1)} %shard_map.66.panel_ref), custom_call_target="tpu_custom_call" | custom-call | flops 268435456 | bytes 6291456 | tf_op jit(solution)/shard_map/pallas_call | solution.py:295
  84.1 35.7 %shard_map.68 = f32[256,128]{1,0:T(8,128)} custom-call(f32[2,8,2,256,128]{4,3,2,1,0:T(8,128)} %bitcast.9, f32[4,64,128]{2,1,0:T(8,128)} %broadcast_in_dim.14.scale_ref, bf16[4,64,128]{2,1,0:T(8,128)(2,1)} %bitcast.13), custom_call_target="tpu_custom_call" | custom-call | tf_op jit(solution)/shard_map/pallas_call | solution.py:172
  119.8 1.5 %convert_element_type.7 = bf16[256,128]{1,0:T(8,128)(2,1)} convert(f32[256,128]{1,0:T(8,128)} %shard_map.68) | non-fusion elementwise | flops 32768 | bytes 196608 | tf_op jit(solution)/shard_map/convert_element_type | solution.py:333
